TPU v7x, 32 devices: a whole 2x2x4 slice. The times are simulated.
32 devices in a mesh: seq: 4 (over y, core), dp: 8 (over z, x).
Axes of the slice: x: 2, y: 2, z: 4, core: 2. Of those that a mesh axis runs over, the one named last changes fastest.
Arguments:
- tokens: bfloat16 [8, 2048, 768], P('dp', 'seq'), may hold values from -6 to 6
- lengths: int32 [8, 8], P('dp'), may hold values from 16 to 1536, as said below
- classes: bfloat16 [150, 768], replicated, may hold values from -6 to 6
- norm_gains: bfloat16 [5, 768], replicated, may hold values from 0.5 to 1.5
- mask_gain: bfloat16 [150], replicated, may hold values from 0.5 to 1.5
- enc_qkv: bfloat16 [768, 2304], P('dp'), may hold values from -0.21875 to 0.21875
- enc_out: bfloat16 [768, 768], P('dp'), may hold values from -3 to 3
- enc_up: bfloat16 [768, 3072], P('dp'), may hold values from -0.21875 to 0.21875
- enc_down: bfloat16 [3072, 768], P('dp'), may hold values from -0.109375 to 0.109375
- dec_qkv: bfloat16 [768, 2304], P('dp'), may hold values from -0.21875 to 0.21875
- dec_out: bfloat16 [768, 768], P('dp'), may hold values from -3 to 3
- dec_up: bfloat16 [768, 3072], P('dp'), may hold values from -0.21875 to 0.21875
- dec_down: bfloat16 [3072, 768], P('dp'), may hold values from -0.109375 to 0.109375
- patch_proj: bfloat16 [768, 768], P('dp'), may hold values from -0.21875 to 0.21875
- class_proj: bfloat16 [768, 768], P('dp'), may hold values from -0.21875 to 0.21875
- mask_cot: float32 [8, 2048, 150], P('dp', 'seq'), may hold values from -6 to 6
Outputs:
- masks: float32 [8, 2048, 150], P('dp', 'seq')
- grad_tokens: float32 [8, 2048, 768], P('dp', 'seq')
- grad_classes: float32 [150, 768], replicated
- grad_gains: float32 [5, 768], replicated
- grad_mask_gain: float32 [150], replicated
- grad_enc_qkv: float32 [768, 2304], P('dp')
- grad_enc_out: float32 [768, 768], P('dp')
- grad_enc_up: float32 [768, 3072], P('dp')
- grad_enc_down: float32 [3072, 768], P('dp')
- grad_dec_qkv: float32 [768, 2304], P('dp')
- grad_dec_out: float32 [768, 768], P('dp')
- grad_dec_up: float32 [768, 3072], P('dp')
- grad_dec_down: float32 [3072, 768], P('dp')
- grad_patch_proj: float32 [768, 768], P('dp')
- grad_class_proj: float32 [768, 768], P('dp')
Inputs may be any that keep to these rules, and one draw needn't show every extreme that they name: Each row holds the lengths of 8 images in packing order; they sum to 1984, the positions after them being padding; one image of each row has exactly 1536 patches.
All inputs are finite; a program needn't handle non-finite values.
Results may differ from a plain program's by a relative error of at most 0.03.
Values may be sent and summed in bfloat16 or wider, within the bound.
No kernel may reach another device: no remote copies, remote signals or barrier semaphores. Data moves between devices by JAX's collectives and lax.ppermute only.
A program may use at most 320 MiB of HBM per device.

v0:
```python
import math

import jax
import jax.numpy as jnp
from jax import lax
from jax.sharding import PartitionSpec as P

D = 768
HEADS = 12
HD = 64
IMGS = 8


NEG_FILL = -1e30
PRECISE = lax.Precision.HIGHEST


def norm_rows(values, gain_row):
    centre = values - jnp.mean(values, axis=-1, keepdims=True)
    return centre * lax.rsqrt(jnp.mean(centre * centre, axis=-1, keepdims=True) + 1e-06) * gain_row


def class_norm(logits, gain_row):
    centre = logits - jnp.mean(logits, axis=-1, keepdims=True)
    return centre * lax.rsqrt(jnp.mean(centre * centre, axis=-1, keepdims=True) + 1e-05) * gain_row


def unit_rows(values):
    return values * lax.rsqrt(jnp.sum(values * values, axis=-1, keepdims=True) + 1e-06)


def segments(seq_lengths, first_row, row_count):
    boundary = jnp.cumsum(seq_lengths)
    places = first_row + jnp.arange(row_count, dtype=jnp.int32)
    return jnp.sum((places[:, None] >= boundary[None, :]).astype(jnp.int32), axis=1)


def allowed(seg_query, seg_key):
    return (seg_query[:, None] == seg_key[None, :]) | (seg_key[None, :] < 0)


def heads_of(values):
    return values.reshape(values.shape[0], HEADS, HD)


def online_step(run_state, query_heads, seg_query, key_heads, value_heads, seg_key):
    run_max, run_sum, run_acc = run_state
    scores = jnp.einsum(
        "qhd,khd->hqk", query_heads, key_heads, preferred_element_type=jnp.float32
    ) * (1.0 / math.sqrt(HD))
    permit = allowed(seg_query, seg_key)[None]
    scores = jnp.where(permit, scores, NEG_FILL)
    new_max = jnp.maximum(run_max, jnp.max(scores, axis=-1))
    weights = jnp.where(permit, jnp.exp(scores - new_max[..., None]), 0.0)
    factor = jnp.exp(run_max - new_max)
    run_sum = factor * run_sum + jnp.sum(weights, axis=-1)
    run_acc = run_acc * factor.T[:, :, None] + jnp.einsum(
        "hqk,khd->qhd",
        weights.astype(jnp.bfloat16),
        value_heads,
        preferred_element_type=jnp.float32,
    )
    return (new_max, run_sum, run_acc)


def attend_forward(queries, keyval, seq_lengths, first_row, class_kv):
    row_count = queries.shape[0]
    query_heads = heads_of(queries)
    seg_query = segments(seq_lengths, first_row, row_count)
    run_state = (
        jnp.full((HEADS, row_count), NEG_FILL, jnp.float32),
        jnp.zeros((HEADS, row_count), jnp.float32),
        jnp.zeros((row_count, HEADS, HD), jnp.float32),
    )
    if class_kv is not None:
        class_seg = jnp.full((class_kv.shape[0],), -1, jnp.int32)
        run_state = online_step(
            run_state,
            query_heads,
            seg_query,
            heads_of(class_kv[:, :D]),
            heads_of(class_kv[:, D:]),
            class_seg,
        )
    fold_state = run_state
    arrived = lax.all_gather(keyval, "seq", axis=0, tiled=True)
    piece_rows = arrived.shape[0]
    block_rows = math.gcd(piece_rows, 1024)
    block_count = piece_rows // block_rows
    seg_piece = segments(seq_lengths, jnp.int32(0), piece_rows).reshape(block_count, block_rows)
    keys_all = arrived[:, :D].reshape(block_count, block_rows, HEADS, HD)
    values_all = arrived[:, D:].reshape(block_count, block_rows, HEADS, HD)

    def attend_step_block(inner_state, inner_parts):
        return (
            online_step(
                inner_state, query_heads, seg_query, inner_parts[0], inner_parts[1], inner_parts[2]
            ),
            None,
        )

    fold_state, _ = lax.scan(attend_step_block, fold_state, (keys_all, values_all, seg_piece))
    run_max, run_sum, run_acc = fold_state
    result = (run_acc / run_sum.T[:, :, None]).reshape(row_count, D)
    return (result, run_max + jnp.log(run_sum))


def grad_block(query_heads, grad_heads, log_total, delta_rows, key_heads, value_heads, permit):
    scale = 1.0 / math.sqrt(HD)
    scores = (
        jnp.einsum("qhd,khd->hqk", query_heads, key_heads, preferred_element_type=jnp.float32)
        * scale
    )
    weights = jnp.where(permit, jnp.exp(scores - log_total[..., None]), 0.0)
    grad_prob = jnp.einsum(
        "qhd,khd->hqk", grad_heads, value_heads, preferred_element_type=jnp.float32
    )
    grad_score = (weights * (grad_prob - delta_rows[..., None])).astype(jnp.bfloat16)
    grad_query = (
        jnp.einsum("hqk,khd->qhd", grad_score, key_heads, preferred_element_type=jnp.float32)
        * scale
    )
    grad_key = (
        jnp.einsum("hqk,qhd->khd", grad_score, query_heads, preferred_element_type=jnp.float32)
        * scale
    )
    grad_value = jnp.einsum(
        "hqk,qhd->khd", weights.astype(jnp.bfloat16), grad_heads, preferred_element_type=jnp.float32
    )
    return (grad_query, grad_key, grad_value)


def attention_back(
    queries, keyval, grad_attended, attended, log_total, seq_lengths, first_row, class_kv
):
    row_count = queries.shape[0]
    query_heads = heads_of(queries)
    grad_heads = heads_of(grad_attended)
    seg_query = segments(seq_lengths, first_row, row_count)
    delta_rows = jnp.sum(grad_heads.astype(jnp.float32) * heads_of(attended), axis=-1).T
    cycle_size = lax.axis_size("seq")
    grad_query = jnp.zeros((row_count, HEADS, HD), jnp.float32)
    grad_class = None
    if class_kv is not None:
        class_count = class_kv.shape[0]
        permit = jnp.ones((1, row_count, class_count), jnp.bool_)
        grad_query, class_key, class_value = grad_block(
            query_heads,
            grad_heads,
            log_total,
            delta_rows,
            heads_of(class_kv[:, :D]),
            heads_of(class_kv[:, D:]),
            permit,
        )
        grad_class = jnp.concatenate(
            [class_key.reshape(class_count, D), class_value.reshape(class_count, D)], axis=1
        )
    start_state = (grad_query, jnp.zeros((row_count * cycle_size, 2 * D), jnp.float32))
    fold_state = start_state
    arrived = lax.all_gather(keyval, "seq", axis=0, tiled=True)
    piece_rows = arrived.shape[0]
    block_rows = math.gcd(piece_rows, 1024)
    block_count = piece_rows // block_rows
    seg_piece = segments(seq_lengths, jnp.int32(0), piece_rows).reshape(block_count, block_rows)
    offsets = jnp.arange(block_count, dtype=jnp.int32) * block_rows

    def attention_step_block(inner_state, inner_parts):
        query_run, keyval_all = inner_state
        key_rows, value_rows, seg_rows, offset = inner_parts
        permit = allowed(seg_query, seg_rows)[None]
        part_query, part_key, part_value = grad_block(
            query_heads, grad_heads, log_total, delta_rows, key_rows, value_rows, permit
        )
        fresh = jnp.concatenate(
            [part_key.reshape(block_rows, D), part_value.reshape(block_rows, D)], axis=1
        )
        keyval_all = lax.dynamic_update_slice_in_dim(keyval_all, fresh, offset, 0)
        return ((query_run + part_query, keyval_all), None)

    fold_state, _ = lax.scan(
        attention_step_block,
        fold_state,
        (
            arrived[:, :D].reshape(block_count, block_rows, HEADS, HD),
            arrived[:, D:].reshape(block_count, block_rows, HEADS, HD),
            seg_piece,
            offsets,
        ),
    )
    grad_query, keyval_all = fold_state
    grad_query = grad_query.reshape(row_count, D)
    grad_keyval = lax.psum_scatter(
        keyval_all.astype(jnp.bfloat16), "seq", scatter_dimension=0, tiled=True
    ).astype(jnp.float32)
    return (grad_query, grad_keyval, grad_class)


def block_forward(
    hidden, gain_a, gain_b, w_qkv, w_out, w_up, w_down, seq_lengths, first_row, class_kv
):
    normed = norm_rows(hidden, gain_a).astype(jnp.bfloat16)
    projected = jnp.dot(normed, w_qkv, preferred_element_type=jnp.float32).astype(jnp.bfloat16)
    attended, log_total = attend_forward(
        projected[:, :D], projected[:, D:], seq_lengths, first_row, class_kv
    )
    attended_low = attended.astype(jnp.bfloat16)
    middle = hidden + jnp.dot(attended_low, w_out, preferred_element_type=jnp.float32)
    second = norm_rows(middle, gain_b).astype(jnp.bfloat16)
    upward = jnp.dot(second, w_up, preferred_element_type=jnp.float32)
    active = jax.nn.gelu(upward).astype(jnp.bfloat16)
    result = middle + jnp.dot(active, w_down, preferred_element_type=jnp.float32)
    return (
        result,
        (normed, projected, attended, log_total, attended_low, middle, second, upward, active),
    )


def block_backward(
    grad_result,
    hidden,
    kept,
    gain_a,
    gain_b,
    w_qkv,
    w_out,
    w_up,
    w_down,
    seq_lengths,
    first_row,
    class_kv,
):
    normed, projected, attended, log_total, attended_low, middle, second, upward, active = kept
    grad_branch = grad_result.astype(jnp.bfloat16)
    grad_down = jnp.einsum("sf,sd->fd", active, grad_branch, preferred_element_type=jnp.float32)
    grad_active = jnp.dot(grad_branch, w_down.T, preferred_element_type=jnp.float32)
    _, gelu_back = jax.vjp(jax.nn.gelu, upward)
    grad_upward = gelu_back(grad_active)[0].astype(jnp.bfloat16)
    grad_up = jnp.einsum("sd,sf->df", second, grad_upward, preferred_element_type=jnp.float32)
    grad_second = jnp.dot(grad_upward, w_up.T, preferred_element_type=jnp.float32)
    _, second_back = jax.vjp(norm_rows, middle, gain_b)
    grad_middle, grad_gain_b = second_back(grad_second)
    grad_middle = grad_middle + grad_result
    grad_attn = grad_middle.astype(jnp.bfloat16)
    grad_out = jnp.einsum("sd,se->de", attended_low, grad_attn, preferred_element_type=jnp.float32)
    grad_attended = jnp.dot(grad_attn, w_out.T, preferred_element_type=jnp.float32).astype(
        jnp.bfloat16
    )
    grad_query, grad_keyval, grad_class = attention_back(
        projected[:, :D],
        projected[:, D:],
        grad_attended,
        attended,
        log_total,
        seq_lengths,
        first_row,
        class_kv,
    )
    grad_proj = jnp.concatenate([grad_query, grad_keyval], axis=1).astype(jnp.bfloat16)
    grad_qkv = jnp.einsum("sd,se->de", normed, grad_proj, preferred_element_type=jnp.float32)
    grad_normed = jnp.dot(grad_proj, w_qkv.T, preferred_element_type=jnp.float32)
    _, first_back = jax.vjp(norm_rows, hidden, gain_a)
    grad_hidden, grad_gain_a = first_back(grad_normed)
    return (
        grad_hidden + grad_middle,
        (grad_qkv, grad_out, grad_up, grad_down),
        grad_gain_a,
        grad_gain_b,
        grad_class,
    )


def local(
    tokens,
    lengths,
    classes,
    norm_gains,
    mask_gain,
    enc_qkv,
    enc_out,
    enc_up,
    enc_down,
    dec_qkv,
    dec_out,
    dec_up,
    dec_down,
    patch_proj,
    class_proj,
    mask_cot,
):
    gathered = (
        lax.all_gather(enc_qkv, "dp", axis=0, tiled=True),
        lax.all_gather(enc_out, "dp", axis=0, tiled=True),
        lax.all_gather(enc_up, "dp", axis=0, tiled=True),
        lax.all_gather(enc_down, "dp", axis=0, tiled=True),
        lax.all_gather(dec_qkv, "dp", axis=0, tiled=True),
        lax.all_gather(dec_out, "dp", axis=0, tiled=True),
        lax.all_gather(dec_up, "dp", axis=0, tiled=True),
        lax.all_gather(dec_down, "dp", axis=0, tiled=True),
        lax.all_gather(patch_proj, "dp", axis=0, tiled=True),
        lax.all_gather(class_proj, "dp", axis=0, tiled=True),
    )
    row_count = tokens.shape[1]
    first_row = lax.axis_index("seq") * row_count
    seq_lengths = lengths[0]
    inputs_f = tokens[0].astype(jnp.float32)
    gains_f = norm_gains.astype(jnp.float32)
    classes_f = classes.astype(jnp.float32)
    mask_gain_f = mask_gain.astype(jnp.float32)
    valid_rows = (segments(seq_lengths, first_row, row_count) < IMGS).astype(jnp.float32)[:, None]
    encoded, _ = block_forward(
        inputs_f,
        gains_f[0],
        gains_f[1],
        gathered[0],
        gathered[1],
        gathered[2],
        gathered[3],
        seq_lengths,
        first_row,
        None,
    )
    class_normed = norm_rows(classes_f, gains_f[2]).astype(jnp.bfloat16)
    class_kv = jnp.dot(class_normed, gathered[4][:, D:], preferred_element_type=jnp.float32).astype(
        jnp.bfloat16
    )
    decoded, dec_kept = block_forward(
        encoded,
        gains_f[2],
        gains_f[3],
        gathered[4],
        gathered[5],
        gathered[6],
        gathered[7],
        seq_lengths,
        first_row,
        class_kv,
    )
    final_normed = norm_rows(decoded, gains_f[4]).astype(jnp.bfloat16)
    patch_rows = jnp.dot(final_normed, gathered[8], preferred_element_type=jnp.float32).astype(
        jnp.bfloat16
    )
    class_rows = jnp.dot(classes, gathered[9], preferred_element_type=jnp.float32)
    class_unit = unit_rows(class_rows).astype(jnp.bfloat16)
    logits = jnp.dot(patch_rows, class_unit.T, preferred_element_type=jnp.float32)
    mask_out = class_norm(logits, mask_gain_f) * valid_rows
    _, head_back = jax.vjp(class_norm, logits, mask_gain_f)
    grad_logits, grad_mask_gain = head_back(mask_cot[0] * valid_rows)
    grad_logits_low = grad_logits.astype(jnp.bfloat16)
    grad_patch_rows = jnp.dot(
        grad_logits_low, class_unit, preferred_element_type=jnp.float32
    ).astype(jnp.bfloat16)
    grad_unit = jnp.einsum(
        "sc,sd->cd", grad_logits_low, patch_rows, preferred_element_type=jnp.float32
    )
    grad_patch_proj = jnp.einsum(
        "sd,se->de", final_normed, grad_patch_rows, preferred_element_type=jnp.float32
    )
    grad_final = jnp.dot(grad_patch_rows, gathered[8].T, preferred_element_type=jnp.float32)
    _, final_back = jax.vjp(norm_rows, decoded, gains_f[4])
    grad_decoded, grad_gain_last = final_back(grad_final)
    _, unit_back = jax.vjp(unit_rows, class_rows)
    grad_class_rows = unit_back(grad_unit)[0]
    grad_class_proj = jnp.einsum(
        "cd,ce->de",
        classes_f,
        grad_class_rows,
        precision=PRECISE,
        preferred_element_type=jnp.float32,
    )
    grad_classes = jnp.dot(
        grad_class_rows,
        gathered[9].astype(jnp.float32).T,
        precision=PRECISE,
        preferred_element_type=jnp.float32,
    )
    grad_encoded, dec_grads, grad_gain_two, grad_gain_three, grad_class_kv = block_backward(
        grad_decoded,
        encoded,
        dec_kept,
        gains_f[2],
        gains_f[3],
        gathered[4],
        gathered[5],
        gathered[6],
        gathered[7],
        seq_lengths,
        first_row,
        class_kv,
    )
    class_part = jnp.einsum(
        "cd,ce->de",
        class_normed.astype(jnp.float32),
        grad_class_kv,
        precision=PRECISE,
        preferred_element_type=jnp.float32,
    )
    grad_dec_qkv = dec_grads[0] + jnp.concatenate(
        [jnp.zeros((D, D), jnp.float32), class_part], axis=1
    )
    grad_class_normed = jnp.dot(
        grad_class_kv,
        gathered[4][:, D:].astype(jnp.float32).T,
        precision=PRECISE,
        preferred_element_type=jnp.float32,
    )
    _, class_back = jax.vjp(norm_rows, classes_f, gains_f[2])
    grad_classes_kv, grad_gain_class = class_back(grad_class_normed)
    _, enc_kept = block_forward(
        inputs_f,
        gains_f[0],
        gains_f[1],
        gathered[0],
        gathered[1],
        gathered[2],
        gathered[3],
        seq_lengths,
        first_row,
        None,
    )
    grad_inputs, enc_grads, grad_gain_zero, grad_gain_one, _ = block_backward(
        grad_encoded,
        inputs_f,
        enc_kept,
        gains_f[0],
        gains_f[1],
        gathered[0],
        gathered[1],
        gathered[2],
        gathered[3],
        seq_lengths,
        first_row,
        None,
    )
    weight_parts = (
        lax.psum_scatter(
            enc_grads[0].astype(jnp.bfloat16), "dp", scatter_dimension=0, tiled=True
        ).astype(jnp.float32),
        lax.psum_scatter(
            enc_grads[1].astype(jnp.bfloat16), "dp", scatter_dimension=0, tiled=True
        ).astype(jnp.float32),
        lax.psum_scatter(
            enc_grads[2].astype(jnp.bfloat16), "dp", scatter_dimension=0, tiled=True
        ).astype(jnp.float32),
        lax.psum_scatter(
            enc_grads[3].astype(jnp.bfloat16), "dp", scatter_dimension=0, tiled=True
        ).astype(jnp.float32),
        lax.psum_scatter(
            grad_dec_qkv.astype(jnp.bfloat16), "dp", scatter_dimension=0, tiled=True
        ).astype(jnp.float32),
        lax.psum_scatter(
            dec_grads[1].astype(jnp.bfloat16), "dp", scatter_dimension=0, tiled=True
        ).astype(jnp.float32),
        lax.psum_scatter(
            dec_grads[2].astype(jnp.bfloat16), "dp", scatter_dimension=0, tiled=True
        ).astype(jnp.float32),
        lax.psum_scatter(
            dec_grads[3].astype(jnp.bfloat16), "dp", scatter_dimension=0, tiled=True
        ).astype(jnp.float32),
        lax.psum_scatter(
            grad_patch_proj.astype(jnp.bfloat16), "dp", scatter_dimension=0, tiled=True
        ).astype(jnp.float32),
        lax.psum_scatter(
            grad_class_proj.astype(jnp.bfloat16), "dp", scatter_dimension=0, tiled=True
        ).astype(jnp.float32),
    )
    weight_sums = (
        lax.psum(weight_parts[0].astype(jnp.bfloat16), "seq").astype(jnp.float32),
        lax.psum(weight_parts[1].astype(jnp.bfloat16), "seq").astype(jnp.float32),
        lax.psum(weight_parts[2].astype(jnp.bfloat16), "seq").astype(jnp.float32),
        lax.psum(weight_parts[3].astype(jnp.bfloat16), "seq").astype(jnp.float32),
        lax.psum(weight_parts[4].astype(jnp.bfloat16), "seq").astype(jnp.float32),
        lax.psum(weight_parts[5].astype(jnp.bfloat16), "seq").astype(jnp.float32),
        lax.psum(weight_parts[6].astype(jnp.bfloat16), "seq").astype(jnp.float32),
        lax.psum(weight_parts[7].astype(jnp.bfloat16), "seq").astype(jnp.float32),
        lax.psum(weight_parts[8].astype(jnp.bfloat16), "seq").astype(jnp.float32),
        lax.psum(weight_parts[9].astype(jnp.bfloat16), "seq").astype(jnp.float32),
    )
    gain_terms = jnp.stack(
        [
            grad_gain_zero,
            grad_gain_one,
            grad_gain_two + grad_gain_class,
            grad_gain_three,
            grad_gain_last,
        ]
    )
    shared = lax.psum((grad_classes + grad_classes_kv, gain_terms, grad_mask_gain), ("seq", "dp"))
    return (
        mask_out[None],
        grad_inputs[None],
        shared[0],
        shared[1],
        shared[2],
        weight_sums[0],
        weight_sums[1],
        weight_sums[2],
        weight_sums[3],
        weight_sums[4],
        weight_sums[5],
        weight_sums[6],
        weight_sums[7],
        weight_sums[8],
        weight_sums[9],
    )


def solution(mesh):
    placed = (
        P("dp", "seq", None),
        P("dp", None),
        P(),
        P(),
        P(),
        P("dp", None),
        P("dp", None),
        P("dp", None),
        P("dp", None),
        P("dp", None),
        P("dp", None),
        P("dp", None),
        P("dp", None),
        P("dp", None),
        P("dp", None),
        P("dp", "seq", None),
    )
    return jax.shard_map(
        local,
        mesh=mesh,
        in_specs=placed,
        out_specs=(
            P("dp", "seq", None),
            P("dp", "seq", None),
            P(),
            P(),
            P(),
            P("dp", None),
            P("dp", None),
            P("dp", None),
            P("dp", None),
            P("dp", None),
            P("dp", None),
            P("dp", None),
            P("dp", None),
            P("dp", None),
            P("dp", None),
        ),
        check_vma=False,
    )
```

profile of v0, /device:TPU:0, one launch (start us, length us, event | category | flops | bytes accessed | tf_op | source)
XLA Modules:
  0.0 2341.5 jit_solution(13398695250539798656)
XLA Ops:
  12.7 65.4 %all-gather.13.cloned.1.call-done = bf16[768,2304]{1,0:T(8,128)(2,1)} async-done(((bf16[96,2304]{1,0:T(8,128)(2,1)}), bf16[768,2304]{1,0:T(8,128)(2,1)}) %all-gather.13.cloned.1.call-update) | async-done | bytes 3538960 | tf_op jit(solution)/shard_map/all_gather | solution.py:292
  88.7 40.1 %all-gather.15.cloned.1.call-done = bf16[2048,1536]{1,0:T(8,128)(2,1)} async-done(((bf16[512,1536]{1,0:T(8,128)(2,1)}), bf16[2048,1536]{1,0:T(8,128)(2,1)}) %all-gather.15.cloned.1.call-update) | async-done | bytes 6291472 | tf_op jit(solution)/shard_map/all_gather | solution.py:86
  158.8 76.6 %while.62 = (s32[]{:T(128)}, f32[12,512]{1,0:T(8,128)S(1)}, f32[12,512]{1,0:T(8,128)S(1)}, f32[512,12,64]{0,2,1:T(8,128)S(1)}, s32[512]{0:T(512)S(1)}, /*index=5...) while((s32[]{:T(128)}, f32[12,512]{1,0:T(8,128)S(1)}, ...), condition=%wide.region_8.9_spmd.clone, body=%wide.region_5.0_spmd.clone.sunk | while | flops 1694667776 | bytes 97681568 | solution.py:102
  261.2 71.8 %all-gather.21.cloned.1.call-done = bf16[3072,768]{1,0:T(8,128)(2,1)} async-done(((bf16[384,768]{1,0:T(8,128)(2,1)}), bf16[3072,768]{1,0:T(8,128)(2,1)}) %all-gather.21.cloned.1.call-update) | async-done | bytes 4718608 | tf_op jit(solution)/shard_map/all_gather | solution.py:295
  340.7 57.7 %all-gather.23.cloned.1.call-done = bf16[768,2304]{1,0:T(8,128)(2,1)} async-done(((bf16[96,2304]{1,0:T(8,128)(2,1)}), bf16[768,2304]{1,0:T(8,128)(2,1)}) %all-gather.23.cloned.1.call-update) | async-done | bytes 3538960 | tf_op jit(solution)/shard_map/all_gather | solution.py:296
  452.6 34.2 %all-gather.25.cloned.1.call-done = bf16[2048,1536]{1,0:T(8,128)(2,1)} async-done(((bf16[512,1536]{1,0:T(8,128)(2,1)}), bf16[2048,1536]{1,0:T(8,128)(2,1)}) %all-gather.25.cloned.1.call-update) | async-done | bytes 6291472 | tf_op jit(solution)/shard_map/all_gather | solution.py:86
  524.3 76.5 %while.60 = (s32[]{:T(128)}, f32[12,512]{1,0:T(8,128)S(1)}, f32[12,512]{1,0:T(8,128)S(1)}, f32[512,12,64]{0,2,1:T(8,128)S(1)}, s32[512]{0:T(512)S(1)}, /*index=5...) while((s32[]{:T(128)}, f32[12,512]{1,0:T(8,128)S(1)}, ...), condition=%wide.region_20.21_spmd, body=%wide.region_17.20_spmd.sunk | while | flops 1694256128 | bytes 97681560 | solution.py:102
  619.0 72.1 %all-gather.31.cloned.1.call-done = bf16[3072,768]{1,0:T(8,128)(2,1)} async-done(((bf16[384,768]{1,0:T(8,128)(2,1)}), bf16[3072,768]{1,0:T(8,128)(2,1)}) %all-gather.31.cloned.1.call-update) | async-done | bytes 4718608 | tf_op jit(solution)/shard_map/all_gather | solution.py:299
  701.0 31.3 %all-gather.33.cloned.1.call-done = bf16[768,768]{1,0:T(8,128)(2,1)} async-done(((bf16[96,768]{1,0:T(8,128)(2,1)}), bf16[768,768]{1,0:T(8,128)(2,1)}) %all-gather.33.cloned.1.call-update) | async-done | bytes 1179664 | tf_op jit(solution)/shard_map/all_gather | solution.py:300
  769.6 185.2 %while.61 = (s32[]{:T(128)}, f32[512,12,64]{0,2,1:T(8,128)}, bf16[2048,1536]{0,1:T(8,128)(2,1)}, bf16[2,1024,12,64]{1,3,2,0:T(8,128)(2,1)}, s32[512]{0:T(512)S(1...) while((s32[]{:T(128)}, f32[512,12,64]{0,2,1:T(8,128)}, ...), condition=%wide.region_36.37_spmd, body=%wide.region_35.36_spmd.sunk | while | flops 4099146752 | bytes 141648112 | solution.py:181
  957.2 54.9 %reduce-scatter.15.cloned.1.call-done = bf16[512,1536]{0,1:T(8,128)(2,1)} async-done(((bf16[2048,1536]{0,1:T(8,128)(2,1)}), bf16[512,1536]{0,1:T(8,128)(2,1)}) %reduce-scatter.15.cloned.1.call-update) | async-done | bytes 1572880 | tf_op jit(solution)/shard_map/reduce_scatter | solution.py:193
  1041.4 185.3 %while.63 = (s32[]{:T(128)}, f32[512,12,64]{0,2,1:T(8,128)}, bf16[2048,1536]{0,1:T(8,128)(2,1)}, bf16[2,1024,12,64]{1,3,2,0:T(8,128)(2,1)}, s32[512]{0:T(512)S(1...) while((s32[]{:T(128)}, f32[512,12,64]{0,2,1:T(8,128)}, ...), condition=%wide.region_44.45_spmd.clone, body=%wide.region_43.44_spmd.clone.sunk | while | flops 4099539968 | bytes 141648112 | solution.py:181
  1300.5 52.6 %reduce-scatter.37.cloned.1.call-done = bf16[96,768]{1,0:T(8,128)(2,1)} async-done(((bf16[768,768]{1,0:T(8,128)(2,1)}), bf16[96,768]{1,0:T(8,128)(2,1)}) %reduce-scatter.37.cloned.1.call-update) | async-done | bytes 147472
  1354.8 65.1 %reduce-scatter.35.cloned.1.call-done = bf16[96,768]{1,0:T(8,128)(2,1)} async-done(((bf16[768,768]{1,0:T(8,128)(2,1)}), bf16[96,768]{1,0:T(8,128)(2,1)}) %reduce-scatter.35.cloned.1.call-update) | async-done | bytes 147472 | tf_op jit(solution)/shard_map/reduce_scatter | solution.py:460
  1419.9 66.8 %reduce-scatter.29.cloned.1.call-done = bf16[96,768]{1,0:T(8,128)(2,1)} async-done(((bf16[768,768]{1,0:T(8,128)(2,1)}), bf16[96,768]{1,0:T(8,128)(2,1)}) %reduce-scatter.29.cloned.1.call-update) | async-done | bytes 147472 | tf_op jit(solution)/shard_map/reduce_scatter | solution.py:451
  1486.8 97.9 %reduce-scatter.31.cloned.1.call-done = bf16[96,3072]{1,0:T(8,128)(2,1)} async-done(((bf16[768,3072]{1,0:T(8,128)(2,1)}), bf16[96,3072]{1,0:T(8,128)(2,1)}) %reduce-scatter.31.cloned.1.call-update) | async-done | bytes 589840 | tf_op jit(solution)/shard_map/reduce_scatter | solution.py:454
  1584.7 98.8 %reduce-scatter.33.cloned.1.call-done = bf16[384,768]{1,0:T(8,128)(2,1)} async-done(((bf16[3072,768]{1,0:T(8,128)(2,1)}), bf16[384,768]{1,0:T(8,128)(2,1)}) %reduce-scatter.33.cloned.1.call-update) | async-done | bytes 589840 | tf_op jit(solution)/shard_map/reduce_scatter | solution.py:457
  1683.5 67.6 %reduce-scatter.21.cloned.1.call-done = bf16[96,768]{1,0:T(8,128)(2,1)} async-done(((bf16[768,768]{1,0:T(8,128)(2,1)}), bf16[96,768]{1,0:T(8,128)(2,1)}) %reduce-scatter.21.cloned.1.call-update) | async-done | bytes 147472 | tf_op jit(solution)/shard_map/reduce_scatter | solution.py:439
  1751.1 81.8 %reduce-scatter.27.cloned.1.call-done = bf16[96,2304]{1,0:T(8,128)(2,1)} async-done(((bf16[768,2304]{1,0:T(8,128)(2,1)}), bf16[96,2304]{1,0:T(8,128)(2,1)}) %reduce-scatter.27.cloned.1.call-update) | async-done | bytes 442384 | tf_op jit(solution)/shard_map/reduce_scatter | solution.py:448
  1832.9 98.6 %reduce-scatter.23.cloned.1.call-done = bf16[96,3072]{1,0:T(8,128)(2,1)} async-done(((bf16[768,3072]{1,0:T(8,128)(2,1)}), bf16[96,3072]{1,0:T(8,128)(2,1)}) %reduce-scatter.23.cloned.1.call-update) | async-done | bytes 589840 | tf_op jit(solution)/shard_map/reduce_scatter | solution.py:442
  1931.6 98.8 %reduce-scatter.25.cloned.1.call-done = bf16[384,768]{1,0:T(8,128)(2,1)} async-done(((bf16[3072,768]{1,0:T(8,128)(2,1)}), bf16[384,768]{1,0:T(8,128)(2,1)}) %reduce-scatter.25.cloned.1.call-update) | async-done | bytes 589840 | tf_op jit(solution)/shard_map/reduce_scatter | solution.py:445
  2030.4 82.4 %reduce-scatter.19.cloned.1.call-done = bf16[96,2304]{1,0:T(8,128)(2,1)} async-done(((bf16[768,2304]{1,0:T(8,128)(2,1)}), bf16[96,2304]{1,0:T(8,128)(2,1)}) %reduce-scatter.19.cloned.1.call-update) | async-done | bytes 442384 | tf_op jit(solution)/shard_map/reduce_scatter | solution.py:436
  2130.2 41.8 %all-reduce.1 = (f32[5,768]{1,0:T(8,128)}, f32[150]{0:T(256)}) all-reduce(f32[5,768]{1,0:T(8,128)S(1)} %stack.2, f32[150]{0:T(256)S(1)} %copy-done.130), channel_id=1, replica_groups=mesh['seq'=4,'dp'=8] {'seq','dp'}, use_global_device_ids=true, to_apply=%region_58.59 | all-reduce | flops 3990 | bytes 31920 | tf_op jit(solution)/shard_map/psum | solution.py:488
  2213.8 119.1 %all-reduce.6.cloned.1.call-done = f32[150,768]{1,0:T(8,128)} async-done(((f32[150,768]{1,0:T(8,128)}), f32[150,768]{1,0:T(8,128)}) %all-reduce.6.cloned.1.call-update) | async-done | bytes 460816 | tf_op jit(solution)/shard_map/psum | solution.py:488
  (607 shorter events, 916.5 us)
Async XLA Ops:
  83.8 151.9 %all-gather.17.cloned.1.call-start = ((), (), s32[]{:S(2)}) async-start(), calls=%async_computation.14 | async-start | bytes 1327104 | tf_op jit(solution)/shard_map/all_gather | solution.py:293
  84.6 168.3 %all-gather.19.cloned.1.call-start = ((), (), s32[]{:S(2)}) async-start(), calls=%async_computation.15 | async-start | bytes 5308416 | tf_op jit(solution)/shard_map/all_gather | solution.py:294
  85.1 247.8 %all-gather.21.cloned.1.call-start = ((), (), s32[]{:S(2)}) async-start(), calls=%async_computation.16 | async-start | bytes 5308416 | tf_op jit(solution)/shard_map/all_gather | solution.py:295
  85.7 312.6 %all-gather.23.cloned.1.call-start = ((), (), s32[]{:S(2)}) async-start(), calls=%async_computation.17 | async-start | bytes 3981312 | tf_op jit(solution)/shard_map/all_gather | solution.py:296
  86.3 353.8 %all-gather.35.cloned.1.call-start = ((), (), s32[]{:S(2)}) async-start(), calls=%async_computation.23 | async-start | bytes 1327104 | tf_op jit(solution)/shard_map/all_gather | solution.py:301
  87.1 399.8 %all-gather.25.cloned.1.call-start = ((), (), s32[]{:S(2)}) async-start(), calls=%async_computation.18 | async-start | bytes 7864320 | tf_op jit(solution)/shard_map/all_gather | solution.py:86
  405.2 195.8 %all-gather.27.cloned.1.call-start = ((), (), s32[]{:S(2)}) async-start(), calls=%async_computation.19 | async-start | bytes 1327104 | tf_op jit(solution)/shard_map/all_gather | solution.py:297
  406.0 204.9 %all-gather.29.cloned.1.call-start = ((), (), s32[]{:S(2)}) async-start(), calls=%async_computation.20 | async-start | bytes 5308416 | tf_op jit(solution)/shard_map/all_gather | solution.py:298
  406.6 284.5 %all-gather.31.cloned.1.call-start = ((), (), s32[]{:S(2)}) async-start(), calls=%async_computation.21 | async-start | bytes 5308416 | tf_op jit(solution)/shard_map/all_gather | solution.py:299
  407.3 325.0 %all-gather.33.cloned.1.call-start = ((), (), s32[]{:S(2)}) async-start(), calls=%async_computation.22 | async-start | bytes 1327104 | tf_op jit(solution)/shard_map/all_gather | solution.py:300
  407.9 604.3 %reduce-scatter.15.cloned.1.call-start = ((), (), s32[]{:S(2)}) async-start(), calls=%async_computation.24 | async-start | bytes 7864320 | tf_op jit(solution)/shard_map/reduce_scatter | solution.py:193
  955.4 339.2 %reduce-scatter.17.cloned.1.call-start = ((), (), s32[]{:S(2)}) async-start(), calls=%async_computation.25 | async-start | bytes 7864320 | tf_op jit(solution)/shard_map/reduce_scatter | solution.py:193
  1226.7 126.4 %reduce-scatter.37.cloned.1.call-start = ((), (), s32[]{:S(2)}) async-start(), calls=%async_computation.36 | async-start | bytes 1327104
  1231.4 188.6 %reduce-scatter.35.cloned.1.call-start = ((), (), s32[]{:S(2)}) async-start(), calls=%async_computation.35 | async-start | bytes 1327104 | tf_op jit(solution)/shard_map/reduce_scatter | solution.py:460
  1236.0 250.8 %reduce-scatter.29.cloned.1.call-start = ((), (), s32[]{:S(2)}) async-start(), calls=%async_computation.32 | async-start | bytes 1327104 | tf_op jit(solution)/shard_map/reduce_scatter | solution.py:451
  1237.8 346.8 %reduce-scatter.31.cloned.1.call-start = ((), (), s32[]{:S(2)}) async-start(), calls=%async_computation.33 | async-start | bytes 5308416 | tf_op jit(solution)/shard_map/reduce_scatter | solution.py:454
  1245.5 438.0 %reduce-scatter.33.cloned.1.call-start = ((), (), s32[]{:S(2)}) async-start(), calls=%async_computation.34 | async-start | bytes 5308416 | tf_op jit(solution)/shard_map/reduce_scatter | solution.py:457
  1256.2 494.9 %reduce-scatter.21.cloned.1.call-start = ((), (), s32[]{:S(2)}) async-start(), calls=%async_computation.28 | async-start | bytes 1327104 | tf_op jit(solution)/shard_map/reduce_scatter | solution.py:439
  1260.6 572.4 %reduce-scatter.27.cloned.1.call-start = ((), (), s32[]{:S(2)}) async-start(), calls=%async_computation.31 | async-start | bytes 3981312 | tf_op jit(solution)/shard_map/reduce_scatter | solution.py:448
  1275.0 656.6 %reduce-scatter.23.cloned.1.call-start = ((), (), s32[]{:S(2)}) async-start(), calls=%async_computation.29 | async-start | bytes 5308416 | tf_op jit(solution)/shard_map/reduce_scatter | solution.py:442
  1282.9 747.5 %reduce-scatter.25.cloned.1.call-start = ((), (), s32[]{:S(2)}) async-start(), calls=%async_computation.30 | async-start | bytes 5308416 | tf_op jit(solution)/shard_map/reduce_scatter | solution.py:445
  1292.8 820.0 %reduce-scatter.19.cloned.1.call-start = ((), (), s32[]{:S(2)}) async-start(), calls=%async_computation.27 | async-start | bytes 3981312 | tf_op jit(solution)/shard_map/reduce_scatter | solution.py:436
  1300.4 899.1 %all-reduce.8.cloned.1.call-start = ((), (), s32[]{:S(2)}) async-start(), calls=%async_computation.37 | async-start | bytes 7766016 | tf_op jit(solution)/shard_map/psum | solution.py:477
  2112.8 220.1 %all-reduce.6.cloned.1.call-start = ((), (), s32[]{:S(2)}) async-start(), calls=%async_computation.26 | async-start | bytes 933888 | tf_op jit(solution)/shard_map/psum | solution.py:488
  (156 other events, 5677.8 us)
Sparse Core Ops, SparseCore 0:
  10.2 67.8 all-gather.12
  83.9 44.8 all-gather.14
  131.1 41.0 all-gather.16
  174.2 78.6 all-gather.18
  254.9 78.0 all-gather.20
  335.0 63.3 all-gather.22
  441.6 45.1 all-gather.24
  489.0 41.0 all-gather.26
  532.1 78.6 all-gather.28
  613.0 78.0 all-gather.30
  955.0 57.1 reduce-scatter.14
  1226.9 58.3 reduce-scatter.16
  1289.1 63.9 reduce-scatter.36
  1356.9 62.9 reduce-scatter.34
  1423.8 62.9 reduce-scatter.28
  1490.3 94.3 reduce-scatter.30
  1588.3 95.1 reduce-scatter.32
  1687.3 63.7 reduce-scatter.20
  1754.8 78.1 reduce-scatter.26
  1836.6 94.9 reduce-scatter.22
  1935.2 95.1 reduce-scatter.24
  2033.9 78.8 reduce-scatter.18
  2116.5 83.0 all-reduce.7
  2206.2 126.7 all-reduce.5
  (2 shorter events, 78.6 us)
where the time goes:
time: 2350 us; the launch traced here: 2340 us
  waiting for transfers between devices  1440 us (61%)
  matrix products  511 us (22%)
  local copies, waits for them, and re-layouts  227 us (10%)
  other arithmetic  99.1 us (4%)
  blocking collectives  41.8 us (2%)
    psum x1, waiting for transfers between devices, local(): lax.psum((grad_classes + grad_classes_kv, gain_terms, grad_mask_gain), ('...  119 us
    dynamic_update_slice x4, local copies, waits for them, and re-layouts, attention_step_block(): keyval_all = lax.dynamic_update_slice_in_dim(keyval_all, fresh, offset, 0)  108 us
    reduce_scatter x1, waiting for transfers between devices, local(): lax.psum_scatter(enc_grads[3].astype(jnp.bfloat16), 'dp', scatter_dimensi...  98.8 us
    reduce_scatter x1, waiting for transfers between devices, local(): lax.psum_scatter(dec_grads[3].astype(jnp.bfloat16), 'dp', scatter_dimensi...  98.8 us
    reduce_scatter x1, waiting for transfers between devices, local(): lax.psum_scatter(enc_grads[2].astype(jnp.bfloat16), 'dp', scatter_dimensi...  98.6 us
    reduce_scatter x1, waiting for transfers between devices, local(): lax.psum_scatter(dec_grads[2].astype(jnp.bfloat16), 'dp', scatter_dimensi...  97.9 us
    reduce_scatter x1, waiting for transfers between devices, local(): lax.psum_scatter(enc_grads[0].astype(jnp.bfloat16), 'dp', scatter_dimensi...  82.4 us
    reduce_scatter x1, waiting for transfers between devices, local(): lax.psum_scatter(grad_dec_qkv.astype(jnp.bfloat16), 'dp', scatter_dimensi...  81.8 us
  transfers between devices with their start and end apart: 26, of which 23 were waited for; matrix products, arithmetic and copies ran while one was open for 16% of the time, Pallas kernels for 0%

commit v1 on v0

v1 whole, which is shorter than its diff:
```python
import jax, jax.numpy as jnp
from jax import lax
from jax.experimental import pallas as pl
from jax.experimental.pallas import tpu as pltpu
from jax.sharding import PartitionSpec as P
HD=64
KB=256
LSE_LANE=10
NEG=-1e30
NT=(((1,),(1,)),((),()))
NN=(((1,),(0,)),((),()))

def split3(v):
    hi=v.astype(jnp.bfloat16).astype(jnp.float32)
    mid=(v-hi).astype(jnp.bfloat16).astype(jnp.float32)
    return hi,mid,v-hi-mid

def fwd_kernel(idx_ref,q_ref,k_ref,v_ref,fq_ref,fk_ref,o_ref,ol_ref,qa_ref,ka,va,s_ref,m_ref,acc_ref):
    rows=q_ref.shape[0]
    cnt=idx_ref[0]
    lane=lax.broadcasted_iota(jnp.int32,(1,128),1)
    low=lane<HD
    q2=q_ref[...]*jnp.bfloat16(0.125)
    fq=fq_ref[...]
    qs=(jnp.where(low,q2,fq),jnp.where(low,fq,q2))
    k2=k_ref[...];v2=v_ref[...];fk=fk_ref[...]
    ka[0]=jnp.where(low,k2,fk);ka[1]=jnp.where(low,fk,k2)
    va[0]=jnp.where(low,v2,fk);va[1]=jnp.where(low,fk,v2)
    m_ref[...]=jnp.full(m_ref.shape,2*NEG,jnp.float32)
    def first(i,_):
        r=pl.ds(pl.multiple_of(idx_ref[i+1]*KB,KB),KB)
        for h in range(2):
            s=lax.dot_general(qs[h],ka[h,r,:],NT,preferred_element_type=jnp.float32)
            s_ref[h,i]=s
            m_ref[h]=jnp.maximum(m_ref[h],jnp.maximum(s[:,:128],s[:,128:]))
        return 0
    lax.fori_loop(0,cnt,first,0)
    tops=[jnp.max(m_ref[h],axis=1,keepdims=True) for h in range(2)]
    acc_ref[...]=jnp.zeros(acc_ref.shape,jnp.float32)
    def second(i,_):
        r=pl.ds(pl.multiple_of(idx_ref[i+1]*KB,KB),KB)
        for h in range(2):
            p=jnp.exp(s_ref[h,i]-tops[h]).astype(jnp.bfloat16)
            acc_ref[h]+=lax.dot_general(p,va[h,r,:],NN,preferred_element_type=jnp.float32)
        return 0
    lax.fori_loop(0,cnt,second,0)
    outs=[]
    for h in range(2):
        base=HD+LSE_LANE if h==0 else LSE_LANE
        acc=acc_ref[h]
        total=acc[:,base:base+1]
        outs.append(acc/total)
        hi,mid,lo=split3(-(tops[h]+jnp.log(total)))
        qa=qs[h].astype(jnp.float32)
        for j,t in enumerate((hi,mid,lo)):
            qa=jnp.where(lane==base+j,t,qa)
        qa_ref[h]=qa.astype(jnp.bfloat16)
    o=jnp.where(low,outs[0],outs[1])
    o_ref[...]=o
    ol_ref[...]=o.astype(jnp.bfloat16)

def attend(q,kv,idx,fq,fk,heads=12):
    rows,d=q.shape
    nk=kv.shape[0]
    pairs=heads//2
    nb=nk//KB
    spec=pltpu.PrefetchScalarGridSpec(num_scalar_prefetch=1,grid=(pairs,),
        in_specs=[pl.BlockSpec((rows,128),lambda p,i:(0,p)),
                  pl.BlockSpec((nk,128),lambda p,i:(0,p)),
                  pl.BlockSpec((nk,128),lambda p,i:(0,p+pairs)),
                  pl.BlockSpec((rows,128),lambda p,i:(0,0)),
                  pl.BlockSpec((nk,128),lambda p,i:(0,0))],
        out_specs=[pl.BlockSpec((rows,128),lambda p,i:(0,p)),
                   pl.BlockSpec((rows,128),lambda p,i:(0,p)),
                   pl.BlockSpec((2,rows,128),lambda p,i:(p,0,0))],
        scratch_shapes=[pltpu.VMEM((2,nk,128),jnp.bfloat16),pltpu.VMEM((2,nk,128),jnp.bfloat16),
                        pltpu.VMEM((2,nb,rows,KB),jnp.float32),pltpu.VMEM((2,rows,128),jnp.float32),
                        pltpu.VMEM((2,rows,128),jnp.float32)])
    return pl.pallas_call(fwd_kernel,grid_spec=spec,
        out_shape=[jax.ShapeDtypeStruct((rows,d),jnp.float32),jax.ShapeDtypeStruct((rows,d),jnp.bfloat16),
                   jax.ShapeDtypeStruct((heads,rows,128),jnp.bfloat16)],
        compiler_params=pltpu.CompilerParams(vmem_limit_bytes=60<<20),
        cost_estimate=pl.CostEstimate(flops=2*2*rows*nk*256*heads,bytes_accessed=nk*d*4+rows*d*10,transcendentals=rows*nk*heads),
        name="attend")(idx,q,kv,kv,fq,fk)

def bwd_kernel(idx_ref,qa_ref,k_ref,v_ref,fk_ref,g_ref,o_ref,dq_ref,dk_ref,dv_ref,dqt):
    cnt=idx_ref[0]
    lane=lax.broadcasted_iota(jnp.int32,(1,128),1)
    low=lane<HD
    g=g_ref[...].astype(jnp.float32)
    prod=g*o_ref[...]
    gs=[]
    for h in range(2):
        own=low if h==0 else jnp.logical_not(low)
        base=HD+LSE_LANE if h==0 else LSE_LANE
        delta=jnp.sum(jnp.where(own,prod,0.0),axis=1,keepdims=True)
        hi,mid,lo=split3(-delta)
        ga=jnp.where(own,g,0.0)
        for j,t in enumerate((hi,mid,lo)):
            ga=jnp.where(lane==base+j,t,ga)
        gs.append(ga.astype(jnp.bfloat16))
    dk_ref[...]=jnp.zeros(dk_ref.shape,dk_ref.dtype)
    dv_ref[...]=jnp.zeros(dv_ref.shape,dv_ref.dtype)
    dqt[...]=jnp.zeros(dqt.shape,jnp.float32)
    qs=(qa_ref[0],qa_ref[1])
    def step(i,_):
        r=pl.ds(pl.multiple_of(idx_ref[i+1]*KB,KB),KB)
        k2=k_ref[r,:];v2=v_ref[r,:];fk=fk_ref[r,:]
        dks=[];dvs=[]
        for h in range(2):
            ka=jnp.where(low,k2,fk) if h==0 else jnp.where(low,fk,k2)
            va=jnp.where(low,v2,fk) if h==0 else jnp.where(low,fk,v2)
            st=lax.dot_general(ka,qs[h],NT,preferred_element_type=jnp.float32)
            dpt=lax.dot_general(va,gs[h],NT,preferred_element_type=jnp.float32)
            pt=jnp.exp(st)
            ds=(pt*dpt).astype(jnp.bfloat16)
            dvs.append(lax.dot_general(pt.astype(jnp.bfloat16),gs[h],NN,preferred_element_type=jnp.float32))
            dks.append(lax.dot_general(ds,qs[h],NN,preferred_element_type=jnp.float32))
            dqt[h]+=lax.dot_general(ka.T,ds,NN,preferred_element_type=jnp.float32)
        dk_ref[r,:]=jnp.where(low,dks[0],dks[1]).astype(dk_ref.dtype)
        dv_ref[r,:]=jnp.where(low,dvs[0],dvs[1]).astype(dv_ref.dtype)
        return 0
    lax.fori_loop(0,cnt,step,0)
    dq_ref[...]=(jnp.where(low,dqt[0].T,dqt[1].T)*0.125).astype(dq_ref.dtype)

def attend_back(qa,kv,idx,fk,g,o,heads=12):
    rows,d=g.shape
    nk=kv.shape[0]
    pairs=heads//2
    spec=pltpu.PrefetchScalarGridSpec(num_scalar_prefetch=1,grid=(pairs,),
        in_specs=[pl.BlockSpec((2,rows,128),lambda p,i:(p,0,0)),
                  pl.BlockSpec((nk,128),lambda p,i:(0,p)),
                  pl.BlockSpec((nk,128),lambda p,i:(0,p+pairs)),
                  pl.BlockSpec((nk,128),lambda p,i:(0,0)),
                  pl.BlockSpec((rows,128),lambda p,i:(0,p)),
                  pl.BlockSpec((rows,128),lambda p,i:(0,p))],
        out_specs=[pl.BlockSpec((rows,128),lambda p,i:(0,p)),
                   pl.BlockSpec((nk,128),lambda p,i:(0,p)),
                   pl.BlockSpec((nk,128),lambda p,i:(0,p))],
        scratch_shapes=[pltpu.VMEM((2,128,rows),jnp.float32)])
    return pl.pallas_call(bwd_kernel,grid_spec=spec,
        out_shape=[jax.ShapeDtypeStruct((rows,d),jnp.bfloat16),jax.ShapeDtypeStruct((nk,d),jnp.bfloat16),
                   jax.ShapeDtypeStruct((nk,d),jnp.bfloat16)],
        compiler_params=pltpu.CompilerParams(vmem_limit_bytes=60<<20),
        cost_estimate=pl.CostEstimate(flops=5*2*rows*nk*256*heads,bytes_accessed=nk*d*8+rows*d*10,transcendentals=rows*nk*heads),
        name="attend_back")(idx,qa,kv,kv,fk,g,o)

def features(seg_query,seg_key):
    j=jnp.arange(128,dtype=jnp.int32)[None,:]%HD
    fq=jnp.where((j<10)&(j!=seg_query[:,None]),NEG,0.0).astype(jnp.bfloat16)
    fk=(((j<10)&(j==seg_key[:,None]))|((j>=LSE_LANE)&(j<LSE_LANE+3))).astype(jnp.bfloat16)
    return fq,fk

def active(seg_query,seg_key):
    nb=seg_key.shape[0]//KB
    lo=jnp.min(seg_query);hi=jnp.max(seg_query)
    sk=seg_key.reshape(nb,KB)
    use=jnp.any((sk<0)|((sk>=lo)&(sk<=hi)),axis=1)
    slot=jnp.arange(nb,dtype=jnp.int32)
    rank=jnp.sum((use[None,:]&(slot[None,:]<slot[:,None])).astype(jnp.int32),axis=1)
    order=jnp.sum(jnp.where(use[None,:]&(rank[None,:]==slot[:,None]),slot[None,:],0),axis=1)
    return jnp.concatenate([jnp.sum(use.astype(jnp.int32))[None],order]).astype(jnp.int32)


D = 768
HEADS = 12
IMGS = 8
CLASS_ROWS = 256
WIDE = 384


def norm_rows(values, gain_row):
    centre = values - jnp.mean(values, axis=-1, keepdims=True)
    return centre * lax.rsqrt(jnp.mean(centre * centre, axis=-1, keepdims=True) + 1e-06) * gain_row


def class_norm(logits, gain_row):
    centre = logits - jnp.mean(logits, axis=-1, keepdims=True)
    return centre * lax.rsqrt(jnp.mean(centre * centre, axis=-1, keepdims=True) + 1e-05) * gain_row


def unit_rows(values):
    return values * lax.rsqrt(jnp.sum(values * values, axis=-1, keepdims=True) + 1e-06)


def dot(left, right):
    return jnp.dot(left, right, preferred_element_type=jnp.float32)


def dot_rows(left, right):
    return lax.dot_general(left, right, (((0,), (0,)), ((), ())), preferred_element_type=jnp.float32)


def dot_turned(left, right):
    return lax.dot_general(left, right, (((1,), (1,)), ((), ())), preferred_element_type=jnp.float32)


def low(values):
    return values.astype(jnp.bfloat16)


def bits_of(axis):
    return [1 << i for i in range(lax.axis_size(axis).bit_length() - 1)]


def swap(values, axis, bit):
    count = lax.axis_size(axis)
    return lax.ppermute(values, axis, [(i, i ^ bit) for i in range(count)])


def own_bit(axis, bit):
    return (lax.axis_index(axis) // bit) % 2


def gather_rows(rows):
    for bit in reversed(bits_of("seq")):
        rows = jnp.concatenate([rows, swap(rows, "seq", bit)], axis=0)
    return rows


def relative():
    order = [0]
    for bit in reversed(bits_of("seq")):
        order = order + [i ^ bit for i in order]
    return order


def scatter_rows(rows):
    for bit in bits_of("seq"):
        half = rows.shape[0] // 2
        rows = rows[:half] + swap(low(rows[half:]), "seq", bit).astype(jnp.float32)
    return rows


def segment_of(places, seq_lengths):
    count = seq_lengths.shape[0]
    before = jnp.arange(count)[None, :] <= jnp.arange(count)[:, None]
    boundary = jnp.sum(jnp.where(before, seq_lengths[None, :], 0), axis=1)
    return jnp.sum((places[:, None] >= boundary[None, :]).astype(jnp.int32), axis=1)


def bundle(shards):
    count, index = lax.axis_size("seq"), lax.axis_index("seq")
    pieces = []
    for shard in shards:
        rows = shard.shape[0] // count
        part = lax.dynamic_slice_in_dim(shard, index * rows, rows, 0)
        pieces += [part[:, i : i + D] for i in range(0, shard.shape[1], D)]
    return jnp.concatenate(pieces, axis=0)


def unbundle(gathered, shards):
    count = lax.axis_size("seq")
    devices = gathered.shape[0]
    weights, at = [], 0
    for shard in shards:
        rows, wide = shard.shape[0] // count, shard.shape[1] // D
        part = gathered[:, at : at + rows * wide].reshape(devices, wide, rows, D)
        weights.append(part.transpose(0, 2, 1, 3).reshape(devices * rows, wide * D))
        at += rows * wide
    return weights


def gather_weights(shards):
    return unbundle(lax.all_gather(bundle(shards), ("dp", "seq"), axis=0), shards)


def core_half(left, right):
    core = own_bit("seq", 1)
    half = right.shape[1] // 2
    send = lax.dynamic_slice_in_dim(right, (1 - core) * half, half, 1)
    keep = lax.dynamic_slice_in_dim(right, core * half, half, 1)
    arrived = swap(low(dot_rows(left, send)), "seq", 1)
    total = low(dot_rows(left, keep) + arrived.astype(jnp.float32))
    return [total[:, i : i + WIDE] for i in range(0, half, WIDE)]


def halve(values, dim, axis, bit):
    own = own_bit(axis, bit)
    arrived = swap(lax.dynamic_index_in_dim(values, 1 - own, dim), axis, bit)
    kept = lax.dynamic_index_in_dim(values, own, dim)
    return low(kept.astype(jnp.float32) + arrived.astype(jnp.float32))


def double(values, dim, axis, bit):
    own = own_bit(axis, bit)
    arrived = swap(values, axis, bit)
    return jnp.concatenate(
        [jnp.where(own == 0, values, arrived), jnp.where(own == 0, arrived, values)], axis=dim
    )


def reduce_weights(products):
    dp_bits, y_bits = bits_of("dp"), bits_of("seq")[1:]
    devices, y_count = lax.axis_size("dp"), lax.axis_size("seq") // 2
    pieces, shape = [], []
    for left, right in products:
        mine = core_half(left, right)
        rows = left.shape[1] // (devices * y_count)
        pieces += [t.reshape(devices, y_count, rows, WIDE) for t in mine]
        shape.append((rows, len(mine)))
    total = jnp.concatenate(pieces, axis=2)
    steps = [("dp", b, len(dp_bits) - 1 - i) for i, b in enumerate(dp_bits)]
    y_steps = [("seq", b, len(dp_bits) + len(y_bits) - 1 - i) for i, b in enumerate(y_bits)]
    cut = total.shape[2] // 2
    done = []
    for part, order in (
        (total[:, :, :cut], y_steps + steps),
        (total[:, :, cut:], steps[:1] + y_steps + steps[1:]),
    ):
        part = part.reshape((2,) * (len(dp_bits) + len(y_bits)) + part.shape[2:])
        for axis, bit, dim in order:
            part = halve(part, dim, axis, bit)
        done.append(part.reshape((1,) + part.shape[-2:]))
    mine = jnp.concatenate(done, axis=1)
    for bit in y_bits:
        mine = double(mine, 0, "seq", bit)
    other = swap(mine, "seq", 1)
    core = own_bit("seq", 1)
    sides = [jnp.where(core == 0, mine, other), jnp.where(core == 0, other, mine)]
    results, at = [], 0
    for rows, wide in shape:
        columns = [
            side[:, at + i * rows : at + (i + 1) * rows].reshape(y_count * rows, WIDE)
            for side in sides
            for i in range(wide)
        ]
        results.append(jnp.concatenate(columns, axis=1).astype(jnp.float32))
        at += rows * wide
    return results


def sum_everywhere(values):
    steps = [("seq", b) for b in bits_of("seq")] + [("dp", b) for b in bits_of("dp")]
    parts = 1 << len(steps)
    rows = values.shape[0]
    total = jnp.pad(values, ((0, -rows % parts), (0, 0)))
    if rows >= parts:
        for axis, bit in steps:
            own, half = own_bit(axis, bit), total.shape[0] // 2
            kept = lax.dynamic_slice_in_dim(total, own * half, half, 0)
            total = kept + swap(lax.dynamic_slice_in_dim(total, (1 - own) * half, half, 0), axis, bit)
        for axis, bit in reversed(steps):
            total = double(total, 0, axis, bit)
    else:
        total = values
        for axis, bit in steps:
            total = total + swap(total, axis, bit)
    return total[:rows]


def block_forward(hidden, gain_a, gain_b, weights, mask, class_normed):
    w_qkv, w_out, w_up, w_down = weights
    idx, feature_q, feature_k = mask
    normed = low(norm_rows(hidden, gain_a))
    rows_all = gather_rows(normed)
    if class_normed is not None:
        rows_all = jnp.concatenate([rows_all, class_normed], axis=0)
    queries = low(dot(normed, w_qkv[:, :D]))
    keyval = low(dot(rows_all, w_qkv[:, D:]))
    attended, attended_low, kept_q = attend(queries, keyval, idx, feature_q, feature_k)
    middle = hidden + dot(attended_low, w_out)
    second = low(norm_rows(middle, gain_b))
    upward = dot(second, w_up)
    active_rows = low(jax.nn.gelu(upward))
    result = middle + dot(active_rows, w_down)
    return result, (normed, rows_all, keyval, attended, attended_low, kept_q, middle, second, upward, active_rows)


def block_backward(grad_result, hidden, kept, gain_a, gain_b, weights, mask):
    w_qkv, w_out, w_up, w_down = weights
    idx, _, feature_k = mask
    normed, rows_all, keyval, attended, attended_low, kept_q, middle, second, upward, active_rows = kept
    grad_branch = low(grad_result)
    grad_active = dot_turned(grad_branch, w_down)
    _, gelu_back = jax.vjp(jax.nn.gelu, upward)
    grad_upward = low(gelu_back(grad_active)[0])
    mlp_products = [(second, grad_upward), (active_rows, grad_branch)]
    grad_second = dot_turned(grad_upward, w_up)
    _, second_back = jax.vjp(norm_rows, middle, gain_b)
    grad_middle, grad_gain_b = second_back(grad_second)
    grad_middle = grad_middle + grad_result
    grad_attn = low(grad_middle)
    grad_attended = low(dot_turned(grad_attn, w_out))
    grad_query, grad_key, grad_value = attend_back(kept_q, keyval, idx, feature_k, grad_attended, attended)
    grad_keyval = jnp.concatenate([grad_key, grad_value], axis=1)
    grad_all = dot_turned(grad_keyval, w_qkv[:, D:])
    token_rows = rows_all.shape[0] // hidden.shape[0] * hidden.shape[0]
    grad_class_normed = grad_all[token_rows:]
    grad_normed = dot_turned(grad_query, w_qkv[:, :D]) + scatter_rows(grad_all[:token_rows])
    attn_products = [(normed, grad_query), (rows_all, grad_keyval), (attended_low, grad_attn)]
    _, first_back = jax.vjp(norm_rows, hidden, gain_a)
    grad_hidden, grad_gain_a = first_back(grad_normed)
    return grad_hidden + grad_middle, mlp_products, attn_products, grad_gain_a, grad_gain_b, grad_class_normed


def local(
    tokens,
    lengths,
    classes,
    norm_gains,
    mask_gain,
    enc_qkv,
    enc_out,
    enc_up,
    enc_down,
    dec_qkv,
    dec_out,
    dec_up,
    dec_down,
    patch_proj,
    class_proj,
    mask_cot,
):
    enc_weights = gather_weights((enc_qkv, enc_out, enc_up, enc_down))
    *dec_weights, w_patch, w_class = gather_weights(
        (dec_qkv, dec_out, dec_up, dec_down, patch_proj, class_proj)
    )
    row_count = tokens.shape[1]
    index = lax.axis_index("seq")
    seq_lengths = lengths[0]
    inputs_f = tokens[0].astype(jnp.float32)
    gains_f = norm_gains.astype(jnp.float32)
    classes_f = classes.astype(jnp.float32)
    class_count = classes.shape[0]
    mask_gain_f = mask_gain.astype(jnp.float32)
    steps = jnp.arange(row_count, dtype=jnp.int32)
    seg_query = segment_of(index * row_count + steps, seq_lengths)
    starts = jnp.stack([(index ^ r) * row_count for r in relative()])
    seg_rows = segment_of((starts[:, None] + steps[None, :]).reshape(-1), seq_lengths)
    class_slots = jnp.arange(CLASS_ROWS, dtype=jnp.int32)
    seg_key = jnp.concatenate([seg_rows, jnp.where(class_slots < class_count, -1, IMGS + 1)])
    feature_q, feature_k = features(seg_query, seg_key)
    enc_mask = (active(seg_query, seg_rows), feature_q, feature_k[: seg_rows.shape[0]])
    dec_mask = (active(seg_query, seg_key), feature_q, feature_k)
    valid_rows = (seg_query < IMGS).astype(jnp.float32)[:, None]
    encoded, enc_kept = block_forward(inputs_f, gains_f[0], gains_f[1], enc_weights, enc_mask, None)
    class_normed = low(norm_rows(classes_f, gains_f[2]))
    class_padded = jnp.pad(class_normed, ((0, CLASS_ROWS - class_count), (0, 0)))
    decoded, dec_kept = block_forward(
        encoded, gains_f[2], gains_f[3], dec_weights, dec_mask, class_padded
    )
    final_normed = low(norm_rows(decoded, gains_f[4]))
    patch_rows = low(dot(final_normed, w_patch))
    class_rows = dot(classes, w_class)
    class_unit = low(unit_rows(class_rows))
    logits = dot_turned(patch_rows, class_unit)
    mask_out = class_norm(logits, mask_gain_f) * valid_rows
    _, head_back = jax.vjp(class_norm, logits, mask_gain_f)
    grad_logits, grad_mask_gain = head_back(mask_cot[0] * valid_rows)
    grad_logits_low = low(grad_logits)
    grad_patch_rows = low(dot(grad_logits_low, class_unit))
    grad_unit = dot_rows(grad_logits_low, patch_rows)
    grad_final = dot_turned(grad_patch_rows, w_patch)
    _, final_back = jax.vjp(norm_rows, decoded, gains_f[4])
    grad_decoded, grad_gain_last = final_back(grad_final)
    _, unit_back = jax.vjp(unit_rows, class_rows)
    grad_class_rows = low(unit_back(grad_unit)[0])
    grad_classes = dot_turned(grad_class_rows, w_class)
    grad_encoded, dec_mlp, dec_attn, grad_gain_two, grad_gain_three, grad_class_normed = block_backward(
        grad_decoded, encoded, dec_kept, gains_f[2], gains_f[3], dec_weights, dec_mask
    )
    _, class_back = jax.vjp(norm_rows, classes_f, gains_f[2])
    grad_classes_kv, grad_gain_class = class_back(grad_class_normed[:class_count])
    early = [grad_gain_two + grad_gain_class, grad_gain_three, grad_gain_last]
    padded_mask_gain = jnp.pad(grad_mask_gain, (0, D - class_count))
    shared = sum_everywhere(
        jnp.concatenate([grad_classes + grad_classes_kv, jnp.stack(early + [padded_mask_gain])], axis=0)
    )
    dec_up_down = reduce_weights(
        dec_mlp + [(final_normed, grad_patch_rows), (classes, grad_class_rows)]
    )
    dec_proj = reduce_weights(dec_attn)
    grad_inputs, enc_mlp, enc_attn, grad_gain_zero, grad_gain_one, _ = block_backward(
        grad_encoded, inputs_f, enc_kept, gains_f[0], gains_f[1], enc_weights, enc_mask
    )
    enc_up_down = reduce_weights(enc_mlp)
    enc_proj = reduce_weights(enc_attn)
    late = sum_everywhere(jnp.stack([grad_gain_zero, grad_gain_one]))
    gain_sums = jnp.concatenate([late, shared[class_count : class_count + 3]], axis=0)
    return (
        mask_out[None],
        grad_inputs[None],
        shared[:class_count],
        gain_sums,
        shared[class_count + 3, :class_count],
        jnp.concatenate(enc_proj[:2], axis=1),
        enc_proj[2],
        enc_up_down[0],
        enc_up_down[1],
        jnp.concatenate(dec_proj[:2], axis=1),
        dec_proj[2],
        dec_up_down[0],
        dec_up_down[1],
        dec_up_down[2],
        dec_up_down[3],
    )


def solution(mesh):
    placed = (
        P("dp", "seq", None),
        P("dp", None),
        P(),
        P(),
        P(),
        P("dp", None),
        P("dp", None),
        P("dp", None),
        P("dp", None),
        P("dp", None),
        P("dp", None),
        P("dp", None),
        P("dp", None),
        P("dp", None),
        P("dp", None),
        P("dp", "seq", None),
    )
    return jax.shard_map(
        local,
        mesh=mesh,
        in_specs=placed,
        out_specs=(
            P("dp", "seq", None),
            P("dp", "seq", None),
            P(),
            P(),
            P(),
            P("dp", None),
            P("dp", None),
            P("dp", None),
            P("dp", None),
            P("dp", None),
            P("dp", None),
            P("dp", None),
            P("dp", None),
            P("dp", None),
            P("dp", None),
        ),
        check_vma=False,
    )
```

time: 2350 us -> 938 us (0.40)
  waiting for transfers between devices: 1440 us -> 351 us
  matrix products: 511 us -> 158 us
  Pallas kernels: 0 us -> 181 us
  local copies, waits for them, and re-layouts: 227 us -> 101 us
  starting transfers between devices: 1.43 us -> 73.8 us
  other arithmetic: 99.1 us -> 51.4 us
  blocking collectives: 41.8 us -> 0 us
    reduce_scatter x11 -> x0, waiting for transfers between devices: 813 us -> none  [the longest x1 98.8 us: local(): lax.psum_scatter(enc_grads[3].astype(jnp.bfloat16), 'dp', scatter_dimensi...]
    dot_general x70 -> x51, matrix products: 511 us -> 158 us  [the longest x25 65.5 us: dot_rows(): lax.dot_general(left, right, (((0,), (0,)), ((), ())), preferred_element_...]
    all_gather x12 -> x2, waiting for transfers between devices: 420 us -> 79.4 us  [gather_weights(): lax.all_gather(bundle(shards), ('dp', 'seq'), axis=0)]
    ppermute x0 -> x75, waiting for transfers between devices: none -> 272 us  [swap(): return lax.ppermute(values, axis, [(i, i ^ bit) for i in range(count)])]
    pallas_call x0 -> x4, Pallas kernels: none -> 181 us  [the longest x2 95.3 us: attend_back(): pl.pallas_call(bwd_kernel, grid_spec=spec, out_shape=[jax.ShapeDtypeStruc...]
    psum x2 -> x0, waiting for transfers between devices: 144 us -> none  [the longest x1 119 us: local(): lax.psum((grad_classes + grad_classes_kv, gain_terms, grad_mask_gain), ('...]
    dynamic_update_slice x4 -> x0, local copies, waits for them, and re-layouts: 108 us -> none  [attention_step_block(): keyval_all = lax.dynamic_update_slice_in_dim(keyval_all, fresh, offset, 0)]
    ppermute x0 -> x75, starting transfers between devices: none -> 73.7 us  [swap(): return lax.ppermute(values, axis, [(i, i ^ bit) for i in range(count)])]
  transfers between devices with their start and end apart: 26 -> 77, of which waited for: 23 -> 41; matrix products, arithmetic and copies ran while one was open for 16% -> 25% of each run, Pallas kernels for 0% -> 15%
where the time goes in v1:
time: 938 us; the launch traced here: 935 us
  waiting for transfers between devices  351 us (37%)
  Pallas kernels  181 us (19%)
  matrix products  158 us (17%)
  local copies, waits for them, and re-layouts  101 us (11%)
  starting transfers between devices  73.8 us (8%)
  other arithmetic  51.4 us (5%)
  between operations  17.4 us (2%)
    ppermute x75, waiting for transfers between devices, swap(): return lax.ppermute(values, axis, [(i, i ^ bit) for i in range(count)])  272 us
    pallas_call x2, Pallas kernels, attend_back(): pl.pallas_call(bwd_kernel, grid_spec=spec, out_shape=[jax.ShapeDtypeStruc...  95.3 us
    pallas_call x2, Pallas kernels, attend(): pl.pallas_call(fwd_kernel, grid_spec=spec, out_shape=[jax.ShapeDtypeStruc...  85.7 us
    all_gather x2, waiting for transfers between devices, gather_weights(): lax.all_gather(bundle(shards), ('dp', 'seq'), axis=0)  79.4 us
    ppermute x75, starting transfers between devices, swap(): return lax.ppermute(values, axis, [(i, i ^ bit) for i in range(count)])  73.7 us
    dot_general x25, matrix products, dot_rows(): lax.dot_general(left, right, (((0,), (0,)), ((), ())), preferred_element_...  65.5 us
    unnamed x336, local copies, waits for them, and re-layouts  51.6 us
    dot_general x13, matrix products, dot(): return jnp.dot(left, right, preferred_element_type=jnp.float32)  51.3 us
  transfers between devices with their start and end apart: 77, of which 41 were waited for; matrix products, arithmetic and copies ran while one was open for 25% of the time, Pallas kernels for 15%

profile of v1, /device:TPU:0, one launch (start us, length us, event | category | flops | bytes accessed | tf_op | source)
XLA Modules:
  0.0 934.6 jit_solution(13780687603387986285)
XLA Ops:
  37.2 12.3 %collective-permute-done = bf16[512,768]{1,0:T(8,128)(2,1)S(1)} collective-permute-done((bf16[512,768]{1,0:T(8,128)(2,1)S(1)}, bf16[512,768]{1,0:T(8,128)(2,1)S(1)}, u32[]{:S(2)}, u32[]{:S(2)}) %collective-permute-start) | collective-permute-done | bytes 786464 | tf_op jit(solution)/shard_map/ppermute | solution.py:208
  52.9 70.5 %all-gather.5.cloned.1.call-done = bf16[9216,768]{1,0:T(8,128)(2,1)} async-done(((bf16[288,768]{1,0:T(8,128)(2,1)}), bf16[9216,768]{1,0:T(8,128)(2,1)}) %all-gather.5.cloned.1.call-update) | async-done | bytes 14155792 | tf_op jit(solution)/shard_map/all_gather | solution.py:265
  129.2 6.6 fusion.195
  146.6 8.5 convolution_convert_fusion.1.k_ref.v_ref
  155.0 40.7 %attend.2 = (f32[512,768]{1,0:T(8,128)}, bf16[512,768]{1,0:T(8,128)(2,1)}, bf16[12,512,128]{2,1,0:T(8,128)(2,1)}) custom-call(s32[9]{0:T(128)} %pad_add_fusion.2.idx_ref, bf16[512,768]{1,0:T(8,128)(2,1)} %convolution_convert_fusion.10.q_ref, bf16[2048,1536]{1,0:T(8,128)(2,1)} %convolution_convert_fusion.1.k_ref.v_ref, ...), custom_call_target="tpu_custom_call" | custom-call | flops 12884901888 | bytes 10223616 | tf_op jit(solution)/shard_map/attend/pallas_call | solution.py:79
  198.1 9.0 multiply_convert_fusion.1
  212.2 22.4 %collective-permute-done.2 = bf16[512,768]{1,0:T(8,128)(2,1)S(1)} collective-permute-done((bf16[512,768]{1,0:T(8,128)(2,1)S(1)}, bf16[512,768]{1,0:T(8,128)(2,1)S(1)}, u32[]{:S(2)}, u32[]{:S(2)}) %collective-permute-start.2) | collective-permute-done | bytes 786464 | tf_op jit(solution)/shard_map/ppermute | solution.py:208
  236.0 9.0 all-gather.7.cloned.1.call-done
  270.9 12.7 %convolution_convert_fusion.k_ref.v_ref = bf16[2304,1536]{1,0:T(8,128)(2,1)} fusion(bf16[768,2304]{1,0:T(8,128)(2,1)S(1)} %bitcast.283, bf16[150,768]{1,0:T(8,128)(2,1)S(1)} %fusion.85, bf16[1024,768]{1,0:T(8,128)(2,1)} %collective-permute-done.3, bf16[512,768]{1,0:T(8,128)(2,1)S(1)} %copy-done.64, bf16[512,768]{1,0:T(8,128)(2,1)S(1)} %copy-done.31), kind=kOutput, calls=%fused_computation | convolution fusion | flops 5457051648 | bytes 12816384 | tf_op jit(solution)/shard_map/dot_general | solution.py:187
  283.6 45.0 %attend.3 = (f32[512,768]{1,0:T(8,128)}, bf16[512,768]{1,0:T(8,128)(2,1)}, bf16[12,512,128]{2,1,0:T(8,128)(2,1)}) custom-call(s32[10]{0:T(128)} %pad_add_fusion.3.idx_ref, bf16[512,768]{1,0:T(8,128)(2,1)} %convolution_convert_fusion.9.q_ref, bf16[2304,1536]{1,0:T(8,128)(2,1)} %convolution_convert_fusion.k_ref.v_ref, ...), custom_call_target="tpu_custom_call" | custom-call | flops 14495514624 | bytes 11010048 | tf_op jit(solution)/shard_map/attend/pallas_call | solution.py:79
  370.5 50.4 %attend_back.2 = (bf16[512,768]{1,0:T(8,128)(2,1)}, bf16[2304,768]{1,0:T(8,128)(2,1)}, bf16[2304,768]{1,0:T(8,128)(2,1)}) custom-call(s32[10]{0:T(128)} %pad_add_fusion.3.idx_ref, bf16[12,512,128]{2,1,0:T(8,128)(2,1)} %get-tuple-element.30.qa_ref, bf16[2304,1536]{1,0:T(8,128)(2,1)} %convolution_convert_fusion.k_ref.v_ref, ...), custom_call_target="tpu_custom_call" | custom-call | flops 36238786560 | bytes 18087936 | tf_op jit(solution)/shard_map/attend_back/pallas_call | solution.py:141
  495.8 7.0 collective-permute-done.56
  529.9 6.6 fusion.7
  543.4 45.0 %attend_back.3 = (bf16[512,768]{1,0:T(8,128)(2,1)}, bf16[2048,768]{1,0:T(8,128)(2,1)}, bf16[2048,768]{1,0:T(8,128)(2,1)}) custom-call(s32[9]{0:T(128)} %pad_add_fusion.2.idx_ref, bf16[12,512,128]{2,1,0:T(8,128)(2,1)} %get-tuple-element.29.qa_ref, bf16[2048,1536]{1,0:T(8,128)(2,1)} %convolution_convert_fusion.1.k_ref.v_ref, ...), custom_call_target="tpu_custom_call" | custom-call | flops 32212254720 | bytes 16515072 | tf_op jit(solution)/shard_map/attend_back/pallas_call | solution.py:141
  689.1 26.5 %collective-permute-done.63 = bf16[2,2,2,1,240,384]{5,4,3,2,1,0:T(8,128)(2,1)S(1)} collective-permute-done((bf16[2,2,2,1,240,384]{5,4,3,2,1,0:T(8,128)(2,1)S(1)}, bf16[2,2,2,1,240,384]{5,4,3,2,1,0:T(8,128)(2,1)S(1)}, u32[]{:S(2)}, u32[]{:S(2)}) %collective-permute-start.63) | collective-permute-done | bytes 1474592 | tf_op jit(solution)/shard_map/ppermute | solution.py:208
  719.0 9.2 collective-permute-done.25
  731.6 20.2 %collective-permute-done.26 = bf16[2,2,1,1,96,384]{5,4,3,2,1,0:T(8,128)(2,1)S(1)} collective-permute-done((bf16[2,2,1,1,96,384]{5,4,3,2,1,0:T(8,128)(2,1)S(1)}, bf16[2,2,1,1,96,384]{5,4,3,2,1,0:T(8,128)(2,1)S(1)}, u32[]{:S(2)}, u32[]{:S(2)}) %collective-permute-start.26) | collective-permute-done | bytes 294944 | tf_op jit(solution)/shard_map/ppermute | solution.py:208
  801.7 22.2 %collective-permute-done.19 = f32[2,768]{1,0:T(2,128)S(1)} collective-permute-done((f32[2,768]{1,0:T(2,128)S(1)}, f32[2,768]{1,0:T(2,128)S(1)}, u32[]{:S(2)}, u32[]{:S(2)}) %collective-permute-start.19) | collective-permute-done | bytes 6176 | tf_op jit(solution)/shard_map/ppermute | solution.py:208
  841.6 12.9 %collective-permute-done.72 = bf16[1,1,1,1,240,384]{5,4,3,2,1,0:T(8,128)(2,1)S(1)} collective-permute-done((bf16[1,1,1,1,240,384]{5,4,3,2,1,0:T(8,128)(2,1)S(1)}, bf16[1,1,1,1,240,384]{5,4,3,2,1,0:T(8,128)(2,1)S(1)}, u32[]{:S(2)}, u32[]{:S(2)}) %collective-permute-start.72) | collective-permute-done | bytes 184352 | tf_op jit(solution)/shard_map/ppermute | solution.py:208
  860.5 8.3 collective-permute-done.73
  871.7 13.7 %collective-permute-done.38 = bf16[2,2,1,1,192,384]{5,4,3,2,1,0:T(8,128)(2,1)S(1)} collective-permute-done((bf16[2,2,1,1,192,384]{5,4,3,2,1,0:T(8,128)(2,1)S(1)}, bf16[2,2,1,1,192,384]{5,4,3,2,1,0:T(8,128)(2,1)S(1)}, u32[]{:S(2)}, u32[]{:S(2)}) %collective-permute-start.38) | collective-permute-done | bytes 589856 | tf_op jit(solution)/shard_map/ppermute | solution.py:208
  888.0 7.6 collective-permute-done.39
  904.6 7.8 collective-permute-done.45
  913.0 8.4 collective-permute-done.46
  (792 shorter events, 434.7 us)
Async XLA Ops:
  7.2 116.2 %all-gather.5.cloned.1.call-start = ((), (), s32[]{:S(2)}) async-start(), calls=%async_computation | async-start | bytes 14598144 | tf_op jit(solution)/shard_map/all_gather | solution.py:265
  15.2 229.8 %all-gather.7.cloned.1.call-start = ((), (), s32[]{:S(2)}) async-start(), calls=%async_computation.1 | async-start | bytes 17031168 | tf_op jit(solution)/shard_map/all_gather | solution.py:265
  50.9 95.3 %collective-permute-start.1 = (bf16[1024,768]{1,0:T(8,128)(2,1)}, bf16[1024,768]{1,0:T(8,128)(2,1)}, u32[]{:S(2)}, u32[]{:S(2)}) collective-permute-start(bf16[1024,768]{1,0:T(8,128)(2,1)} %pad_maximum_fusion.4), channel_id=1, source_target_pairs={{0,8},{8,0},{16,24},{24,16},{1,9},{9,1},{17,25},{25,17},{2,10},{10... | collective-permute-start | bytes 4718600 | tf_op jit(solution)/shard_map/ppermute | solution.py:208
  236.0 34.9 %collective-permute-start.3 = (bf16[1024,768]{1,0:T(8,128)(2,1)}, bf16[1024,768]{1,0:T(8,128)(2,1)}, u32[]{:S(2)}, u32[]{:S(2)}) collective-permute-start(bf16[1024,768]{1,0:T(8,128)(2,1)} %pad_maximum_fusion.5), channel_id=1, source_target_pairs={{0,8},{8,0},{16,24},{24,16},{1,9},{9,1},{17,25},{25,17},{2,10},{10... | collective-permute-start | bytes 4718600 | tf_op jit(solution)/shard_map/ppermute | solution.py:208
  370.0 93.9 %collective-permute-start.68 = (bf16[768,384]{0,1:T(8,128)(2,1)}, bf16[768,384]{0,1:T(8,128)(2,1)}, u32[]{:S(2)}, u32[]{:S(2)}) collective-permute-start(bf16[768,384]{0,1:T(8,128)(2,1)} %fusion.64), channel_id=1, source_target_pairs={{0,8},{8,0},{16,24},{24,16},{1,9},{9,1},{17,25},{25,17},{2,10},{10... | collective-permute-start | bytes 1769480 | tf_op jit(solution)/shard_map/ppermute | solution.py:208
  370.0 80.6 %collective-permute-start.67 = (bf16[768,384]{1,0:T(8,128)(2,1)}, bf16[768,384]{1,0:T(8,128)(2,1)}, u32[]{:S(2)}, u32[]{:S(2)}) collective-permute-start(bf16[768,384]{1,0:T(8,128)(2,1)} %convolution_convert_fusion.13), channel_id=1, source_target_pairs={{0,8},{8,0},{16,24},{24,16},{1,9},{9,1},{17,25},{25,17},{2,10},{10... | collective-permute-start | bytes 1769480 | tf_op jit(solution)/shard_map/ppermute | solution.py:208
  450.6 65.4 %collective-permute-start.62 = (bf16[3072,384]{1,0:T(8,128)(2,1)}, bf16[3072,384]{1,0:T(8,128)(2,1)}, u32[]{:S(2)}, u32[]{:S(2)}) collective-permute-start(bf16[3072,384]{1,0:T(8,128)(2,1)} %convolution_convert_fusion.2), channel_id=1, source_target_pairs={{0,8},{8,0},{16,24},{24,16},{1,9},{9,1},{17,25},{25,17},{2,10},{10... | collective-permute-start | bytes 7077896 | tf_op jit(solution)/shard_map/ppermute | solution.py:208
  453.9 148.4 %collective-permute-start.61 = (bf16[768,1536]{1,0:T(8,128)(2,1)}, bf16[768,1536]{1,0:T(8,128)(2,1)}, u32[]{:S(2)}, u32[]{:S(2)}) collective-permute-start(bf16[768,1536]{1,0:T(8,128)(2,1)} %convolution_convert_fusion.4), channel_id=1, source_target_pairs={{0,8},{8,0},{16,24},{24,16},{1,9},{9,1},{17,25},{25,17},{2,10},{10... | collective-permute-start | bytes 7077896 | tf_op jit(solution)/shard_map/ppermute | solution.py:208
  472.2 54.3 %collective-permute-start.5 = (bf16[512,768]{1,0:T(8,128)(2,1)S(1)}, bf16[512,768]{1,0:T(8,128)(2,1)S(1)}, u32[]{:S(2)}, u32[]{:S(2)}) collective-permute-start(bf16[512,768]{1,0:T(8,128)(2,1)S(1)} %slice.566), channel_id=1, source_target_pairs={{0,16},{8,24},{16,0},{24,8},{1,17},{9,25},{17,1},{25,9},{2,18},{10... | collective-permute-start | bytes 2359304 | tf_op jit(solution)/shard_map/ppermute | solution.py:208
  515.5 112.4 %collective-permute-start.59 = (bf16[1,192,384]{2,1,0:T(8,128)(2,1)}, bf16[1,192,384]{2,1,0:T(8,128)(2,1)}, u32[]{:S(2)}, u32[]{:S(2)}) collective-permute-start(bf16[1,192,384]{2,1,0:T(8,128)(2,1)} %pad_maximum_fusion.15), channel_id=1, source_target_pairs={{0,16},{8,24},{16,0},{24,8},{1,17},{9,25},{17,1},{25,9},{2,18},{10... | collective-permute-start | bytes 442376 | tf_op jit(solution)/shard_map/ppermute | solution.py:208
  522.4 163.1 %collective-permute-start.69 = (bf16[2,2,1,2,240,384]{5,4,3,2,1,0:T(8,128)(2,1)}, bf16[2,2,1,2,240,384]{5,4,3,2,1,0:T(8,128)(2,1)}, u32[]{:S(2)}, u32[]{:S(2)}) collective-permute-start(bf16[2,2,1,2,240,384]{5,4,3,2,1,0:T(8,128)(2,1)} %constant_dynamic-slice_fusion.3), channel_id=1, source_target_pairs={{0,1},{1,0},{2,3},{3,2},{4,5},{5,4},{6,7},{7,6},{8,9},{9,8},{10,11... | collective-permute-start | bytes 4423688 | tf_op jit(solution)/shard_map/ppermute | solution.py:208
  608.4 59.0 %collective-permute-start.29 = (bf16[768,384]{1,0:T(8,128)(2,1)}, bf16[768,384]{1,0:T(8,128)(2,1)}, u32[]{:S(2)}, u32[]{:S(2)}) collective-permute-start(bf16[768,384]{1,0:T(8,128)(2,1)} %convolution_convert_fusion.16), channel_id=1, source_target_pairs={{0,8},{8,0},{16,24},{24,16},{1,9},{9,1},{17,25},{25,17},{2,10},{10... | collective-permute-start | bytes 1769480 | tf_op jit(solution)/shard_map/ppermute | solution.py:208
  608.8 64.4 %collective-permute-start.23 = (bf16[768,384]{1,0:T(8,128)(2,1)}, bf16[768,384]{1,0:T(8,128)(2,1)S(1)}, u32[]{:S(2)}, u32[]{:S(2)}) collective-permute-start(bf16[768,384]{1,0:T(8,128)(2,1)} %convolution_convert_fusion.17), channel_id=1, source_target_pairs={{0,8},{8,0},{16,24},{24,16},{1,9},{9,1},{17,25},{25,17},{2,10},{10... | collective-permute-start | bytes 1769480 | tf_op jit(solution)/shard_map/ppermute | solution.py:208
  629.3 163.5 %collective-permute-start.36 = (bf16[768,1536]{1,0:T(8,128)(2,1)S(1)}, bf16[768,1536]{1,0:T(8,128)(2,1)S(1)}, u32[]{:S(2)}, u32[]{:S(2)}) collective-permute-start(bf16[768,1536]{1,0:T(8,128)(2,1)S(1)} %copy-done.110), channel_id=1, source_target_pairs={{0,8},{8,0},{16,24},{24,16},{1,9},{9,1},{17,25},{25,17},{2,10},{10... | collective-permute-start | bytes 7077896 | tf_op jit(solution)/shard_map/ppermute | solution.py:208
  673.2 122.6 %collective-permute-start.41 = (bf16[3072,384]{1,0:T(8,128)(2,1)S(1)}, bf16[3072,384]{1,0:T(8,128)(2,1)}, u32[]{:S(2)}, u32[]{:S(2)}) collective-permute-start(bf16[3072,384]{1,0:T(8,128)(2,1)S(1)} %copy-done.109), channel_id=1, source_target_pairs={{0,8},{8,0},{16,24},{24,16},{1,9},{9,1},{17,25},{25,17},{2,10},{10... | collective-permute-start | bytes 7077896 | tf_op jit(solution)/shard_map/ppermute | solution.py:208
  677.7 40.6 %collective-permute-start.6 = (bf16[1024,768]{1,0:T(8,128)(2,1)S(1)}, bf16[1024,768]{1,0:T(8,128)(2,1)S(1)}, u32[]{:S(2)}, u32[]{:S(2)}) collective-permute-start(bf16[1024,768]{1,0:T(8,128)(2,1)S(1)} %slice.563), channel_id=1, source_target_pairs={{0,8},{8,0},{16,24},{24,16},{1,9},{9,1},{17,25},{25,17},{2,10},{10... | collective-permute-start | bytes 4718600 | tf_op jit(solution)/shard_map/ppermute | solution.py:208
  680.5 35.1 %collective-permute-start.63 = (bf16[2,2,2,1,240,384]{5,4,3,2,1,0:T(8,128)(2,1)S(1)}, bf16[2,2,2,1,240,384]{5,4,3,2,1,0:T(8,128)(2,1)S(1)}, u32[]{:S(2)}, u32[]{:S(2)}) collective-permute-start(bf16[2,2,2,1,240,384]{5,4,3,2,1,0:T(8,128)(2,1)S(1)} %constant_dynamic-slice_fusion.7), channel_id=1, source_target_pairs={{0,16},{8,24},{16,0},{24,8},{1,17},{9,25},{17,1},{25,9},{2,18},{10... | collective-permute-start | bytes 4423688 | tf_op jit(solution)/shard_map/ppermute | solution.py:208
  685.5 42.7 %collective-permute-start.25 = (bf16[2,2,2,1,96,384]{5,4,3,2,1,0:T(8,128)(2,1)S(1)}, bf16[2,2,2,1,96,384]{5,4,3,2,1,0:T(8,128)(2,1)S(1)}, u32[]{:S(2)}, u32[]{:S(2)}) collective-permute-start(bf16[2,2,2,1,96,384]{5,4,3,2,1,0:T(8,128)(2,1)S(1)} %fusion.77), channel_id=1, source_target_pairs={{0,16},{8,24},{16,0},{24,8},{1,17},{9,25},{17,1},{25,9},{2,18},{10... | collective-permute-start | bytes 1769480 | tf_op jit(solution)/shard_map/ppermute | solution.py:208
  718.2 47.0 %collective-permute-start.70 = (bf16[2,2,1,1,240,384]{5,4,3,2,1,0:T(8,128)(2,1)S(1)}, bf16[2,2,1,1,240,384]{5,4,3,2,1,0:T(8,128)(2,1)S(1)}, u32[]{:S(2)}, u32[]{:S(2)}) collective-permute-start(bf16[2,2,1,1,240,384]{5,4,3,2,1,0:T(8,128)(2,1)S(1)} %constant_dynamic-slice_fusion.2), channel_id=1, source_target_pairs={{0,16},{8,24},{16,0},{24,8},{1,17},{9,25},{17,1},{25,9},{2,18},{10... | collective-permute-start | bytes 2211848 | tf_op jit(solution)/shard_map/ppermute | solution.py:208
  728.3 45.8 %collective-permute-start.64 = (bf16[2,2,1,1,240,384]{5,4,3,2,1,0:T(8,128)(2,1)S(1)}, bf16[2,2,1,1,240,384]{5,4,3,2,1,0:T(8,128)(2,1)S(1)}, u32[]{:S(2)}, u32[]{:S(2)}) collective-permute-start(bf16[2,2,1,1,240,384]{5,4,3,2,1,0:T(8,128)(2,1)S(1)} %constant_dynamic-slice_fusion.6), channel_id=1, source_target_pairs={{0,1},{1,0},{2,3},{3,2},{4,5},{5,4},{6,7},{7,6},{8,9},{9,8},{10,11... | collective-permute-start | bytes 2211848 | tf_op jit(solution)/shard_map/ppermute | solution.py:208
  772.8 65.2 %collective-permute-start.71 = (bf16[2,1,1,1,240,384]{5,4,3,2,1,0:T(8,128)(2,1)S(1)}, bf16[2,1,1,1,240,384]{5,4,3,2,1,0:T(8,128)(2,1)S(1)}, u32[]{:S(2)}, u32[]{:S(2)}) collective-permute-start(bf16[2,1,1,1,240,384]{5,4,3,2,1,0:T(8,128)(2,1)S(1)} %constant_dynamic-slice_fusion.1), channel_id=1, source_target_pairs={{0,2},{1,3},{2,0},{3,1},{4,6},{5,7},{6,4},{7,5},{8,10},{9,11},{10,... | collective-permute-start | bytes 1105928 | tf_op jit(solution)/shard_map/ppermute | solution.py:208
  787.7 53.4 %collective-permute-start.65 = (bf16[2,1,1,1,240,384]{5,4,3,2,1,0:T(8,128)(2,1)S(1)}, bf16[2,1,1,1,240,384]{5,4,3,2,1,0:T(8,128)(2,1)S(1)}, u32[]{:S(2)}, u32[]{:S(2)}) collective-permute-start(bf16[2,1,1,1,240,384]{5,4,3,2,1,0:T(8,128)(2,1)S(1)} %constant_dynamic-slice_fusion.5), channel_id=1, source_target_pairs={{0,2},{1,3},{2,0},{3,1},{4,6},{5,7},{6,4},{7,5},{8,10},{9,11},{10,... | collective-permute-start | bytes 1105928 | tf_op jit(solution)/shard_map/ppermute | solution.py:208
  788.3 49.5 %collective-permute-start.34 = (bf16[1,192,384]{2,1,0:T(8,128)(2,1)S(1)}, bf16[1,192,384]{2,1,0:T(8,128)(2,1)S(1)}, u32[]{:S(2)}, u32[]{:S(2)}) collective-permute-start(bf16[1,192,384]{2,1,0:T(8,128)(2,1)S(1)} %pad_maximum_fusion.14), channel_id=1, source_target_pairs={{0,16},{8,24},{16,0},{24,8},{1,17},{9,25},{17,1},{25,9},{2,18},{10... | collective-permute-start | bytes 442376 | tf_op jit(solution)/shard_map/ppermute | solution.py:208
  795.7 73.5 %collective-permute-start.37 = (bf16[2,2,2,1,192,384]{5,4,3,2,1,0:T(8,128)(2,1)S(1)}, bf16[2,2,2,1,192,384]{5,4,3,2,1,0:T(8,128)(2,1)S(1)}, u32[]{:S(2)}, u32[]{:S(2)}) collective-permute-start(bf16[2,2,2,1,192,384]{5,4,3,2,1,0:T(8,128)(2,1)S(1)} %constant_dynamic-slice_fusion.21), channel_id=1, source_target_pairs={{0,16},{8,24},{16,0},{24,8},{1,17},{9,25},{17,1},{25,9},{2,18},{10... | collective-permute-start | bytes 3538952 | tf_op jit(solution)/shard_map/ppermute | solution.py:208
  (194 other events, 2514.0 us)
Sparse Core Ops, SparseCore 0:
  15.3 108.0 all-gather.4
  126.9 118.0 all-gather.6

commit v2 on v1

v2 whole, which is shorter than its diff:
```python
import functools
import math

import jax
import jax.numpy as jnp
from jax import lax
from jax.experimental import pallas as pl
from jax.experimental.pallas import tpu as pltpu
from jax.sharding import PartitionSpec as P
HD=64
KB=256
LSE_LANE=10
NEG=-1e30
NT=(((1,),(1,)),((),()))
NN=(((1,),(0,)),((),()))

def split3(v):
    hi=v.astype(jnp.bfloat16).astype(jnp.float32)
    mid=(v-hi).astype(jnp.bfloat16).astype(jnp.float32)
    return hi,mid,v-hi-mid

def fwd_kernel(idx_ref,q_ref,k_ref,v_ref,fq_ref,fk_ref,o_ref,ol_ref,qa_ref,ka,va,s_ref,m_ref,acc_ref):
    rows=q_ref.shape[0]
    cnt=idx_ref[0]
    lane=lax.broadcasted_iota(jnp.int32,(1,128),1)
    low=lane<HD
    q2=q_ref[...]*jnp.bfloat16(0.125)
    fq=fq_ref[...]
    qs=(jnp.where(low,q2,fq),jnp.where(low,fq,q2))
    k2=k_ref[...];v2=v_ref[...];fk=fk_ref[...]
    ka[0]=jnp.where(low,k2,fk);ka[1]=jnp.where(low,fk,k2)
    va[0]=jnp.where(low,v2,fk);va[1]=jnp.where(low,fk,v2)
    m_ref[...]=jnp.full(m_ref.shape,2*NEG,jnp.float32)
    def first(i,_):
        r=pl.ds(pl.multiple_of(idx_ref[i+1]*KB,KB),KB)
        for h in range(2):
            s=lax.dot_general(qs[h],ka[h,r,:],NT,preferred_element_type=jnp.float32)
            s_ref[h,i]=s
            m_ref[h]=jnp.maximum(m_ref[h],jnp.maximum(s[:,:128],s[:,128:]))
        return 0
    lax.fori_loop(0,cnt,first,0)
    tops=[jnp.max(m_ref[h],axis=1,keepdims=True) for h in range(2)]
    acc_ref[...]=jnp.zeros(acc_ref.shape,jnp.float32)
    def second(i,_):
        r=pl.ds(pl.multiple_of(idx_ref[i+1]*KB,KB),KB)
        for h in range(2):
            p=jnp.exp(s_ref[h,i]-tops[h]).astype(jnp.bfloat16)
            acc_ref[h]+=lax.dot_general(p,va[h,r,:],NN,preferred_element_type=jnp.float32)
        return 0
    lax.fori_loop(0,cnt,second,0)
    outs=[]
    for h in range(2):
        base=HD+LSE_LANE if h==0 else LSE_LANE
        acc=acc_ref[h]
        total=acc[:,base:base+1]
        outs.append(acc/total)
        hi,mid,lo=split3(-(tops[h]+jnp.log(total)))
        qa=qs[h].astype(jnp.float32)
        for j,t in enumerate((hi,mid,lo)):
            qa=jnp.where(lane==base+j,t,qa)
        qa_ref[h]=qa.astype(jnp.bfloat16)
    o=jnp.where(low,outs[0],outs[1])
    o_ref[...]=o
    ol_ref[...]=o.astype(jnp.bfloat16)

def attend(q,kv,idx,fq,fk,heads=12):
    rows,d=q.shape
    nk=kv.shape[0]
    pairs=heads//2
    nb=nk//KB
    spec=pltpu.PrefetchScalarGridSpec(num_scalar_prefetch=1,grid=(pairs,),
        in_specs=[pl.BlockSpec((rows,128),lambda p,i:(0,p)),
                  pl.BlockSpec((nk,128),lambda p,i:(0,p)),
                  pl.BlockSpec((nk,128),lambda p,i:(0,p+pairs)),
                  pl.BlockSpec((rows,128),lambda p,i:(0,0)),
                  pl.BlockSpec((nk,128),lambda p,i:(0,0))],
        out_specs=[pl.BlockSpec((rows,128),lambda p,i:(0,p)),
                   pl.BlockSpec((rows,128),lambda p,i:(0,p)),
                   pl.BlockSpec((2,rows,128),lambda p,i:(p,0,0))],
        scratch_shapes=[pltpu.VMEM((2,nk,128),jnp.bfloat16),pltpu.VMEM((2,nk,128),jnp.bfloat16),
                        pltpu.VMEM((2,nb,rows,KB),jnp.float32),pltpu.VMEM((2,rows,128),jnp.float32),
                        pltpu.VMEM((2,rows,128),jnp.float32)])
    return pl.pallas_call(fwd_kernel,grid_spec=spec,
        out_shape=[jax.ShapeDtypeStruct((rows,d),jnp.float32),jax.ShapeDtypeStruct((rows,d),jnp.bfloat16),
                   jax.ShapeDtypeStruct((heads,rows,128),jnp.bfloat16)],
        compiler_params=pltpu.CompilerParams(vmem_limit_bytes=60<<20),
        cost_estimate=pl.CostEstimate(flops=rows*nk,bytes_accessed=rows*d,transcendentals=0),
        name="attend")(idx,q,kv,kv,fq,fk)

def bwd_kernel(idx_ref,qa_ref,k_ref,v_ref,fk_ref,g_ref,o_ref,dq_ref,dk_ref,dv_ref,dqt):
    cnt=idx_ref[0]
    lane=lax.broadcasted_iota(jnp.int32,(1,128),1)
    low=lane<HD
    g=g_ref[...].astype(jnp.float32)
    prod=g*o_ref[...]
    gs=[]
    for h in range(2):
        own=low if h==0 else jnp.logical_not(low)
        base=HD+LSE_LANE if h==0 else LSE_LANE
        delta=jnp.sum(jnp.where(own,prod,0.0),axis=1,keepdims=True)
        hi,mid,lo=split3(-delta)
        ga=jnp.where(own,g,0.0)
        for j,t in enumerate((hi,mid,lo)):
            ga=jnp.where(lane==base+j,t,ga)
        gs.append(ga.astype(jnp.bfloat16))
    dk_ref[...]=jnp.zeros(dk_ref.shape,dk_ref.dtype)
    dv_ref[...]=jnp.zeros(dv_ref.shape,dv_ref.dtype)
    dqt[...]=jnp.zeros(dqt.shape,jnp.float32)
    qs=(qa_ref[0],qa_ref[1])
    def step(i,_):
        r=pl.ds(pl.multiple_of(idx_ref[i+1]*KB,KB),KB)
        k2=k_ref[r,:];v2=v_ref[r,:];fk=fk_ref[r,:]
        dks=[];dvs=[]
        for h in range(2):
            ka=jnp.where(low,k2,fk) if h==0 else jnp.where(low,fk,k2)
            va=jnp.where(low,v2,fk) if h==0 else jnp.where(low,fk,v2)
            st=lax.dot_general(ka,qs[h],NT,preferred_element_type=jnp.float32)
            dpt=lax.dot_general(va,gs[h],NT,preferred_element_type=jnp.float32)
            pt=jnp.exp(st)
            ds=(pt*dpt).astype(jnp.bfloat16)
            dvs.append(lax.dot_general(pt.astype(jnp.bfloat16),gs[h],NN,preferred_element_type=jnp.float32))
            dks.append(lax.dot_general(ds,qs[h],NN,preferred_element_type=jnp.float32))
            dqt[h]+=lax.dot_general(ka.T,ds,NN,preferred_element_type=jnp.float32)
        dk_ref[r,:]=jnp.where(low,dks[0],dks[1]).astype(dk_ref.dtype)
        dv_ref[r,:]=jnp.where(low,dvs[0],dvs[1]).astype(dv_ref.dtype)
        return 0
    lax.fori_loop(0,cnt,step,0)
    dq_ref[...]=(jnp.where(low,dqt[0].T,dqt[1].T)*0.125).astype(dq_ref.dtype)

def attend_back(qa,kv,idx,fk,g,o,first,count,heads=12):
    rows,d=g.shape
    nk=kv.shape[0]
    pairs=heads//2
    spec=pltpu.PrefetchScalarGridSpec(num_scalar_prefetch=1,grid=(count,),
        in_specs=[pl.BlockSpec((2,rows,128),lambda p,i:(p+first,0,0)),
                  pl.BlockSpec((nk,128),lambda p,i:(0,p+first)),
                  pl.BlockSpec((nk,128),lambda p,i:(0,p+first+pairs)),
                  pl.BlockSpec((nk,128),lambda p,i:(0,0)),
                  pl.BlockSpec((rows,128),lambda p,i:(0,p+first)),
                  pl.BlockSpec((rows,128),lambda p,i:(0,p+first))],
        out_specs=[pl.BlockSpec((rows,128),lambda p,i:(0,p)),
                   pl.BlockSpec((nk,128),lambda p,i:(0,p)),
                   pl.BlockSpec((nk,128),lambda p,i:(0,p))],
        scratch_shapes=[pltpu.VMEM((2,128,rows),jnp.float32)])
    return pl.pallas_call(bwd_kernel,grid_spec=spec,
        out_shape=[jax.ShapeDtypeStruct((rows,128*count),jnp.bfloat16),jax.ShapeDtypeStruct((nk,128*count),jnp.bfloat16),
                   jax.ShapeDtypeStruct((nk,128*count),jnp.bfloat16)],
        compiler_params=pltpu.CompilerParams(vmem_limit_bytes=60<<20),
        cost_estimate=pl.CostEstimate(flops=rows*nk,bytes_accessed=rows*d,transcendentals=0),
        name="attend_back")(idx,qa,kv,kv,fk,g,o)

def features(seg_query,seg_key):
    j=jnp.arange(128,dtype=jnp.int32)[None,:]%HD
    fq=jnp.where((j<10)&(j!=seg_query[:,None]),NEG,0.0).astype(jnp.bfloat16)
    fk=(((j<10)&(j==seg_key[:,None]))|((j>=LSE_LANE)&(j<LSE_LANE+3))).astype(jnp.bfloat16)
    return fq,fk

def active(seg_query,seg_key):
    nb=seg_key.shape[0]//KB
    lo=jnp.min(seg_query);hi=jnp.max(seg_query)
    sk=seg_key.reshape(nb,KB)
    use=jnp.any((sk<0)|((sk>=lo)&(sk<=hi)),axis=1)
    slot=jnp.arange(nb,dtype=jnp.int32)
    rank=jnp.sum((use[None,:]&(slot[None,:]<slot[:,None])).astype(jnp.int32),axis=1)
    order=jnp.sum(jnp.where(use[None,:]&(rank[None,:]==slot[:,None]),slot[None,:],0),axis=1)
    return jnp.concatenate([jnp.sum(use.astype(jnp.int32))[None],order]).astype(jnp.int32)


D = 768
HEADS = 12
IMGS = 8
CLASS_ROWS = 256
WIDE = 384


def norm_rows(values, gain_row):
    centre = values - jnp.mean(values, axis=-1, keepdims=True)
    return centre * lax.rsqrt(jnp.mean(centre * centre, axis=-1, keepdims=True) + 1e-06) * gain_row


def class_norm(logits, gain_row):
    centre = logits - jnp.mean(logits, axis=-1, keepdims=True)
    return centre * lax.rsqrt(jnp.mean(centre * centre, axis=-1, keepdims=True) + 1e-05) * gain_row


def unit_rows(values):
    return values * lax.rsqrt(jnp.sum(values * values, axis=-1, keepdims=True) + 1e-06)


def dot(left, right):
    return jnp.dot(left, right, preferred_element_type=jnp.float32)


def dot_rows(left, right):
    return lax.dot_general(left, right, (((0,), (0,)), ((), ())), preferred_element_type=jnp.float32)


def dot_turned(left, right):
    return lax.dot_general(left, right, (((1,), (1,)), ((), ())), preferred_element_type=jnp.float32)


def low(values):
    return values.astype(jnp.bfloat16)


BOTH = ("dp", "seq")


def bits_of(count):
    return [1 << i for i in range(count.bit_length() - 1)]


def seq_bits():
    return bits_of(lax.axis_size("seq"))


def chip_bits():
    return bits_of(lax.axis_size("seq") * lax.axis_size("dp"))[1:]


def swap(values, mask):
    inner, outer = lax.axis_size("seq"), lax.axis_size("dp")
    place = [(i % inner) * outer + i // inner for i in range(inner * outer)]
    pairs = [(place[i], place[i ^ mask]) for i in range(inner * outer)]
    return lax.ppermute(values, ("seq", "dp"), pairs)


def own_bit(bit):
    return (lax.axis_index(BOTH) // bit) % 2


def masks_of(bits):
    masks = [0]
    for bit in bits:
        masks = masks + [m | bit for m in masks]
    return masks


def groups_of(bits):
    return [bits[i : i + 2] for i in range(0, len(bits), 2)]


def absolute(pieces, bits):
    for i, bit in enumerate(bits):
        same = own_bit(bit) == 0
        pieces = [jnp.where(same, p, pieces[k ^ (1 << i)]) for k, p in enumerate(pieces)]
    return pieces


def gather_rows(rows):
    for bit in reversed(seq_bits()):
        rows = jnp.concatenate([rows, swap(rows, bit)], axis=0)
    return rows


def relative():
    return masks_of(seq_bits()[::-1])


def segment_of(places, seq_lengths):
    count = seq_lengths.shape[0]
    before = jnp.arange(count)[None, :] <= jnp.arange(count)[:, None]
    boundary = jnp.sum(jnp.where(before, seq_lengths[None, :], 0), axis=1)
    return jnp.sum((places[:, None] >= boundary[None, :]).astype(jnp.int32), axis=1)


def from_sequence(mine):
    bits = seq_bits()
    return absolute([mine if m == 0 else swap(mine, m) for m in masks_of(bits)], bits)


def share_low(total, group, width):
    values = total.reshape((total.shape[0] // width, width) + total.shape[1:])
    own = lax.axis_index(BOTH)
    pieces = []
    for m in masks_of(group):
        place = ((own ^ m) // group[0]) % width
        piece = lax.dynamic_index_in_dim(values, place, 1, keepdims=False)
        pieces.append(piece if m == 0 else swap(piece, m))
    return sum(p.astype(jnp.float32) for p in pieces).astype(total.dtype)


BLOCKS = 16
PIECE = 48
TALL = 192
TN = (((0,), (0,)), ((), ()))


def cheap(rows):
    return pl.CostEstimate(flops=rows, bytes_accessed=rows, transcendentals=0)


def dot_nn(left, right):
    return lax.dot_general(left, right, NN, preferred_element_type=jnp.float32)


def dot_nt(left, right):
    return lax.dot_general(left, right, NT, preferred_element_type=jnp.float32)


def mat(chunk):
    return chunk.reshape(-1, WIDE)


def columns(c):
    return slice(c * WIDE, (c + 1) * WIDE)


def gelu_parts(u):
    root = math.sqrt(2.0 / math.pi)
    t = jnp.tanh(root * (u + 0.044715 * (u * u * u)))
    return 0.5 * (1.0 + t), 0.5 * u * (1.0 - t * t) * (root * (1.0 + (3 * 0.044715) * (u * u)))


def qkv_kernel(rows_ref, w_ref, kv_ref, q_ref):
    step = pl.program_id(0)
    weight = mat(w_ref[:, 0])

    @pl.when(step < 4)
    def _():
        kv_ref[...] = dot_nn(rows_ref[...], weight).astype(kv_ref.dtype)

    @pl.when(step >= 4)
    def _():
        q_ref[...] = dot_nn(rows_ref[: q_ref.shape[0]], weight).astype(q_ref.dtype)


def project(rows_all, own, weights, first):
    count = rows_all.shape[0]
    return pl.pallas_call(
        qkv_kernel,
        grid=(6,),
        in_specs=[
            pl.BlockSpec((count, D), lambda t: (0, 0)),
            pl.BlockSpec(
                (BLOCKS, 1, PIECE, WIDE),
                lambda t: (0, t % 2, jnp.where(t < 4, first + 1 + t // 2, first), 0),
            ),
        ],
        out_specs=[
            pl.BlockSpec((count, WIDE), lambda t: (0, jnp.minimum(t, 3))),
            pl.BlockSpec((own, WIDE), lambda t: (0, jnp.maximum(t - 4, 0))),
        ],
        out_shape=[
            jax.ShapeDtypeStruct((count, 2 * D), jnp.bfloat16),
            jax.ShapeDtypeStruct((own, D), jnp.bfloat16),
        ],
        compiler_params=pltpu.CompilerParams(vmem_limit_bytes=60 << 20),
        cost_estimate=cheap(own),
        name="project",
    )(rows_all, weights)


def mlp_kernel(h_ref, o_ref, gain_ref, next_ref, wo_ref, wu_ref, wd_ref, mid_ref, sec_ref, u_ref, act_ref, res_ref, nrm_ref):
    step = pl.program_id(0)

    @pl.when(step == 0)
    def _():
        for c in range(2):
            part = dot_nn(o_ref[...], mat(wo_ref[:, c]))
            mid_ref[:, columns(c)] = h_ref[:, columns(c)].astype(jnp.float32) + part
        middle = mid_ref[...]
        sec_ref[...] = norm_rows(middle, gain_ref[...]).astype(sec_ref.dtype)
        res_ref[...] = middle

    for p in range(2):
        u = dot_nn(sec_ref[...], mat(wu_ref[:, 0, p * PIECE : (p + 1) * PIECE]))
        u_ref[:, columns(p)] = u.astype(u_ref.dtype)
        act_ref[:, columns(p)] = (u * gelu_parts(u)[0]).astype(act_ref.dtype)
    for c in range(2):
        res_ref[:, columns(c)] += dot_nn(act_ref[...], mat(wd_ref[:, c]))

    @pl.when(step == 3)
    def _():
        nrm_ref[...] = norm_rows(res_ref[...], next_ref[...]).astype(nrm_ref.dtype)


def mlp_specs(out_piece):
    return [
        pl.BlockSpec((BLOCKS, 2, PIECE, WIDE), lambda t: (0, 0, out_piece, 0)),
        pl.BlockSpec((BLOCKS, 1, 2 * PIECE, WIDE), lambda t: (0, t // 2, 2 + t % 2, 0)),
        pl.BlockSpec((BLOCKS // 4, 2, TALL, WIDE), lambda t: (t, 0, 0, 0)),
    ]


def whole(shape):
    return pl.BlockSpec(shape, lambda t: (0,) * len(shape))


def feed_forward(hidden, attended, gain, next_gain, w_out, out_piece, w_mlp):
    rows = hidden.shape[0]
    full, tile = (rows, D), pl.BlockSpec((rows, D), lambda t: (0, t))
    return pl.pallas_call(
        mlp_kernel,
        grid=(4,),
        in_specs=[whole(full), whole(full), whole((1, D)), whole((1, D)), *mlp_specs(out_piece)],
        out_specs=[whole(full), whole(full), tile, tile, whole(full), whole(full)],
        out_shape=[
            jax.ShapeDtypeStruct(full, jnp.float32),
            jax.ShapeDtypeStruct(full, jnp.bfloat16),
            jax.ShapeDtypeStruct((rows, 4 * D), jnp.bfloat16),
            jax.ShapeDtypeStruct((rows, 4 * D), jnp.bfloat16),
            jax.ShapeDtypeStruct(full, jnp.float32),
            jax.ShapeDtypeStruct(full, jnp.bfloat16),
        ],
        compiler_params=pltpu.CompilerParams(vmem_limit_bytes=60 << 20),
        cost_estimate=cheap(rows),
        name="feed_forward",
    )(hidden, attended, gain[None], next_gain[None], w_out, w_mlp, w_mlp)


def norm_back(grad, values, gain):
    centre = values - jnp.mean(values, axis=-1, keepdims=True)
    scale = lax.rsqrt(jnp.mean(centre * centre, axis=-1, keepdims=True) + 1e-06)
    unit = centre * scale
    inner = grad * gain
    inner = inner - jnp.mean(inner, axis=-1, keepdims=True) - unit * jnp.mean(inner * unit, axis=-1, keepdims=True)
    return inner * scale, grad * unit


def mlp_back_kernel(g_ref, u_ref, mid_ref, gain_ref, wo_ref, wu_ref, wd_ref, gb_ref, gu_ref, gm_ref, ga_ref, gat_ref, gg_ref, acc):
    step = pl.program_id(0)

    @pl.when(step == 0)
    def _():
        gb_ref[...] = g_ref[...].astype(gb_ref.dtype)
        acc[...] = jnp.zeros(acc.shape, jnp.float32)

    low_grad = gb_ref[...]
    for p in range(2):
        part = slice(p * 2, p * 2 + 2)
        grad = sum(dot_nt(low_grad[:, columns(c)], mat(wd_ref[part, c])) for c in range(2))
        u = u_ref[:, columns(p)].astype(jnp.float32)
        gu = (grad * sum(gelu_parts(u))).astype(gu_ref.dtype)
        gu_ref[:, columns(p)] = gu
        acc[...] += dot_nt(gu, mat(wu_ref[:, 0, p * PIECE : (p + 1) * PIECE]))

    @pl.when(step == 3)
    def _():
        back, gain_rows = norm_back(acc[...], mid_ref[...], gain_ref[...])
        middle = back + g_ref[...]
        gm_ref[...] = middle
        gg_ref[...] = jnp.sum(gain_rows, axis=0, keepdims=True)
        low_middle = middle.astype(ga_ref.dtype)
        ga_ref[...] = low_middle
        gat_ref[...] = sum(dot_nt(low_middle[:, columns(c)], mat(wo_ref[:, c])) for c in range(2)).astype(gat_ref.dtype)


def feed_forward_back(grad, upward, middle, gain, w_out, out_piece, w_mlp):
    rows = grad.shape[0]
    full, tile = (rows, D), pl.BlockSpec((rows, D), lambda t: (0, t))
    return pl.pallas_call(
        mlp_back_kernel,
        grid=(4,),
        in_specs=[whole(full), tile, whole(full), whole((1, D)), *mlp_specs(out_piece)],
        out_specs=[whole(full), tile, whole(full), whole(full), whole(full), whole((1, D))],
        out_shape=[
            jax.ShapeDtypeStruct(full, jnp.bfloat16),
            jax.ShapeDtypeStruct((rows, 4 * D), jnp.bfloat16),
            jax.ShapeDtypeStruct(full, jnp.float32),
            jax.ShapeDtypeStruct(full, jnp.bfloat16),
            jax.ShapeDtypeStruct(full, jnp.bfloat16),
            jax.ShapeDtypeStruct((1, D), jnp.float32),
        ],
        scratch_shapes=[pltpu.VMEM(full, jnp.float32)],
        compiler_params=pltpu.CompilerParams(vmem_limit_bytes=60 << 20),
        cost_estimate=cheap(rows),
        name="feed_forward_back",
    )(grad, upward, middle, gain[None], w_out, w_mlp, w_mlp)


def rows_back_kernel(own, dk0, dk1, dv0, dv1, dq0, dq1, wq_ref, wk_ref, wv_ref, out_ref):
    total = sum(
        dot_nt(d[...], mat(w[:, c]))
        for d, w, c in ((dk0, wk_ref, 0), (dk1, wk_ref, 1), (dv0, wv_ref, 0), (dv1, wv_ref, 1))
    )
    out_ref[...] = total

    @pl.when(pl.program_id(0) < own)
    def _():
        out_ref[...] += sum(dot_nt(d[...], mat(wq_ref[:, c])) for d, c in ((dq0, 0), (dq1, 1)))


def rows_back(one, two, weights, first):
    count, own = one[1].shape[0], one[0].shape[0] // KB
    tile = pl.BlockSpec((KB, WIDE), lambda t: (t, 0))
    query = pl.BlockSpec((KB, WIDE), lambda t: (jnp.minimum(t, own - 1), 0))
    piece = lambda i: pl.BlockSpec((BLOCKS, 2, PIECE, WIDE), lambda t: (0, 0, first + i, 0))
    return pl.pallas_call(
        functools.partial(rows_back_kernel, own),
        grid=(count // KB,),
        in_specs=[tile, tile, tile, tile, query, query, piece(0), piece(1), piece(2)],
        out_specs=pl.BlockSpec((KB, D), lambda t: (t, 0)),
        out_shape=jax.ShapeDtypeStruct((count, D), jnp.float32),
        compiler_params=pltpu.CompilerParams(vmem_limit_bytes=60 << 20),
        cost_estimate=cheap(count),
        name="rows_back",
    )(one[1], two[1], one[2], two[2], one[0], two[0], weights, weights, weights)


def products_kernel(plan, *refs):
    *ins, out_ref, turned = refs
    held = None
    for left, column, count, right, at_column, block, half, at, tall in plan:
        if held != (left, column):
            turned[:, :count] = ins[left][:, column : column + D].T
            held = (left, column)
        part = dot_nn(turned[:, :count], ins[right][:, at_column : at_column + WIDE]).astype(out_ref.dtype)
        if tall:
            out_ref[block : block + 4, half, at : at + TALL] = part.reshape(4, TALL, WIDE)
        else:
            out_ref[:, half, at : at + PIECE] = part.reshape(BLOCKS, PIECE, WIDE)


def products(wanted):
    arrays, plan, at = [], [], 0

    def place(array):
        for i, known in enumerate(arrays):
            if known is array:
                return i
        arrays.append(array)
        return len(arrays) - 1

    for left, rights in wanted:
        pieces = [(place(r), i) for r in rights for i in range(0, r.shape[1], WIDE)]
        index, count = place(left), left.shape[0]
        if left.shape[1] == D:
            wide = len(pieces) // 2
            for n, (right, column) in enumerate(pieces):
                plan.append((index, 0, count, right, column, 0, n // wide, at + n % wide * PIECE, False))
            at += wide * PIECE
        else:
            for block in range(4):
                for half, (right, column) in enumerate(pieces):
                    plan.append((index, block * D, count, right, column, block * 4, half, at, True))
            at += TALL
    longest = max(left.shape[0] for left, _ in wanted)
    return pl.pallas_call(
        functools.partial(products_kernel, plan),
        out_shape=jax.ShapeDtypeStruct((BLOCKS, 2, at, WIDE), jnp.bfloat16),
        scratch_shapes=[pltpu.VMEM((D, longest), jnp.bfloat16)],
        compiler_params=pltpu.CompilerParams(vmem_limit_bytes=60 << 20),
        cost_estimate=cheap(longest),
        name="products",
    )(*arrays)


def to_blocks(gathered, sizes):
    places = gathered.shape[0] // 2
    chunks = gathered.reshape(places, 2, -1, WIDE)
    if places == BLOCKS:
        return chunks
    pieces, at = [], 0
    for size in sizes:
        rows = size * BLOCKS // places
        part = chunks[:, :, at : at + rows].reshape(BLOCKS, -1, 2, rows, WIDE)
        pieces.append(part.transpose(0, 2, 1, 3, 4).reshape(BLOCKS, 2, size, WIDE))
        at += rows
    return jnp.concatenate(pieces, axis=2)


def from_blocks(chunks, sizes):
    places = 1 << len(chip_bits())
    if places == BLOCKS:
        return chunks
    pieces, at = [], 0
    for size in sizes:
        rows = size * BLOCKS // places
        part = chunks[:, :, at : at + size].reshape(BLOCKS, 2, -1, rows, WIDE)
        pieces.append(part.transpose(0, 2, 1, 3, 4).reshape(places, 2, rows, WIDE))
        at += size
    return jnp.concatenate(pieces, axis=2)


def bundle(shards):
    chips, index = lax.axis_size("seq") // 2, lax.axis_index("seq")
    pieces = []
    for shard in shards:
        rows, half = shard.shape[0] // chips, shard.shape[1] // 2
        part = lax.dynamic_slice(shard, (index // 2 * rows, index % 2 * half), (rows, half))
        pieces += [part[:, i : i + WIDE] for i in range(0, half, WIDE)]
    return jnp.concatenate(pieces, axis=0)


def sizes_of(shards):
    tall = lambda s: s.shape[0] * lax.axis_size("dp") // BLOCKS
    return [tall(s) for s in shards for _ in range(0, s.shape[1] // 2, WIDE)]


def thirds_of(shard):
    return [shard[:, i : i + D] for i in range(0, 3 * D, D)]


def gather_weights(shards):
    return lax.all_gather(bundle(shards), BOTH, axis=0)


def gather_first(shards, after):
    values = bundle(shards)
    rows = values.shape[0]
    values = values[None]
    for step, group in enumerate(reversed(groups_of(chip_bits()))):
        pieces = [values if m == 0 else swap(values, m) for m in masks_of(group)]
        if step == 0:
            pieces, after = lax.optimization_barrier((pieces, after))
        values = jnp.stack(absolute(pieces, group), axis=1).reshape(-1, rows, WIDE)
    values = jnp.stack(absolute([values, swap(values, 1)], [1]), axis=1)
    return to_blocks(values.reshape(-1, rows, WIDE), sizes_of(shards)), after


def collect(mine, wanted):
    shares = from_sequence(mine)
    places = 1 << len(chip_bits())
    results, at = [], 0
    for height, width in wanted:
        rows, wide = height // places, width // (2 * WIDE)
        parts = [
            jnp.concatenate([s[at + i * rows : at + (i + 1) * rows] for s in shares[core::2]], axis=0)
            for core in range(2)
            for i in range(wide)
        ]
        results.append(jnp.concatenate(parts, axis=1).astype(jnp.float32))
        at += rows * wide
    return results


def scatter_sums(chunks):
    return lax.psum_scatter(chunks.reshape((-1,) + chunks.shape[2:]), BOTH, scatter_dimension=0)


def stepped_sums(chunks):
    core = own_bit(1)
    arrived = swap(lax.dynamic_index_in_dim(chunks, 1 - core, 1, keepdims=False), 1)
    kept = lax.dynamic_index_in_dim(chunks, core, 1, keepdims=False)
    total = (yield [low(kept.astype(jnp.float32) + arrived.astype(jnp.float32))])[0]
    for group in groups_of(chip_bits()):
        total = (yield [share_low(total, group, 1 << len(group))])[0]
    return total[0]


def everywhere(values):
    groups = groups_of([1] + chip_bits())
    parts = 2 << len(chip_bits())
    rows, wide = values.shape
    if rows < parts:
        for group in groups:
            values = sum(values if m == 0 else swap(values, m) for m in masks_of(group))
            values = (yield [values])[0]
        return values
    total = jnp.pad(values, ((0, -rows % (8 * parts)), (0, 0))).reshape(parts, -1, wide)
    for group in groups:
        total = share_low(total, group, 1 << len(group))
        total = (yield [total])[0]
    for group in reversed(groups):
        pieces = absolute([total if m == 0 else swap(total, m) for m in masks_of(group)], group)
        total = jnp.stack(pieces, axis=1).reshape((-1,) + total.shape[1:])
        total = (yield [total])[0]
    return total.reshape(-1, wide)[:rows]


class Running:
    def __init__(self, steps):
        self.steps, self.values, self.result = steps, None, None
        self.go(None)

    def go(self, values):
        try:
            self.values = self.steps.send(values)
        except StopIteration as end:
            self.values, self.result = [], end.value

    def finish(self):
        while self.result is None:
            self.go(self.values)
        return self.result


def tie(values, *running):
    values, held = lax.optimization_barrier((values, [r.values for r in running]))
    for r, h in zip(running, held):
        if r.result is None:
            r.go(h)
    return values


def attention_backward(grad_attended, kept, mask, between):
    idx, _, feature_k = mask
    keyval, attended, kept_q = kept
    pairs = HEADS // 2
    cut = pairs // 2
    one = attend_back(kept_q, keyval, idx, feature_k, grad_attended, attended, 0, cut)
    one, grad_attended = between((one, grad_attended))
    two = attend_back(kept_q, keyval, idx, feature_k, grad_attended, attended, cut, pairs - cut)
    return one, two


def summed_rows(grad_all):
    rows = grad_all
    for bit in seq_bits()[:-1]:
        half = rows.shape[0] // 2
        rows = rows[:half] + swap(low(rows[half:]), bit).astype(jnp.float32)
    half = rows.shape[0] // 2
    return rows[:half], swap(low(rows[half:]), seq_bits()[-1])


def local(
    tokens,
    lengths,
    classes,
    norm_gains,
    mask_gain,
    enc_qkv,
    enc_out,
    enc_up,
    enc_down,
    dec_qkv,
    dec_out,
    dec_up,
    dec_down,
    patch_proj,
    class_proj,
    mask_cot,
):
    w_first, (tokens, lengths) = gather_first(thirds_of(enc_qkv), (tokens, lengths))
    middle_shards = (enc_down, enc_up, enc_out, *thirds_of(dec_qkv), dec_out)
    last_shards = (dec_down, dec_up, patch_proj, class_proj)
    w_middle = to_blocks(gather_weights(middle_shards), sizes_of(middle_shards))
    gathered_last = gather_weights(last_shards)
    row_count = tokens.shape[1]
    index = lax.axis_index("seq")
    seq_lengths = lengths[0]
    inputs_f = tokens[0].astype(jnp.float32)
    gains_f = norm_gains.astype(jnp.float32)
    classes_f = classes.astype(jnp.float32)
    class_count = classes.shape[0]
    mask_gain_f = mask_gain.astype(jnp.float32)
    steps = jnp.arange(row_count, dtype=jnp.int32)
    seg_query = segment_of(index * row_count + steps, seq_lengths)
    starts = jnp.stack([(index ^ r) * row_count for r in relative()])
    seg_rows = segment_of((starts[:, None] + steps[None, :]).reshape(-1), seq_lengths)
    class_slots = jnp.arange(CLASS_ROWS, dtype=jnp.int32)
    seg_key = jnp.concatenate([seg_rows, jnp.where(class_slots < class_count, -1, IMGS + 1)])
    feature_q, feature_k = features(seg_query, seg_key)
    enc_mask = (active(seg_query, seg_rows), feature_q, feature_k[: seg_rows.shape[0]])
    dec_mask = (active(seg_query, seg_key), feature_q, feature_k)
    valid_rows = (seg_query < IMGS).astype(jnp.float32)[:, None]
    enc_normed = low(norm_rows(inputs_f, gains_f[0]))
    enc_rows = gather_rows(enc_normed)
    keyval, queries = project(enc_rows, row_count, w_first, 0)
    attended, attended_low, kept_q = attend(queries, keyval, *enc_mask)
    enc_attn = (keyval, attended, kept_q)
    enc_low = attended_low
    enc_middle, enc_second, enc_upward, enc_active, encoded, dec_normed = feed_forward(
        tokens[0], attended_low, gains_f[1], gains_f[2], w_middle, 8, w_middle
    )
    class_normed = low(norm_rows(classes_f, gains_f[2]))
    class_padded = jnp.pad(class_normed, ((0, CLASS_ROWS - class_count), (0, 0)))
    dec_rows = jnp.concatenate([gather_rows(dec_normed), class_padded], axis=0)
    keyval, queries = project(dec_rows, row_count, w_middle, 9)
    attended, dec_low, kept_q = attend(queries, keyval, *dec_mask)
    dec_attn = (keyval, attended, kept_q)
    gathered_last, dec_low = lax.optimization_barrier((gathered_last, dec_low))
    w_last = to_blocks(gathered_last, sizes_of(last_shards))
    dec_middle, dec_second, dec_upward, dec_active, decoded, final_normed = feed_forward(
        encoded, dec_low, gains_f[3], gains_f[4], w_middle, 12, w_last
    )
    w_patch, w_class = (
        jnp.concatenate([w_last[:, c, at : at + PIECE].reshape(D, WIDE) for c in range(2)], axis=1)
        for at in (2 * TALL, 2 * TALL + PIECE)
    )
    patch_rows = low(dot(final_normed, w_patch))
    class_rows = dot(classes, w_class)
    class_unit = low(unit_rows(class_rows))
    logits = dot_turned(patch_rows, class_unit)
    mask_out = class_norm(logits, mask_gain_f) * valid_rows
    _, head_back = jax.vjp(class_norm, logits, mask_gain_f)
    grad_logits, grad_mask_gain = head_back(mask_cot[0] * valid_rows)
    grad_logits_low = low(grad_logits)
    grad_patch_rows = low(dot(grad_logits_low, class_unit))
    grad_unit = dot_rows(grad_logits_low, patch_rows)
    grad_final = dot_turned(grad_patch_rows, w_patch)
    _, final_back = jax.vjp(norm_rows, decoded, gains_f[4])
    grad_decoded, grad_gain_last = final_back(grad_final)
    _, unit_back = jax.vjp(unit_rows, class_rows)
    grad_class_rows = low(unit_back(grad_unit)[0])
    grad_classes = dot_turned(grad_class_rows, w_class)
    grad_branch, grad_upward, grad_middle, grad_attn, grad_attended, grad_gain_three = feed_forward_back(
        grad_decoded, dec_upward, dec_middle, gains_f[3], w_middle, 12, w_last
    )
    pad_classes = ((0, CLASS_ROWS - class_count), (0, 0))
    dec_chunks = products(
        [
            (dec_active, [grad_branch]),
            (dec_second, [grad_upward]),
            (dec_low, [grad_attn]),
            (final_normed, [grad_patch_rows]),
            (jnp.pad(classes, pad_classes), [jnp.pad(grad_class_rows, pad_classes)]),
        ]
    )
    dec_chunks, grad_attended = lax.optimization_barrier((dec_chunks, grad_attended))
    dec_sum = scatter_sums(from_blocks(dec_chunks, [TALL] + 7 * [PIECE]))
    one, two = attention_backward(grad_attended, dec_attn, dec_mask, lambda v: v)
    grad_all = rows_back(one, two, w_middle, 9)
    token_rows = row_count * lax.axis_size("seq")
    here, coming = summed_rows(grad_all[:token_rows])
    dec_qkv_chunks = products(
        [(dec_normed, [one[0], two[0]]), (dec_rows, [one[1], two[1]]), (dec_rows, [one[2], two[2]])]
    )
    _, class_back = jax.vjp(norm_rows, classes_f, gains_f[2])
    grad_classes_kv, grad_gain_class = class_back(grad_all[token_rows : token_rows + class_count])
    back, gain_rows = norm_back(here + coming.astype(jnp.float32), encoded, gains_f[2])
    grad_encoded = back + grad_middle
    padded_mask_gain = jnp.pad(grad_mask_gain, (0, D - class_count))
    shared = jnp.concatenate(
        [
            grad_classes + grad_classes_kv,
            jnp.stack(
                [jnp.sum(gain_rows, axis=0) + grad_gain_class, grad_gain_three[0], grad_gain_last, padded_mask_gain]
            ),
        ],
        axis=0,
    )
    shared = Running(everywhere(shared))
    dec_proj = Running(stepped_sums(from_blocks(dec_qkv_chunks, 3 * [PIECE])))
    grad_encoded = tie(grad_encoded, dec_proj, shared)
    grad_branch, grad_upward, grad_middle, grad_attn, grad_attended, grad_gain_one = feed_forward_back(
        grad_encoded, enc_upward, enc_middle, gains_f[1], w_middle, 8, w_middle
    )
    enc_chunks = products(
        [(enc_active, [grad_branch]), (enc_second, [grad_upward]), (enc_low, [grad_attn])]
    )
    enc_chunks, grad_attended, dec_sum = lax.optimization_barrier((enc_chunks, grad_attended, dec_sum))
    enc_sum = scatter_sums(from_blocks(enc_chunks, [TALL] + 5 * [PIECE]))
    grad_attended = tie(grad_attended, dec_proj, shared)
    one, two = attention_backward(
        grad_attended, enc_attn, enc_mask, lambda v: tie(v, dec_proj, shared)
    )
    one, two = tie((one, two), dec_proj, shared)
    grad_all = rows_back(one, two, w_first, 0)
    here, coming = summed_rows(grad_all)
    grad_all, one, two = lax.optimization_barrier((grad_all, one, two))
    enc_qkv_chunks = products(
        [(enc_normed, [one[0], two[0]]), (enc_rows, [one[1], two[1]]), (enc_rows, [one[2], two[2]])]
    )
    enc_proj = Running(stepped_sums(from_blocks(enc_qkv_chunks, 3 * [PIECE])))
    here, coming = tie((here, coming), enc_proj, shared)
    back, gain_rows = norm_back(here + coming.astype(jnp.float32), inputs_f, gains_f[0])
    grad_inputs = back + grad_middle
    late = Running(everywhere(jnp.stack([jnp.sum(gain_rows, axis=0), grad_gain_one[0]])))
    square, wide, tall = (D, D), (D, 4 * D), (4 * D, D)
    thirds = [square] * 3
    out_enc_qkv = jnp.concatenate(collect(enc_proj.finish(), thirds), axis=1)
    late = late.finish()
    out_dec_qkv = jnp.concatenate(collect(dec_proj.finish(), thirds), axis=1)
    shared = shared.finish()
    out_dec = collect(dec_sum, [tall, wide, square, square, square])
    out_enc = collect(enc_sum, [tall, wide, square])
    gain_sums = jnp.concatenate([late, shared[class_count : class_count + 3]], axis=0)
    return (
        mask_out[None],
        grad_inputs[None],
        shared[:class_count],
        gain_sums,
        shared[class_count + 3, :class_count],
        out_enc_qkv,
        out_enc[2],
        out_enc[1],
        out_enc[0],
        out_dec_qkv,
        out_dec[2],
        out_dec[1],
        out_dec[0],
        out_dec[3],
        out_dec[4],
    )


def solution(mesh):
    placed = (
        P("dp", "seq", None),
        P("dp", None),
        P(),
        P(),
        P(),
        P("dp", None),
        P("dp", None),
        P("dp", None),
        P("dp", None),
        P("dp", None),
        P("dp", None),
        P("dp", None),
        P("dp", None),
        P("dp", None),
        P("dp", None),
        P("dp", "seq", None),
    )
    return jax.shard_map(
        local,
        mesh=mesh,
        in_specs=placed,
        out_specs=(
            P("dp", "seq", None),
            P("dp", "seq", None),
            P(),
            P(),
            P(),
            P("dp", None),
            P("dp", None),
            P("dp", None),
            P("dp", None),
            P("dp", None),
            P("dp", None),
            P("dp", None),
            P("dp", None),
            P("dp", None),
            P("dp", None),
        ),
        check_vma=False,
    )
```

time: 938 us -> 748 us (0.80)
  Pallas kernels: 181 us -> 356 us
  waiting for transfers between devices: 351 us -> 185 us
  matrix products: 158 us -> 7.28 us
  local copies, waits for them, and re-layouts: 101 us -> 40.9 us
    pallas_call x0 -> x12, Pallas kernels: none -> 185 us  [the longest x4 61.4 us: products(): pl.pallas_call(functools.partial(products_kernel, plan), out_shape=jax.Sh...]
    ppermute x75 -> x62, waiting for transfers between devices: 272 us -> 185 us  [swap(): return lax.ppermute(values, ('seq', 'dp'), pairs)]
    all_gather x2, waiting for transfers between devices: 79.4 us -> 0.01 us  [gather_weights(): return lax.all_gather(bundle(shards), BOTH, axis=0)]
    dot_general x25 -> x1, matrix products: 65.5 us -> 0.41 us  [dot_rows(): lax.dot_general(left, right, (((0,), (0,)), ((), ())), preferred_element_...]
    dot_general x13 -> x3, matrix products: 51.3 us -> 2.83 us  [dot(): return jnp.dot(left, right, preferred_element_type=jnp.float32)]
    dot_general x13 -> x3, matrix products: 41.7 us -> 4.04 us  [dot_turned(): lax.dot_general(left, right, (((1,), (1,)), ((), ())), preferred_element_...]
    unnamed x336 -> x105, local copies, waits for them, and re-layouts: 51.6 us -> 15.7 us
    slice x24 -> x35, local copies, waits for them, and re-layouts: 29.4 us -> 9.38 us  [the longest x2 4.22 us: summed_rows(): rows = rows[:half] + swap(low(rows[half:]), bit).astype(jnp.float32)]
  transfers between devices with their start and end apart: 77 -> 66, of which waited for: 41 -> 25; matrix products, arithmetic and copies ran while one was open for 25% -> 10% of each run, Pallas kernels for 15% -> 41%
where the time goes in v2:
time: 748 us; the launch traced here: 741 us
  Pallas kernels  356 us (48%)
  waiting for transfers between devices  185 us (25%)
  starting transfers between devices  81.1 us (11%)
  other arithmetic  54.6 us (7%)
  local copies, waits for them, and re-layouts  40.9 us (5%)
  between operations  15.9 us (2%)
    ppermute x62, waiting for transfers between devices, swap(): return lax.ppermute(values, ('seq', 'dp'), pairs)  185 us
    pallas_call x4, Pallas kernels, attend_back(): pl.pallas_call(bwd_kernel, grid_spec=spec, out_shape=[jax.ShapeDtypeStruc...  93.5 us
    ppermute x62, starting transfers between devices, swap(): return lax.ppermute(values, ('seq', 'dp'), pairs)  81 us
    pallas_call x2, Pallas kernels, attend(): pl.pallas_call(fwd_kernel, grid_spec=spec, out_shape=[jax.ShapeDtypeStruc...  78 us
    pallas_call x4, Pallas kernels, products(): pl.pallas_call(functools.partial(products_kernel, plan), out_shape=jax.Sh...  61.4 us
    pallas_call x2, Pallas kernels, feed_forward_back(): pl.pallas_call(mlp_back_kernel, grid=(4,), in_specs=[whole(full), tile, w...  35.6 us
    pallas_call x2, Pallas kernels, feed_forward(): pl.pallas_call(mlp_kernel, grid=(4,), in_specs=[whole(full), whole(full),...  31 us
    pallas_call x2, Pallas kernels, rows_back(): pl.pallas_call(functools.partial(rows_back_kernel, own), grid=(count // K...  29.8 us
  transfers between devices with their start and end apart: 66, of which 25 were waited for; matrix products, arithmetic and copies ran while one was open for 10% of the time, Pallas kernels for 41%

profile of v2, /device:TPU:0, one launch (start us, length us, event | category | flops | bytes accessed | tf_op | source)
XLA Modules:
  0.0 741.0 jit_solution(15503232195570700319)
XLA Ops:
  28.1 12.2 %collective-permute-done.1 = bf16[1,144,384]{2,1,0:T(8,128)(2,1)S(1)} collective-permute-done((bf16[1,144,384]{2,1,0:T(8,128)(2,1)S(1)}, bf16[1,144,384]{2,1,0:T(8,128)(2,1)S(1)}, u32[]{:S(2)}, u32[]{:S(2)}) %collective-permute-start.1) | collective-permute-done | bytes 110624 | tf_op jit(solution)/shard_map/ppermute | solution.py:225
  47.6 19.8 %collective-permute-done.5 = bf16[4,144,384]{2,1,0:T(8,128)(2,1)S(1)} collective-permute-done((bf16[4,144,384]{2,1,0:T(8,128)(2,1)S(1)}, bf16[4,144,384]{2,1,0:T(8,128)(2,1)S(1)}, u32[]{:S(2)}, u32[]{:S(2)}) %collective-permute-start.5) | collective-permute-done | bytes 442400 | tf_op jit(solution)/shard_map/ppermute | solution.py:225
  92.7 13.2 %project.2 = (bf16[2048,1536]{1,0:T(8,128)(2,1)}, bf16[512,768]{1,0:T(8,128)(2,1)}) custom-call(bf16[2048,768]{1,0:T(8,128)(2,1)} %pad_maximum_fusion.1.rows_ref.refs_5_, bf16[16,2,144,384]{3,2,1,0:T(8,128)(2,1)} %pad_maximum_fusion.w_ref.wq_ref.wk_ref.wv_ref), custom_call_target="tpu_custom_call" | custom-call | flops 512 | bytes 512 | tf_op jit(solution)/shard_map/project/pallas_call | solution.py:330
  105.9 36.8 %attend.2 = (f32[512,768]{1,0:T(8,128)}, bf16[512,768]{1,0:T(8,128)(2,1)}, bf16[12,512,128]{2,1,0:T(8,128)(2,1)}) custom-call(s32[9]{0:T(128)} %pad_add_fusion.2.idx_ref, bf16[512,768]{1,0:T(8,128)(2,1)} %get-tuple-element.109.q_ref, bf16[2048,1536]{1,0:T(8,128)(2,1)} %get-tuple-element.110.k_ref.v_ref, bf16[2048,1536]{1,0:T(8,128)(2,1)} %get-tuple-element.110.k_ref.v_ref, ...), custom_call_target="tpu_custom_call" | custom-call | flops 1048576 | bytes 393216 | tf_op jit(solution)/shard_map/attend/pallas_call | solution.py:83
  142.7 15.4 %feed_forward.2 = (f32[512,768]{1,0:T(8,128)}, bf16[512,768]{1,0:T(8,128)(2,1)}, bf16[512,3072]{1,0:T(8,128)(2,1)}, bf16[512,3072]{1,0:T(8,128)(2,1)}, f32[512,768]{1,0:T(8,128)}, /*index=5*/bf16[512,768]{1,0:T(8,128)(2,1)}) custom-call(bf16[512,768]{1,0:T(8,128)(2,1)} %bitcast.213, bf16[512,768]{1,0:T(8,128)(2,1)} %get-tuple-element.111.o_ref.refs_5_, ...), custom_call_target="tpu_custom_call" | custom-call | flops 512 | bytes 512 | tf_op jit(solution)/shard_map/feed_forward/pallas_call | solution.py:393
  160.6 19.3 %collective-permute-done.9 = bf16[512,768]{1,0:T(8,128)(2,1)S(1)} collective-permute-done((bf16[512,768]{1,0:T(8,128)(2,1)}, bf16[512,768]{1,0:T(8,128)(2,1)S(1)}, u32[]{:S(2)}, u32[]{:S(2)}) %collective-permute-start.9) | collective-permute-done | bytes 786464 | tf_op jit(solution)/shard_map/ppermute | solution.py:225
  194.5 13.7 %project.3 = (bf16[2304,1536]{1,0:T(8,128)(2,1)}, bf16[512,768]{1,0:T(8,128)(2,1)}) custom-call(bf16[2304,768]{1,0:T(8,128)(2,1)} %fusion.1.rows_ref.refs_5_, bf16[16,2,624,384]{3,2,1,0:T(8,128)(2,1)} %bitcast.197), custom_call_target="tpu_custom_call" | custom-call | flops 512 | bytes 512 | tf_op jit(solution)/shard_map/project/pallas_call | solution.py:330
  208.2 41.2 %attend.3 = (f32[512,768]{1,0:T(8,128)}, bf16[512,768]{1,0:T(8,128)(2,1)}, bf16[12,512,128]{2,1,0:T(8,128)(2,1)}) custom-call(s32[10]{0:T(128)} %pad_add_fusion.3.idx_ref, bf16[512,768]{1,0:T(8,128)(2,1)} %get-tuple-element.114.q_ref, bf16[2304,1536]{1,0:T(8,128)(2,1)} %get-tuple-element.115.k_ref.v_ref, bf16[2304,1536]{1,0:T(8,128)(2,1)} %get-tuple-element.115.k_ref.v_ref, ...), custom_call_target="tpu_custom_call" | custom-call | flops 1179648 | bytes 393216 | tf_op jit(solution)/shard_map/attend/pallas_call | solution.py:83
  251.7 15.6 %feed_forward.3 = (f32[512,768]{1,0:T(8,128)}, bf16[512,768]{1,0:T(8,128)(2,1)}, bf16[512,3072]{1,0:T(8,128)(2,1)}, bf16[512,3072]{1,0:T(8,128)(2,1)}, f32[512,768]{1,0:T(8,128)}, /*index=5*/bf16[512,768]{1,0:T(8,128)(2,1)}) custom-call(f32[512,768]{1,0:T(8,128)} %get-tuple-element.112.h_ref, bf16[512,768]{1,0:T(8,128)(2,1)} %get-tuple-element.117.o_ref.refs_5_, ...), custom_call_target="tpu_custom_call" | custom-call | flops 512 | bytes 512 | tf_op jit(solution)/shard_map/feed_forward/pallas_call | solution.py:393
  278.2 17.8 %feed_forward_back.2 = (bf16[512,768]{1,0:T(8,128)(2,1)}, bf16[512,3072]{1,0:T(8,128)(2,1)}, f32[512,768]{1,0:T(8,128)}, bf16[512,768]{1,0:T(8,128)(2,1)}, bf16[512,768]{1,0:T(8,128)(2,1)}, /*index=5*/f32[1,768]{1,0:T(1,128)}) custom-call(f32[512,768]{1,0:T(8,128)} %broadcast_add_fusion.g_ref, bf16[512,3072]{1,0:T(8,128)(2,1)} %get-tuple-element.123.u_ref, ...), custom_call_target="tpu_custom_call" | custom-call | flops 512 | bytes 512 | tf_op jit(solution)/shard_map/feed_forward_back/pallas_call | solution.py:452
  296.0 17.9 %products.4 = bf16[16,2,528,384]{3,2,1,0:T(8,128)(2,1)} custom-call(bf16[512,768]{1,0:T(8,128)(2,1)} %get-tuple-element.125.refs_0_, bf16[512,3072]{1,0:T(8,128)(2,1)} %get-tuple-element.126.refs_1_, bf16[512,3072]{1,0:T(8,128)(2,1)} %get-tuple-element.127.refs_2_, bf16[512,768]{1,0:T(8,128)(2,1)} %get-tuple-element.128.refs_3_, ...), custom_call_target="tpu_custom_call" | custom-call | flops 512 | bytes 512 | tf_op jit(solution)/shard_map/products/pallas_call | solution.py:539
  313.9 24.9 %attend_back.5 = (bf16[512,384]{1,0:T(8,128)(2,1)}, bf16[2304,384]{1,0:T(8,128)(2,1)}, bf16[2304,384]{1,0:T(8,128)(2,1)}) custom-call(s32[10]{0:T(128)} %pad_add_fusion.3.idx_ref, bf16[12,512,128]{2,1,0:T(8,128)(2,1)} %get-tuple-element.121.qa_ref, bf16[2304,1536]{1,0:T(8,128)(2,1)} %get-tuple-element.115.k_ref.v_ref, ...), custom_call_target="tpu_custom_call" | custom-call | flops 1179648 | bytes 393216 | tf_op jit(solution)/shard_map/attend_back/pallas_call | solution.py:145
  338.9 24.5 %attend_back.4 = (bf16[512,384]{1,0:T(8,128)(2,1)}, bf16[2304,384]{1,0:T(8,128)(2,1)}, bf16[2304,384]{1,0:T(8,128)(2,1)}) custom-call(s32[10]{0:T(128)} %pad_add_fusion.3.idx_ref, bf16[12,512,128]{2,1,0:T(8,128)(2,1)} %get-tuple-element.121.qa_ref, bf16[2304,1536]{1,0:T(8,128)(2,1)} %get-tuple-element.115.k_ref.v_ref, ...), custom_call_target="tpu_custom_call" | custom-call | flops 1179648 | bytes 393216 | tf_op jit(solution)/shard_map/attend_back/pallas_call | solution.py:145
  363.4 15.4 %rows_back.2 = f32[2304,768]{1,0:T(8,128)} custom-call(bf16[2304,384]{1,0:T(8,128)(2,1)} %get-tuple-element.133.dk0.refs_3_, bf16[2304,384]{1,0:T(8,128)(2,1)} %get-tuple-element.134.dk1.refs_4_, bf16[2304,384]{1,0:T(8,128)(2,1)} %get-tuple-element.135.dv0.refs_6_, bf16[2304,384]{1,0:T(8,128)(2,1)} %get-tuple-element.136.dv1.refs_7_, ...), custom_call_target="tpu_custom_call" | custom-call | flops 2304 | bytes 2304 | tf_op jit(solution)/shard_map/rows_back/pallas_call | solution.py:489
  381.7 14.6 %products.5 = bf16[16,2,144,384]{3,2,1,0:T(8,128)(2,1)} custom-call(bf16[512,384]{1,0:T(8,128)(2,1)} %get-tuple-element.137.dq0.refs_0_, bf16[512,384]{1,0:T(8,128)(2,1)} %get-tuple-element.138.dq1.refs_1_, bf16[512,768]{1,0:T(8,128)(2,1)} %get-tuple-element.113.refs_2_, bf16[2304,384]{1,0:T(8,128)(2,1)} %get-tuple-element.133.dk0.refs_3_, ...), custom_call_target="tpu_custom_call" | custom-call | flops 2304 | bytes 2304 | tf_op jit(solution)/shard_map/products/pallas_call | solution.py:539
  416.7 21.9 %collective-permute-done.12 = bf16[512,768]{1,0:T(8,128)(2,1)S(1)} collective-permute-done((bf16[512,768]{1,0:T(8,128)(2,1)S(1)}, bf16[512,768]{1,0:T(8,128)(2,1)S(1)}, u32[]{:S(2)}, u32[]{:S(2)}) %collective-permute-start.12) | collective-permute-done | bytes 786464 | tf_op jit(solution)/shard_map/ppermute | solution.py:225
  461.4 17.8 %feed_forward_back.3 = (bf16[512,768]{1,0:T(8,128)(2,1)}, bf16[512,3072]{1,0:T(8,128)(2,1)}, f32[512,768]{1,0:T(8,128)}, bf16[512,768]{1,0:T(8,128)(2,1)}, bf16[512,768]{1,0:T(8,128)(2,1)}, /*index=5*/f32[1,768]{1,0:T(1,128)}) custom-call(f32[512,768]{1,0:T(8,128)} %multiply_add_fusion.g_ref, bf16[512,3072]{1,0:T(8,128)(2,1)} %get-tuple-element.142.u_ref, ...), custom_call_target="tpu_custom_call" | custom-call | flops 512 | bytes 512 | tf_op jit(solution)/shard_map/feed_forward_back/pallas_call | solution.py:452
  479.2 15.4 %products.6 = bf16[16,2,432,384]{3,2,1,0:T(8,128)(2,1)} custom-call(bf16[512,768]{1,0:T(8,128)(2,1)} %get-tuple-element.144.refs_0_, bf16[512,3072]{1,0:T(8,128)(2,1)} %get-tuple-element.145.refs_1_, bf16[512,3072]{1,0:T(8,128)(2,1)} %get-tuple-element.146.refs_2_, bf16[512,768]{1,0:T(8,128)(2,1)} %get-tuple-element.147.refs_3_, ...), custom_call_target="tpu_custom_call" | custom-call | flops 512 | bytes 512 | tf_op jit(solution)/shard_map/products/pallas_call | solution.py:539
  502.8 16.2 %collective-permute-done.20 = f32[2,8,768]{2,1,0:T(8,128)S(1)} collective-permute-done((f32[2,8,768]{2,1,0:T(8,128)S(1)}, f32[2,8,768]{2,1,0:T(8,128)S(1)}, u32[]{:S(2)}, u32[]{:S(2)}) %collective-permute-start.20) | collective-permute-done | bytes 49184 | tf_op jit(solution)/shard_map/ppermute | solution.py:225
  531.8 22.1 %attend_back.6 = (bf16[512,384]{1,0:T(8,128)(2,1)}, bf16[2048,384]{1,0:T(8,128)(2,1)}, bf16[2048,384]{1,0:T(8,128)(2,1)}) custom-call(s32[9]{0:T(128)} %pad_add_fusion.2.idx_ref, bf16[12,512,128]{2,1,0:T(8,128)(2,1)} %get-tuple-element.120.qa_ref, bf16[2048,1536]{1,0:T(8,128)(2,1)} %get-tuple-element.110.k_ref.v_ref, ...), custom_call_target="tpu_custom_call" | custom-call | flops 1048576 | bytes 393216 | tf_op jit(solution)/shard_map/attend_back/pallas_call | solution.py:145
  557.4 21.9 %attend_back.7 = (bf16[512,384]{1,0:T(8,128)(2,1)}, bf16[2048,384]{1,0:T(8,128)(2,1)}, bf16[2048,384]{1,0:T(8,128)(2,1)}) custom-call(s32[9]{0:T(128)} %pad_add_fusion.2.idx_ref, bf16[12,512,128]{2,1,0:T(8,128)(2,1)} %get-tuple-element.120.qa_ref, bf16[2048,1536]{1,0:T(8,128)(2,1)} %get-tuple-element.110.k_ref.v_ref, ...), custom_call_target="tpu_custom_call" | custom-call | flops 1048576 | bytes 393216 | tf_op jit(solution)/shard_map/attend_back/pallas_call | solution.py:145
  582.9 14.4 %rows_back.3 = f32[2048,768]{1,0:T(8,128)} custom-call(bf16[2048,384]{1,0:T(8,128)(2,1)} %get-tuple-element.177.dk0.refs_3_, bf16[2048,384]{1,0:T(8,128)(2,1)} %get-tuple-element.178.dk1.refs_4_, bf16[2048,384]{1,0:T(8,128)(2,1)} %get-tuple-element.179.dv0.refs_6_, bf16[2048,384]{1,0:T(8,128)(2,1)} %get-tuple-element.180.dv1.refs_7_, ...), custom_call_target="tpu_custom_call" | custom-call | flops 2048 | bytes 2048 | tf_op jit(solution)/shard_map/rows_back/pallas_call | solution.py:489
  597.3 13.4 %products.7 = bf16[16,2,144,384]{3,2,1,0:T(8,128)(2,1)} custom-call(bf16[512,384]{1,0:T(8,128)(2,1)} %get-tuple-element.175.dq0.refs_0_, bf16[512,384]{1,0:T(8,128)(2,1)} %get-tuple-element.176.dq1.refs_1_, bf16[512,768]{1,0:T(8,128)(2,1)} %copy-done.8, bf16[2048,384]{1,0:T(8,128)(2,1)} %get-tuple-element.177.dk0.refs_3_, ...), custom_call_target="tpu_custom_call" | custom-call | flops 2048 | bytes 2048 | tf_op jit(solution)/shard_map/products/pallas_call | solution.py:539
  643.9 13.6 %collective-permute-done.29 = bf16[512,768]{1,0:T(8,128)(2,1)S(1)} collective-permute-done((bf16[512,768]{1,0:T(8,128)(2,1)S(1)}, bf16[512,768]{1,0:T(8,128)(2,1)S(1)}, u32[]{:S(2)}, u32[]{:S(2)}) %collective-permute-start.29) | collective-permute-done | bytes 786464 | tf_op jit(solution)/shard_map/ppermute | solution.py:225
  (456 shorter events, 266.0 us)
Async XLA Ops:
  7.2 135.5 %all-gather.5.cloned.1.call-start = ((), (), s32[]{:S(2)}) async-start(), calls=%async_computation.4 | async-start | bytes 15814656 | tf_op jit(solution)/shard_map/all_gather | solution.py:596
  14.9 234.5 %all-gather.7.cloned.1.call-start = ((), (), s32[]{:S(2)}) async-start(), calls=%async_computation.5 | async-start | bytes 12165120 | tf_op jit(solution)/shard_map/all_gather | solution.py:596
  21.4 473.2 %reduce-scatter.3.cloned.1.call-start = ((), (), s32[]{:S(2)}) async-start(), calls=%async_computation.2 | async-start | bytes 13381632 | tf_op jit(solution)/shard_map/reduce_scatter | solution.py:629
  40.5 26.9 %collective-permute-start.5 = (bf16[4,144,384]{2,1,0:T(8,128)(2,1)S(1)}, bf16[4,144,384]{2,1,0:T(8,128)(2,1)S(1)}, u32[]{:S(2)}, u32[]{:S(2)}) collective-permute-start(bf16[4,144,384]{2,1,0:T(8,128)(2,1)S(1)} %maximum_bitcast_fusion), channel_id=1, source_target_pairs={{0,16},{8,24},{16,0},{24,8},{1,17},{9,25},{17,1},{25,9},{2,18},{10... | collective-permute-start | bytes 1327112 | tf_op jit(solution)/shard_map/ppermute | solution.py:225
  42.2 25.2 %collective-permute-start.6 = (bf16[4,144,384]{2,1,0:T(8,128)(2,1)S(1)}, bf16[4,144,384]{2,1,0:T(8,128)(2,1)S(1)}, u32[]{:S(2)}, u32[]{:S(2)}) collective-permute-start(bf16[4,144,384]{2,1,0:T(8,128)(2,1)S(1)} %maximum_bitcast_fusion), channel_id=1, source_target_pairs={{0,1},{8,9},{16,17},{24,25},{1,0},{9,8},{17,16},{25,24},{2,3},{10,... | collective-permute-start | bytes 1327112 | tf_op jit(solution)/shard_map/ppermute | solution.py:225
  43.7 23.7 %collective-permute-start.7 = (bf16[4,144,384]{2,1,0:T(8,128)(2,1)S(1)}, bf16[4,144,384]{2,1,0:T(8,128)(2,1)S(1)}, u32[]{:S(2)}, u32[]{:S(2)}) collective-permute-start(bf16[4,144,384]{2,1,0:T(8,128)(2,1)S(1)} %maximum_bitcast_fusion), channel_id=1, source_target_pairs={{0,17},{8,25},{16,1},{24,9},{1,16},{9,24},{17,0},{25,8},{2,19},{10... | collective-permute-start | bytes 1327112 | tf_op jit(solution)/shard_map/ppermute | solution.py:225
  45.0 36.2 %collective-permute-start.3 = (bf16[512,768]{1,0:T(8,128)(2,1)S(1)}, bf16[512,768]{1,0:T(8,128)(2,1)S(1)}, u32[]{:S(2)}, u32[]{:S(2)}) collective-permute-start(bf16[512,768]{1,0:T(8,128)(2,1)S(1)} %fusion.10.refs_2_), channel_id=1, source_target_pairs={{0,16},{8,24},{16,0},{24,8},{1,17},{9,25},{17,1},{25,9},{2,18},{10... | collective-permute-start | bytes 2359304 | tf_op jit(solution)/shard_map/ppermute | solution.py:225
  158.1 21.7 %collective-permute-start.9 = (bf16[512,768]{1,0:T(8,128)(2,1)}, bf16[512,768]{1,0:T(8,128)(2,1)S(1)}, u32[]{:S(2)}, u32[]{:S(2)}) collective-permute-start(bf16[512,768]{1,0:T(8,128)(2,1)} %get-tuple-element.113.refs_2_), channel_id=1, source_target_pairs={{0,16},{8,24},{16,0},{24,8},{1,17},{9,25},{17,1},{25,9},{2,18},{10... | collective-permute-start | bytes 2359304 | tf_op jit(solution)/shard_map/ppermute | solution.py:225
  313.9 399.9 %reduce-scatter.5.cloned.1.call-start = ((), (), s32[]{:S(2)}) async-start(), calls=%async_computation.3 | async-start | bytes 10948608 | tf_op jit(solution)/shard_map/reduce_scatter | solution.py:629
  404.1 34.5 %collective-permute-start.12 = (bf16[512,768]{1,0:T(8,128)(2,1)S(1)}, bf16[512,768]{1,0:T(8,128)(2,1)S(1)}, u32[]{:S(2)}, u32[]{:S(2)}) collective-permute-start(bf16[512,768]{1,0:T(8,128)(2,1)S(1)} %slice.615), channel_id=1, source_target_pairs={{0,16},{8,24},{16,0},{24,8},{1,17},{9,25},{17,1},{25,9},{2,18},{10... | collective-permute-start | bytes 2359304 | tf_op jit(solution)/shard_map/ppermute | solution.py:225
  496.0 28.0 %collective-permute-start.17 = (bf16[4,144,384]{2,1,0:T(8,128)(2,1)}, bf16[4,144,384]{2,1,0:T(8,128)(2,1)S(1)}, u32[]{:S(2)}, u32[]{:S(2)}) collective-permute-start(bf16[4,144,384]{2,1,0:T(8,128)(2,1)} %get-tuple-element.251), channel_id=1, source_target_pairs={{0,16},{8,24},{16,0},{24,8},{1,17},{9,25},{17,1},{25,9},{2,18},{10... | collective-permute-start | bytes 1327112 | tf_op jit(solution)/shard_map/ppermute | solution.py:225
  496.3 27.7 %collective-permute-start.18 = (bf16[4,144,384]{2,1,0:T(8,128)(2,1)}, bf16[4,144,384]{2,1,0:T(8,128)(2,1)S(1)}, u32[]{:S(2)}, u32[]{:S(2)}) collective-permute-start(bf16[4,144,384]{2,1,0:T(8,128)(2,1)} %get-tuple-element.253), channel_id=1, source_target_pairs={{0,1},{8,9},{16,17},{24,25},{1,0},{9,8},{17,16},{25,24},{2,3},{10,... | collective-permute-start | bytes 1327112 | tf_op jit(solution)/shard_map/ppermute | solution.py:225
  496.3 27.7 %collective-permute-start.19 = (bf16[4,144,384]{2,1,0:T(8,128)(2,1)}, bf16[4,144,384]{2,1,0:T(8,128)(2,1)S(1)}, u32[]{:S(2)}, u32[]{:S(2)}) collective-permute-start(bf16[4,144,384]{2,1,0:T(8,128)(2,1)} %get-tuple-element.252), channel_id=1, source_target_pairs={{0,17},{8,25},{16,1},{24,9},{1,16},{9,24},{17,0},{25,8},{2,19},{10... | collective-permute-start | bytes 1327112 | tf_op jit(solution)/shard_map/ppermute | solution.py:225
  499.6 22.3 %collective-permute-start.21 = (f32[2,8,768]{2,1,0:T(8,128)S(1)}, f32[2,8,768]{2,1,0:T(8,128)S(1)}, u32[]{:S(2)}, u32[]{:S(2)}) collective-permute-start(f32[2,8,768]{2,1,0:T(8,128)S(1)} %get-tuple-element.351), channel_id=1, source_target_pairs={{0,2},{8,10},{16,18},{24,26},{1,3},{9,11},{17,19},{25,27},{2,0},{1... | collective-permute-start | bytes 147464 | tf_op jit(solution)/shard_map/ppermute | solution.py:225
  524.3 29.7 %collective-permute-start.26 = (f32[1,8,768]{2,1,0:T(8,128)S(1)}, f32[1,8,768]{2,1,0:T(8,128)S(1)}, u32[]{:S(2)}, u32[]{:S(2)}) collective-permute-start(f32[1,8,768]{2,1,0:T(8,128)S(1)} %constant_dynamic-slice_fusion.3), channel_id=1, source_target_pairs={{0,4},{8,12},{16,20},{24,28},{1,5},{9,13},{17,21},{25,29},{2,6},{1... | collective-permute-start | bytes 73736 | tf_op jit(solution)/shard_map/ppermute | solution.py:225
  527.4 26.6 %collective-permute-start.23 = (bf16[1,144,384]{2,1,0:T(8,128)(2,1)S(1)}, bf16[1,144,384]{2,1,0:T(8,128)(2,1)S(1)}, u32[]{:S(2)}, u32[]{:S(2)}) collective-permute-start(bf16[1,144,384]{2,1,0:T(8,128)(2,1)S(1)} %get-tuple-element.283), channel_id=1, source_target_pairs={{0,2},{8,10},{16,18},{24,26},{1,3},{9,11},{17,19},{25,27},{2,0},{1... | collective-permute-start | bytes 331784 | tf_op jit(solution)/shard_map/ppermute | solution.py:225
  528.7 25.2 %collective-permute-start.24 = (bf16[1,144,384]{2,1,0:T(8,128)(2,1)S(1)}, bf16[1,144,384]{2,1,0:T(8,128)(2,1)S(1)}, u32[]{:S(2)}, u32[]{:S(2)}) collective-permute-start(bf16[1,144,384]{2,1,0:T(8,128)(2,1)S(1)} %get-tuple-element.285), channel_id=1, source_target_pairs={{0,4},{8,12},{16,20},{24,28},{1,5},{9,13},{17,21},{25,29},{2,6},{1... | collective-permute-start | bytes 331784 | tf_op jit(solution)/shard_map/ppermute | solution.py:225
  529.6 24.4 %collective-permute-start.25 = (bf16[1,144,384]{2,1,0:T(8,128)(2,1)S(1)}, bf16[1,144,384]{2,1,0:T(8,128)(2,1)S(1)}, u32[]{:S(2)}, u32[]{:S(2)}) collective-permute-start(bf16[1,144,384]{2,1,0:T(8,128)(2,1)S(1)} %get-tuple-element.284), channel_id=1, source_target_pairs={{0,6},{8,14},{16,22},{24,30},{1,7},{9,15},{17,23},{25,31},{2,4},{1... | collective-permute-start | bytes 331784 | tf_op jit(solution)/shard_map/ppermute | solution.py:225
  554.1 25.2 %collective-permute-start.27 = (f32[1,8,768]{2,1,0:T(8,128)S(1)}, f32[1,8,768]{2,1,0:T(8,128)S(1)}, u32[]{:S(2)}, u32[]{:S(2)}) collective-permute-start(f32[1,8,768]{2,1,0:T(8,128)S(1)} %dynamic-slice_add_fusion), channel_id=1, source_target_pairs={{0,4},{8,12},{16,20},{24,28},{1,5},{9,13},{17,21},{25,29},{2,6},{1... | collective-permute-start | bytes 73736 | tf_op jit(solution)/shard_map/ppermute | solution.py:225
  557.4 68.8 %collective-permute-start.59 = (bf16[528,384]{1,0:T(8,128)(2,1)S(1)}, bf16[528,384]{1,0:T(8,128)(2,1)S(1)}, u32[]{:S(2)}, u32[]{:S(2)}) collective-permute-start(bf16[528,384]{1,0:T(8,128)(2,1)S(1)} %bitcast.242), channel_id=1, source_target_pairs={{0,8},{8,0},{16,24},{24,16},{1,9},{9,1},{17,25},{25,17},{2,10},{10... | collective-permute-start | bytes 1216520 | tf_op jit(solution)/shard_map/ppermute | solution.py:225
  557.4 68.8 %collective-permute-start.60 = (bf16[528,384]{1,0:T(8,128)(2,1)S(1)}, bf16[528,384]{1,0:T(8,128)(2,1)S(1)}, u32[]{:S(2)}, u32[]{:S(2)}) collective-permute-start(bf16[528,384]{1,0:T(8,128)(2,1)S(1)} %bitcast.243), channel_id=1, source_target_pairs={{0,16},{8,24},{16,0},{24,8},{1,17},{9,25},{17,1},{25,9},{2,18},{10... | collective-permute-start | bytes 1216520 | tf_op jit(solution)/shard_map/ppermute | solution.py:225
  579.3 35.1 %collective-permute-start.31 = (f32[2,8,768]{2,1,0:T(8,128)S(1)}, f32[2,8,768]{2,1,0:T(8,128)S(1)}, u32[]{:S(2)}, u32[]{:S(2)}) collective-permute-start(f32[2,8,768]{2,1,0:T(8,128)S(1)} %maximum_bitcast_fusion.2), channel_id=1, source_target_pairs={{0,1},{8,9},{16,17},{24,25},{1,0},{9,8},{17,16},{25,24},{2,3},{10,... | collective-permute-start | bytes 147464 | tf_op jit(solution)/shard_map/ppermute | solution.py:225
  579.4 35.1 %collective-permute-start.32 = (f32[2,8,768]{2,1,0:T(8,128)S(1)}, f32[2,8,768]{2,1,0:T(8,128)S(1)}, u32[]{:S(2)}, u32[]{:S(2)}) collective-permute-start(f32[2,8,768]{2,1,0:T(8,128)S(1)} %maximum_bitcast_fusion.2), channel_id=1, source_target_pairs={{0,2},{8,10},{16,18},{24,26},{1,3},{9,11},{17,19},{25,27},{2,0},{1... | collective-permute-start | bytes 147464 | tf_op jit(solution)/shard_map/ppermute | solution.py:225
  582.7 36.2 %collective-permute-start.33 = (f32[2,8,768]{2,1,0:T(8,128)S(1)}, f32[2,8,768]{2,1,0:T(8,128)S(1)}, u32[]{:S(2)}, u32[]{:S(2)}) collective-permute-start(f32[2,8,768]{2,1,0:T(8,128)S(1)} %maximum_bitcast_fusion.2), channel_id=1, source_target_pairs={{0,3},{8,11},{16,19},{24,27},{1,2},{9,10},{17,18},{25,26},{2,1},{1... | collective-permute-start | bytes 147464 | tf_op jit(solution)/shard_map/ppermute | solution.py:225
  (86 other events, 999.6 us)
Sparse Core Ops, SparseCore 0:
  15.0 125.2 all-gather.4
  143.8 92.2 all-gather.6
  314.0 177.5 reduce-scatter.2
  497.6 146.0 reduce-scatter.4

commit v3 on v2

--- a/solution.py
+++ b/solution.py
@@ -19,151 +19,125 @@
     mid=(v-hi).astype(jnp.bfloat16).astype(jnp.float32)
     return hi,mid,v-hi-mid
 
-def fwd_kernel(idx_ref,q_ref,k_ref,v_ref,fq_ref,fk_ref,o_ref,ol_ref,qa_ref,ka,va,s_ref,m_ref,acc_ref):
-    rows=q_ref.shape[0]
-    cnt=idx_ref[0]
-    lane=lax.broadcasted_iota(jnp.int32,(1,128),1)
-    low=lane<HD
-    q2=q_ref[...]*jnp.bfloat16(0.125)
-    fq=fq_ref[...]
-    qs=(jnp.where(low,q2,fq),jnp.where(low,fq,q2))
-    k2=k_ref[...];v2=v_ref[...];fk=fk_ref[...]
-    ka[0]=jnp.where(low,k2,fk);ka[1]=jnp.where(low,fk,k2)
-    va[0]=jnp.where(low,v2,fk);va[1]=jnp.where(low,fk,v2)
-    m_ref[...]=jnp.full(m_ref.shape,2*NEG,jnp.float32)
-    def first(i,_):
-        r=pl.ds(pl.multiple_of(idx_ref[i+1]*KB,KB),KB)
+def fwd_kernel(q_ref, k_ref, v_ref, fq_ref, fk_ref, o_ref, ol_ref, qa_ref):
+    lane = lax.broadcasted_iota(jnp.int32, (1, 128), 1)
+    low = lane < HD
+    fk, k2, v2 = fk_ref[...], k_ref[...], v_ref[...]
+    keys = (jnp.where(low, k2, fk), jnp.where(low, fk, k2))
+    values = (jnp.where(low, v2, fk), jnp.where(low, fk, v2))
+    size = q_ref.shape[0] // 2
+    for t in range(2):
+        r = slice(t * size, (t + 1) * size)
+        q2, fq = q_ref[r] * jnp.bfloat16(0.125), fq_ref[r]
+        outs = []
+        for h, qs in enumerate((jnp.where(low, q2, fq), jnp.where(low, fq, q2))):
+            s = lax.dot_general(qs, keys[h], NT, preferred_element_type=jnp.float32)
+            top = jnp.max(s, axis=1, keepdims=True)
+            p = jnp.exp(s - top).astype(jnp.bfloat16)
+            acc = lax.dot_general(p, values[h], NN, preferred_element_type=jnp.float32)
+            base = HD + LSE_LANE if h == 0 else LSE_LANE
+            total = acc[:, base : base + 1]
+            outs.append(acc / total)
+            qa = qs.astype(jnp.float32)
+            for j, x in enumerate(split3(-(top + jnp.log(total)))):
+                qa = jnp.where(lane == base + j, x, qa)
+            qa_ref[h, r] = qa.astype(jnp.bfloat16)
+        o = jnp.where(low, outs[0], outs[1])
+        o_ref[r] = o
+        ol_ref[r] = o.astype(jnp.bfloat16)
+
+
+def attend(q, kv, fq, fk, heads=12):
+    rows, d = q.shape
+    nk, pairs = kv.shape[0], heads // 2
+    row = pl.BlockSpec((rows, 128), lambda p: (0, p))
+    return pl.pallas_call(
+        fwd_kernel,
+        grid=(pairs,),
+        in_specs=[
+            row,
+            pl.BlockSpec((nk, 128), lambda p: (0, p)),
+            pl.BlockSpec((nk, 128), lambda p: (0, p + pairs)),
+            pl.BlockSpec((rows, 128), lambda p: (0, 0)),
+            pl.BlockSpec((nk, 128), lambda p: (0, 0)),
+        ],
+        out_specs=[row, row, pl.BlockSpec((2, rows, 128), lambda p: (p, 0, 0))],
+        out_shape=[
+            jax.ShapeDtypeStruct((rows, d), jnp.float32),
+            jax.ShapeDtypeStruct((rows, d), jnp.bfloat16),
+            jax.ShapeDtypeStruct((heads, rows, 128), jnp.bfloat16),
+        ],
+        compiler_params=pltpu.CompilerParams(vmem_limit_bytes=60 << 20),
+        cost_estimate=pl.CostEstimate(flops=rows, bytes_accessed=rows, transcendentals=0),
+        name="attend",
+    )(q, kv, kv, fq, fk)
+
+
+def bwd_kernel(qa_ref, k_ref, v_ref, fk_ref, g_ref, o_ref, dq_ref, dk_ref, dv_ref, ds_ref):
+    nk = k_ref.shape[0]
+    lane = lax.broadcasted_iota(jnp.int32, (1, 128), 1)
+    low = lane < HD
+    g = g_ref[...].astype(jnp.float32)
+    prod = g * o_ref[...]
+    gs = []
+    for h in range(2):
+        own = low if h == 0 else jnp.logical_not(low)
+        base = HD + LSE_LANE if h == 0 else LSE_LANE
+        delta = jnp.sum(jnp.where(own, prod, 0.0), axis=1, keepdims=True)
+        ga = jnp.where(own, g, 0.0)
+        for j, t in enumerate(split3(-delta)):
+            ga = jnp.where(lane == base + j, t, ga)
+        gs.append(ga.astype(jnp.bfloat16))
+    for at in range(0, nk, 3 * KB):
+        r = slice(at, min(at + 3 * KB, nk))
+        k2, v2, fk = k_ref[r], v_ref[r], fk_ref[r]
+        dks, dvs = [], []
         for h in range(2):
-            s=lax.dot_general(qs[h],ka[h,r,:],NT,preferred_element_type=jnp.float32)
-            s_ref[h,i]=s
-            m_ref[h]=jnp.maximum(m_ref[h],jnp.maximum(s[:,:128],s[:,128:]))
-        return 0
-    lax.fori_loop(0,cnt,first,0)
-    tops=[jnp.max(m_ref[h],axis=1,keepdims=True) for h in range(2)]
-    acc_ref[...]=jnp.zeros(acc_ref.shape,jnp.float32)
-    def second(i,_):
-        r=pl.ds(pl.multiple_of(idx_ref[i+1]*KB,KB),KB)
-        for h in range(2):
-            p=jnp.exp(s_ref[h,i]-tops[h]).astype(jnp.bfloat16)
-            acc_ref[h]+=lax.dot_general(p,va[h,r,:],NN,preferred_element_type=jnp.float32)
-        return 0
-    lax.fori_loop(0,cnt,second,0)
-    outs=[]
-    for h in range(2):
-        base=HD+LSE_LANE if h==0 else LSE_LANE
-        acc=acc_ref[h]
-        total=acc[:,base:base+1]
-        outs.append(acc/total)
-        hi,mid,lo=split3(-(tops[h]+jnp.log(total)))
-        qa=qs[h].astype(jnp.float32)
-        for j,t in enumerate((hi,mid,lo)):
-            qa=jnp.where(lane==base+j,t,qa)
-        qa_ref[h]=qa.astype(jnp.bfloat16)
-    o=jnp.where(low,outs[0],outs[1])
-    o_ref[...]=o
-    ol_ref[...]=o.astype(jnp.bfloat16)
-
-def attend(q,kv,idx,fq,fk,heads=12):
-    rows,d=q.shape
-    nk=kv.shape[0]
-    pairs=heads//2
-    nb=nk//KB
-    spec=pltpu.PrefetchScalarGridSpec(num_scalar_prefetch=1,grid=(pairs,),
-        in_specs=[pl.BlockSpec((rows,128),lambda p,i:(0,p)),
-                  pl.BlockSpec((nk,128),lambda p,i:(0,p)),
-                  pl.BlockSpec((nk,128),lambda p,i:(0,p+pairs)),
-                  pl.BlockSpec((rows,128),lambda p,i:(0,0)),
-                  pl.BlockSpec((nk,128),lambda p,i:(0,0))],
-        out_specs=[pl.BlockSpec((rows,128),lambda p,i:(0,p)),
-                   pl.BlockSpec((rows,128),lambda p,i:(0,p)),
-                   pl.BlockSpec((2,rows,128),lambda p,i:(p,0,0))],
-        scratch_shapes=[pltpu.VMEM((2,nk,128),jnp.bfloat16),pltpu.VMEM((2,nk,128),jnp.bfloat16),
-                        pltpu.VMEM((2,nb,rows,KB),jnp.float32),pltpu.VMEM((2,rows,128),jnp.float32),
-                        pltpu.VMEM((2,rows,128),jnp.float32)])
-    return pl.pallas_call(fwd_kernel,grid_spec=spec,
-        out_shape=[jax.ShapeDtypeStruct((rows,d),jnp.float32),jax.ShapeDtypeStruct((rows,d),jnp.bfloat16),
-                   jax.ShapeDtypeStruct((heads,rows,128),jnp.bfloat16)],
-        compiler_params=pltpu.CompilerParams(vmem_limit_bytes=60<<20),
-        cost_estimate=pl.CostEstimate(flops=rows*nk,bytes_accessed=rows*d,transcendentals=0),
-        name="attend")(idx,q,kv,kv,fq,fk)
-
-def bwd_kernel(idx_ref,qa_ref,k_ref,v_ref,fk_ref,g_ref,o_ref,dq_ref,dk_ref,dv_ref,dqt):
-    cnt=idx_ref[0]
-    lane=lax.broadcasted_iota(jnp.int32,(1,128),1)
-    low=lane<HD
-    g=g_ref[...].astype(jnp.float32)
-    prod=g*o_ref[...]
-    gs=[]
-    for h in range(2):
-        own=low if h==0 else jnp.logical_not(low)
-        base=HD+LSE_LANE if h==0 else LSE_LANE
-        delta=jnp.sum(jnp.where(own,prod,0.0),axis=1,keepdims=True)
-        hi,mid,lo=split3(-delta)
-        ga=jnp.where(own,g,0.0)
-        for j,t in enumerate((hi,mid,lo)):
-            ga=jnp.where(lane==base+j,t,ga)
-        gs.append(ga.astype(jnp.bfloat16))
-    dk_ref[...]=jnp.zeros(dk_ref.shape,dk_ref.dtype)
-    dv_ref[...]=jnp.zeros(dv_ref.shape,dv_ref.dtype)
-    dqt[...]=jnp.zeros(dqt.shape,jnp.float32)
-    qs=(qa_ref[0],qa_ref[1])
-    def step(i,_):
-        r=pl.ds(pl.multiple_of(idx_ref[i+1]*KB,KB),KB)
-        k2=k_ref[r,:];v2=v_ref[r,:];fk=fk_ref[r,:]
-        dks=[];dvs=[]
-        for h in range(2):
-            ka=jnp.where(low,k2,fk) if h==0 else jnp.where(low,fk,k2)
-            va=jnp.where(low,v2,fk) if h==0 else jnp.where(low,fk,v2)
-            st=lax.dot_general(ka,qs[h],NT,preferred_element_type=jnp.float32)
-            dpt=lax.dot_general(va,gs[h],NT,preferred_element_type=jnp.float32)
-            pt=jnp.exp(st)
-            ds=(pt*dpt).astype(jnp.bfloat16)
-            dvs.append(lax.dot_general(pt.astype(jnp.bfloat16),gs[h],NN,preferred_element_type=jnp.float32))
-            dks.append(lax.dot_general(ds,qs[h],NN,preferred_element_type=jnp.float32))
-            dqt[h]+=lax.dot_general(ka.T,ds,NN,preferred_element_type=jnp.float32)
-        dk_ref[r,:]=jnp.where(low,dks[0],dks[1]).astype(dk_ref.dtype)
-        dv_ref[r,:]=jnp.where(low,dvs[0],dvs[1]).astype(dv_ref.dtype)
-        return 0
-    lax.fori_loop(0,cnt,step,0)
-    dq_ref[...]=(jnp.where(low,dqt[0].T,dqt[1].T)*0.125).astype(dq_ref.dtype)
-
-def attend_back(qa,kv,idx,fk,g,o,first,count,heads=12):
-    rows,d=g.shape
-    nk=kv.shape[0]
-    pairs=heads//2
-    spec=pltpu.PrefetchScalarGridSpec(num_scalar_prefetch=1,grid=(count,),
-        in_specs=[pl.BlockSpec((2,rows,128),lambda p,i:(p+first,0,0)),
-                  pl.BlockSpec((nk,128),lambda p,i:(0,p+first)),
-                  pl.BlockSpec((nk,128),lambda p,i:(0,p+first+pairs)),
-                  pl.BlockSpec((nk,128),lambda p,i:(0,0)),
-                  pl.BlockSpec((rows,128),lambda p,i:(0,p+first)),
-                  pl.BlockSpec((rows,128),lambda p,i:(0,p+first))],
-        out_specs=[pl.BlockSpec((rows,128),lambda p,i:(0,p)),
-                   pl.BlockSpec((nk,128),lambda p,i:(0,p)),
-                   pl.BlockSpec((nk,128),lambda p,i:(0,p))],
-        scratch_shapes=[pltpu.VMEM((2,128,rows),jnp.float32)])
-    return pl.pallas_call(bwd_kernel,grid_spec=spec,
-        out_shape=[jax.ShapeDtypeStruct((rows,128*count),jnp.bfloat16),jax.ShapeDtypeStruct((nk,128*count),jnp.bfloat16),
-                   jax.ShapeDtypeStruct((nk,128*count),jnp.bfloat16)],
-        compiler_params=pltpu.CompilerParams(vmem_limit_bytes=60<<20),
-        cost_estimate=pl.CostEstimate(flops=rows*nk,bytes_accessed=rows*d,transcendentals=0),
-        name="attend_back")(idx,qa,kv,kv,fk,g,o)
+            ka = jnp.where(low, k2, fk) if h == 0 else jnp.where(low, fk, k2)
+            va = jnp.where(low, v2, fk) if h == 0 else jnp.where(low, fk, v2)
+            pt = jnp.exp(lax.dot_general(ka, qa_ref[h], NT, preferred_element_type=jnp.float32))
+            dpt = lax.dot_general(va, gs[h], NT, preferred_element_type=jnp.float32)
+            ds = (pt * dpt).astype(jnp.bfloat16)
+            ds_ref[h, r] = ds
+            dvs.append(lax.dot_general(pt.astype(jnp.bfloat16), gs[h], NN, preferred_element_type=jnp.float32))
+            dks.append(lax.dot_general(ds, qa_ref[h], NN, preferred_element_type=jnp.float32))
+        dk_ref[r] = jnp.where(low, dks[0], dks[1]).astype(dk_ref.dtype)
+        dv_ref[r] = jnp.where(low, dvs[0], dvs[1]).astype(dv_ref.dtype)
+    kt = k_ref[...].T
+    dqs = [lax.dot_general(kt, ds_ref[h], NN, preferred_element_type=jnp.float32) for h in range(2)]
+    top = lax.broadcasted_iota(jnp.int32, (128, 1), 0) < HD
+    dq_ref[...] = (jnp.where(top, dqs[0], dqs[1]).T * 0.125).astype(dq_ref.dtype)
+
+
+def attend_back(qa, kv, fk, g, o, first, count, heads=12):
+    rows, nk, pairs = g.shape[0], kv.shape[0], heads // 2
+    row = pl.BlockSpec((rows, 128), lambda p: (0, p + first))
+    key = pl.BlockSpec((nk, 128), lambda p: (0, p))
+    return pl.pallas_call(
+        bwd_kernel,
+        grid=(count,),
+        in_specs=[
+            pl.BlockSpec((2, rows, 128), lambda p: (p + first, 0, 0)),
+            pl.BlockSpec((nk, 128), lambda p: (0, p + first)),
+            pl.BlockSpec((nk, 128), lambda p: (0, p + first + pairs)),
+            pl.BlockSpec((nk, 128), lambda p: (0, 0)),
+            row,
+            row,
+        ],
+        out_specs=[pl.BlockSpec((rows, 128), lambda p: (0, p)), key, key],
+        out_shape=[jax.ShapeDtypeStruct((n, 128 * count), jnp.bfloat16) for n in (rows, nk, nk)],
+        scratch_shapes=[pltpu.VMEM((2, nk, rows), jnp.bfloat16)],
+        compiler_params=pltpu.CompilerParams(vmem_limit_bytes=60 << 20),
+        cost_estimate=pl.CostEstimate(flops=rows, bytes_accessed=rows, transcendentals=0),
+        name="attend_back",
+    )(qa, kv, kv, fk, g, o)
+
 
 def features(seg_query,seg_key):
     j=jnp.arange(128,dtype=jnp.int32)[None,:]%HD
     fq=jnp.where((j<10)&(j!=seg_query[:,None]),NEG,0.0).astype(jnp.bfloat16)
     fk=(((j<10)&(j==seg_key[:,None]))|((j>=LSE_LANE)&(j<LSE_LANE+3))).astype(jnp.bfloat16)
     return fq,fk
-
-def active(seg_query,seg_key):
-    nb=seg_key.shape[0]//KB
-    lo=jnp.min(seg_query);hi=jnp.max(seg_query)
-    sk=seg_key.reshape(nb,KB)
-    use=jnp.any((sk<0)|((sk>=lo)&(sk<=hi)),axis=1)
-    slot=jnp.arange(nb,dtype=jnp.int32)
-    rank=jnp.sum((use[None,:]&(slot[None,:]<slot[:,None])).astype(jnp.int32),axis=1)
-    order=jnp.sum(jnp.where(use[None,:]&(rank[None,:]==slot[:,None]),slot[None,:],0),axis=1)
-    return jnp.concatenate([jnp.sum(use.astype(jnp.int32))[None],order]).astype(jnp.int32)
 
 
 D = 768
@@ -306,6 +280,10 @@
     return slice(c * WIDE, (c + 1) * WIDE)
 
 
+def joined(chunk):
+    return jnp.concatenate([mat(chunk[:, 0]), mat(chunk[:, 1])], axis=1)
+
+
 def gelu_parts(u):
     root = math.sqrt(2.0 / math.pi)
     t = jnp.tanh(root * (u + 0.044715 * (u * u * u)))
@@ -314,13 +292,13 @@
 
 def qkv_kernel(rows_ref, w_ref, kv_ref, q_ref):
     step = pl.program_id(0)
-    weight = mat(w_ref[:, 0])
-
-    @pl.when(step < 4)
+    weight = joined(w_ref[...])
+
+    @pl.when(step < 2)
     def _():
         kv_ref[...] = dot_nn(rows_ref[...], weight).astype(kv_ref.dtype)
 
-    @pl.when(step >= 4)
+    @pl.when(step == 2)
     def _():
         q_ref[...] = dot_nn(rows_ref[: q_ref.shape[0]], weight).astype(q_ref.dtype)
 
@@ -329,17 +307,14 @@
     count = rows_all.shape[0]
     return pl.pallas_call(
         qkv_kernel,
-        grid=(6,),
+        grid=(3,),
         in_specs=[
             pl.BlockSpec((count, D), lambda t: (0, 0)),
-            pl.BlockSpec(
-                (BLOCKS, 1, PIECE, WIDE),
-                lambda t: (0, t % 2, jnp.where(t < 4, first + 1 + t // 2, first), 0),
-            ),
+            pl.BlockSpec((BLOCKS, 2, PIECE, WIDE), lambda t: (0, 0, jnp.where(t < 2, first + 1 + t, first), 0)),
         ],
         out_specs=[
-            pl.BlockSpec((count, WIDE), lambda t: (0, jnp.minimum(t, 3))),
-            pl.BlockSpec((own, WIDE), lambda t: (0, jnp.maximum(t - 4, 0))),
+            pl.BlockSpec((count, D), lambda t: (0, jnp.minimum(t, 1))),
+            pl.BlockSpec((own, D), lambda t: (0, 0)),
         ],
         out_shape=[
             jax.ShapeDtypeStruct((count, 2 * D), jnp.bfloat16),
@@ -351,24 +326,29 @@
     )(rows_all, weights)
 
 
+def halves(ref):
+    half = ref.shape[0] // 2
+    return (slice(0, half), slice(half, 2 * half))
+
+
 def mlp_kernel(h_ref, o_ref, gain_ref, next_ref, wo_ref, wu_ref, wd_ref, mid_ref, sec_ref, u_ref, act_ref, res_ref, nrm_ref):
     step = pl.program_id(0)
 
     @pl.when(step == 0)
     def _():
-        for c in range(2):
-            part = dot_nn(o_ref[...], mat(wo_ref[:, c]))
-            mid_ref[:, columns(c)] = h_ref[:, columns(c)].astype(jnp.float32) + part
-        middle = mid_ref[...]
+        middle = h_ref[...].astype(jnp.float32) + dot_nn(o_ref[...], joined(wo_ref[...]))
+        mid_ref[...] = middle
         sec_ref[...] = norm_rows(middle, gain_ref[...]).astype(sec_ref.dtype)
         res_ref[...] = middle
 
-    for p in range(2):
-        u = dot_nn(sec_ref[...], mat(wu_ref[:, 0, p * PIECE : (p + 1) * PIECE]))
-        u_ref[:, columns(p)] = u.astype(u_ref.dtype)
-        act_ref[:, columns(p)] = (u * gelu_parts(u)[0]).astype(act_ref.dtype)
-    for c in range(2):
-        res_ref[:, columns(c)] += dot_nn(act_ref[...], mat(wd_ref[:, c]))
+    up = jnp.concatenate([mat(wu_ref[:, 0, :PIECE]), mat(wu_ref[:, 0, PIECE:])], axis=1)
+    down = joined(wd_ref[...])
+    for part in halves(sec_ref):
+        u = dot_nn(sec_ref[part], up)
+        u_ref[part] = u.astype(u_ref.dtype)
+        active_part = (u * gelu_parts(u)[0]).astype(act_ref.dtype)
+        act_ref[part] = active_part
+        res_ref[part] += dot_nn(active_part, down)
 
     @pl.when(step == 3)
     def _():
@@ -426,14 +406,13 @@
         gb_ref[...] = g_ref[...].astype(gb_ref.dtype)
         acc[...] = jnp.zeros(acc.shape, jnp.float32)
 
-    low_grad = gb_ref[...]
-    for p in range(2):
-        part = slice(p * 2, p * 2 + 2)
-        grad = sum(dot_nt(low_grad[:, columns(c)], mat(wd_ref[part, c])) for c in range(2))
-        u = u_ref[:, columns(p)].astype(jnp.float32)
-        gu = (grad * sum(gelu_parts(u))).astype(gu_ref.dtype)
-        gu_ref[:, columns(p)] = gu
-        acc[...] += dot_nt(gu, mat(wu_ref[:, 0, p * PIECE : (p + 1) * PIECE]))
+    up = jnp.concatenate([mat(wu_ref[:, 0, :PIECE]), mat(wu_ref[:, 0, PIECE:])], axis=1)
+    down = joined(wd_ref[...])
+    for part in halves(gb_ref):
+        grad = dot_nt(gb_ref[part], down)
+        gu = (grad * sum(gelu_parts(u_ref[part].astype(jnp.float32)))).astype(gu_ref.dtype)
+        gu_ref[part] = gu
+        acc[part] += dot_nt(gu, up)
 
     @pl.when(step == 3)
     def _():
@@ -443,7 +422,7 @@
         gg_ref[...] = jnp.sum(gain_rows, axis=0, keepdims=True)
         low_middle = middle.astype(ga_ref.dtype)
         ga_ref[...] = low_middle
-        gat_ref[...] = sum(dot_nt(low_middle[:, columns(c)], mat(wo_ref[:, c])) for c in range(2)).astype(gat_ref.dtype)
+        gat_ref[...] = dot_nt(low_middle, joined(wo_ref[...])).astype(gat_ref.dtype)
 
 
 def feed_forward_back(grad, upward, middle, gain, w_out, out_piece, w_mlp):
@@ -469,51 +448,100 @@
     )(grad, upward, middle, gain[None], w_out, w_mlp, w_mlp)
 
 
-def rows_back_kernel(own, dk0, dk1, dv0, dv1, dq0, dq1, wq_ref, wk_ref, wv_ref, out_ref):
-    total = sum(
-        dot_nt(d[...], mat(w[:, c]))
-        for d, w, c in ((dk0, wk_ref, 0), (dk1, wk_ref, 1), (dv0, wv_ref, 0), (dv1, wv_ref, 1))
-    )
-    out_ref[...] = total
-
-    @pl.when(pl.program_id(0) < own)
+def rows_back_kernel(steps, half, dk0, dk1, dv0, dv1, dq0, dq1, wq_ref, wk_ref, wv_ref, near_ref, far_ref, full):
+    step = pl.program_id(0)
+
+    @pl.when(step == 0)
     def _():
-        out_ref[...] += sum(dot_nt(d[...], mat(wq_ref[:, c])) for d, c in ((dq0, 0), (dq1, 1)))
+        full[:, :D] = joined(wk_ref[...])
+        full[:, D:] = joined(wv_ref[...])
+
+    rows = jnp.concatenate([dk0[...], dk1[...], dv0[...], dv1[...]], axis=1)
+    total = dot_nt(rows, full[...])
+    away = (step >= half) & (step < 2 * half)
+
+    @pl.when(away)
+    def _():
+        far_ref[...] = total.astype(far_ref.dtype)
+
+    @pl.when(jnp.logical_not(away))
+    def _():
+        near_ref[...] = total
+
+    @pl.when(step < steps)
+    def _():
+        near_ref[...] += dot_nt(jnp.concatenate([dq0[...], dq1[...]], axis=1), joined(wq_ref[...]))
 
 
 def rows_back(one, two, weights, first):
-    count, own = one[1].shape[0], one[0].shape[0] // KB
-    tile = pl.BlockSpec((KB, WIDE), lambda t: (t, 0))
-    query = pl.BlockSpec((KB, WIDE), lambda t: (jnp.minimum(t, own - 1), 0))
+    count, size = one[1].shape[0], one[0].shape[0]
+    tokens = count // size * size
+    if count != tokens:
+        size = math.gcd(count, size)
+    steps, half = one[0].shape[0] // size, tokens // (2 * size)
+    tile = pl.BlockSpec((size, WIDE), lambda t: (t, 0))
+    query = pl.BlockSpec((size, WIDE), lambda t: (jnp.minimum(t, steps - 1), 0))
     piece = lambda i: pl.BlockSpec((BLOCKS, 2, PIECE, WIDE), lambda t: (0, 0, first + i, 0))
+    near = lambda t: (jnp.where(t < half, t, jnp.where(t < 2 * half, half, t - half)), 0)
+    far = lambda t: (jnp.clip(t - half, 0, half - 1), 0)
+    rest = count - half * size
+    spare = rest + size if count == tokens else rest
     return pl.pallas_call(
-        functools.partial(rows_back_kernel, own),
-        grid=(count // KB,),
+        functools.partial(rows_back_kernel, steps, half),
+        grid=(count // size,),
         in_specs=[tile, tile, tile, tile, query, query, piece(0), piece(1), piece(2)],
-        out_specs=pl.BlockSpec((KB, D), lambda t: (t, 0)),
-        out_shape=jax.ShapeDtypeStruct((count, D), jnp.float32),
+        out_specs=[pl.BlockSpec((size, D), near), pl.BlockSpec((size, D), far)],
+        out_shape=[
+            jax.ShapeDtypeStruct((spare, D), jnp.float32),
+            jax.ShapeDtypeStruct((half * size, D), jnp.bfloat16),
+        ],
+        scratch_shapes=[pltpu.VMEM((D, 2 * D), jnp.bfloat16)],
         compiler_params=pltpu.CompilerParams(vmem_limit_bytes=60 << 20),
-        cost_estimate=cheap(count),
+        cost_estimate=cheap(size),
         name="rows_back",
     )(one[1], two[1], one[2], two[2], one[0], two[0], weights, weights, weights)
 
 
-def products_kernel(plan, *refs):
-    *ins, out_ref, turned = refs
-    held = None
-    for left, column, count, right, at_column, block, half, at, tall in plan:
-        if held != (left, column):
-            turned[:, :count] = ins[left][:, column : column + D].T
-            held = (left, column)
-        part = dot_nn(turned[:, :count], ins[right][:, at_column : at_column + WIDE]).astype(out_ref.dtype)
-        if tall:
-            out_ref[block : block + 4, half, at : at + TALL] = part.reshape(4, TALL, WIDE)
-        else:
-            out_ref[:, half, at : at + PIECE] = part.reshape(BLOCKS, PIECE, WIDE)
-
-
-def products(wanted):
-    arrays, plan, at = [], [], 0
+def products_kernel(plan, count_in, *refs):
+    ins, (out_ref, turned) = refs[:count_in], refs[-2:]
+    step = pl.program_id(0)
+    for left, rights, begin, tiles, tall in plan:
+        count = ins[left].shape[0]
+
+        @pl.when(step == begin)
+        def _():
+            for i in range(0, ins[left].shape[1], D):
+                part = ins[left][:, i : i + D].T
+                if tall:
+                    turned[i // TALL : (i + D) // TALL, :, :count] = part.reshape(D // TALL, TALL, count)
+                else:
+                    turned[:, :PIECE, :count] = part.reshape(BLOCKS, PIECE, count)
+
+        @pl.when((step >= begin) & (step < begin + tiles))
+        def _():
+            n = step - begin
+            if tall:
+                at = pl.multiple_of(n * PIECE, PIECE)
+                rows = turned[:, pl.ds(at, PIECE), :count].reshape(D, count)
+            else:
+                rows = turned[:, :PIECE, :count].reshape(D, count)
+            if len(rights) == 2:
+                right = jnp.concatenate([ins[r][...] for r in rights], axis=1)
+            elif tall or tiles == 1:
+                right = ins[rights[0]][...]
+            else:
+                half = tiles * WIDE
+                parts = [
+                    ins[rights[0]][:, pl.ds(pl.multiple_of(n * WIDE + c * half, WIDE), WIDE)] for c in range(2)
+                ]
+                right = jnp.concatenate(parts, axis=1)
+            part = dot_nn(rows, right).astype(out_ref.dtype)
+            for c in range(2):
+                out_ref[:, c] = part[:, columns(c)].reshape(BLOCKS, PIECE, WIDE)
+
+
+def products(wanted, into=None, first=0, pieces=None):
+    arrays, plan, steps = [], [], 0
 
     def place(array):
         for i, known in enumerate(arrays):
@@ -523,27 +551,26 @@
         return len(arrays) - 1
 
     for left, rights in wanted:
-        pieces = [(place(r), i) for r in rights for i in range(0, r.shape[1], WIDE)]
-        index, count = place(left), left.shape[0]
-        if left.shape[1] == D:
-            wide = len(pieces) // 2
-            for n, (right, column) in enumerate(pieces):
-                plan.append((index, 0, count, right, column, 0, n // wide, at + n % wide * PIECE, False))
-            at += wide * PIECE
-        else:
-            for block in range(4):
-                for half, (right, column) in enumerate(pieces):
-                    plan.append((index, block * D, count, right, column, block * 4, half, at, True))
-            at += TALL
+        tall = left.shape[1] != D
+        tiles = left.shape[1] // D if tall else sum(r.shape[1] for r in rights) // D
+        plan.append((place(left), [place(r) for r in rights], steps, tiles, tall))
+        steps += tiles
+    given = [] if into is None else [into]
     longest = max(left.shape[0] for left, _ in wanted)
+    height = TALL if any(p[4] for p in plan) else PIECE
     return pl.pallas_call(
-        functools.partial(products_kernel, plan),
-        out_shape=jax.ShapeDtypeStruct((BLOCKS, 2, at, WIDE), jnp.bfloat16),
-        scratch_shapes=[pltpu.VMEM((D, longest), jnp.bfloat16)],
+        functools.partial(products_kernel, plan, len(arrays)),
+        grid=(steps,),
+        in_specs=[pl.BlockSpec(a.shape, lambda t: (0, 0), pipeline_mode=pl.Buffered(1)) for a in arrays]
+        + [pl.BlockSpec(memory_space=pl.ANY)] * len(given),
+        out_specs=pl.BlockSpec((BLOCKS, 2, PIECE, WIDE), lambda t: (0, 0, first + t, 0)),
+        out_shape=jax.ShapeDtypeStruct((BLOCKS, 2, (pieces or steps) * PIECE, WIDE), jnp.bfloat16),
+        input_output_aliases={len(arrays): 0} if given else {},
+        scratch_shapes=[pltpu.VMEM((BLOCKS, height, longest), jnp.bfloat16)],
         compiler_params=pltpu.CompilerParams(vmem_limit_bytes=60 << 20),
         cost_estimate=cheap(longest),
         name="products",
-    )(*arrays)
+    )(*arrays, *given)
 
 
 def to_blocks(gathered, sizes):
@@ -609,20 +636,69 @@
     return to_blocks(values.reshape(-1, rows, WIDE), sizes_of(shards)), after
 
 
-def collect(mine, wanted):
-    shares = from_sequence(mine)
+def collect_kernel(plan, own_ref, *refs):
+    count = len(refs) - len({p[3] for p in plan})
+    ins, outs = refs[:count], refs[count:]
+    for own in range(count):
+
+        @pl.when(own_ref[0] == own)
+        def _():
+            for device in range(count):
+                y, core = device // 2, device % 2
+                for half, at, rows, out, column in plan:
+                    if half == core:
+                        part = ins[device ^ own][at : at + rows].astype(jnp.float32)
+                        outs[out][y * rows : (y + 1) * rows, column : column + WIDE] = part
+
+
+def collect(mine, wanted, outs):
+    bits = seq_bits()
+    held = {0: mine}
+    for bit in reversed(bits):
+        held.update({m | bit: swap(t, bit) for m, t in list(held.items())})
+    pieces = [held[m] for m in masks_of(bits)]
     places = 1 << len(chip_bits())
-    results, at = [], 0
-    for height, width in wanted:
-        rows, wide = height // places, width // (2 * WIDE)
-        parts = [
-            jnp.concatenate([s[at + i * rows : at + (i + 1) * rows] for s in shares[core::2]], axis=0)
-            for core in range(2)
-            for i in range(wide)
-        ]
-        results.append(jnp.concatenate(parts, axis=1).astype(jnp.float32))
-        at += rows * wide
-    return results
+    plan, shapes, at = [], {}, 0
+    for (height, width), out in zip(wanted, outs):
+        rows, half = height // places, width // 2
+        begin = shapes.get(out, (0, 0))[1]
+        for i in range(0, half, WIDE):
+            plan += [(core, at, rows, out, begin + core * half + i) for core in range(2)]
+            at += rows
+        shapes[out] = (height // lax.axis_size("dp"), begin + width)
+    if any(p[2] % 16 for p in plan):
+        shares = absolute(pieces, bits)
+        results = [jnp.zeros(shape, jnp.float32) for shape in shapes.values()]
+        for core, at, rows, out, column in plan:
+            for y, share in enumerate(shares[core::2]):
+                part = share[at : at + rows].astype(jnp.float32)
+                results[out] = results[out].at[y * rows : (y + 1) * rows, column : column + WIDE].set(part)
+        return results, pieces
+    spec = pltpu.PrefetchScalarGridSpec(
+        num_scalar_prefetch=1,
+        grid=(1,),
+        in_specs=[pl.BlockSpec(mine.shape, lambda t, own: (0, 0)) for _ in pieces],
+        out_specs=[pl.BlockSpec(shape, lambda t, own: (0, 0)) for shape in shapes.values()],
+    )
+    results = pl.pallas_call(
+        functools.partial(collect_kernel, plan),
+        grid_spec=spec,
+        out_shape=[jax.ShapeDtypeStruct(shape, jnp.float32) for shape in shapes.values()],
+        compiler_params=pltpu.CompilerParams(vmem_limit_bytes=40 << 20),
+        cost_estimate=cheap(D),
+        name="collect",
+    )(lax.axis_index("seq").reshape(1), *pieces)
+    return results, pieces
+
+
+def across(pieces):
+    shares = absolute(pieces, seq_bits())
+    rows = jnp.concatenate([jnp.concatenate(shares[i : i + 2], axis=1) for i in range(0, len(shares), 2)], axis=0)
+    total = rows[None]
+    for group in groups_of(chip_bits()[len(seq_bits()) - 1 :]):
+        total = jnp.stack(absolute([total if m == 0 else swap(total, m) for m in masks_of(group)], group), axis=0)
+        total = total.reshape((-1,) + rows.shape)
+    return total.reshape(-1, rows.shape[1])
 
 
 def scatter_sums(chunks):
@@ -640,23 +716,14 @@
 
 
 def everywhere(values):
-    groups = groups_of([1] + chip_bits())
-    parts = 2 << len(chip_bits())
-    rows, wide = values.shape
-    if rows < parts:
-        for group in groups:
-            values = sum(values if m == 0 else swap(values, m) for m in masks_of(group))
-            values = (yield [values])[0]
-        return values
-    total = jnp.pad(values, ((0, -rows % (8 * parts)), (0, 0))).reshape(parts, -1, wide)
-    for group in groups:
-        total = share_low(total, group, 1 << len(group))
-        total = (yield [total])[0]
-    for group in reversed(groups):
-        pieces = absolute([total if m == 0 else swap(total, m) for m in masks_of(group)], group)
-        total = jnp.stack(pieces, axis=1).reshape((-1,) + total.shape[1:])
-        total = (yield [total])[0]
-    return total.reshape(-1, wide)[:rows]
+    for group in groups_of([1] + chip_bits()):
+        values = sum(values if m == 0 else swap(values, m) for m in masks_of(group))
+        values = (yield [values])[0]
+    return values
+
+
+def waited(values):
+    return (yield [values])[0]
 
 
 class Running:
@@ -685,23 +752,23 @@
 
 
 def attention_backward(grad_attended, kept, mask, between):
-    idx, _, feature_k = mask
+    feature_k = mask[1]
     keyval, attended, kept_q = kept
     pairs = HEADS // 2
     cut = pairs // 2
-    one = attend_back(kept_q, keyval, idx, feature_k, grad_attended, attended, 0, cut)
+    one = attend_back(kept_q, keyval, feature_k, grad_attended, attended, 0, cut)
     one, grad_attended = between((one, grad_attended))
-    two = attend_back(kept_q, keyval, idx, feature_k, grad_attended, attended, cut, pairs - cut)
+    two = attend_back(kept_q, keyval, feature_k, grad_attended, attended, cut, pairs - cut)
     return one, two
 
 
-def summed_rows(grad_all):
-    rows = grad_all
-    for bit in seq_bits()[:-1]:
+def summed_rows(near, far):
+    rows = near[: far.shape[0]] + swap(far, 1).astype(jnp.float32)
+    for bit in seq_bits()[1:-1]:
         half = rows.shape[0] // 2
         rows = rows[:half] + swap(low(rows[half:]), bit).astype(jnp.float32)
     half = rows.shape[0] // 2
-    return rows[:half], swap(low(rows[half:]), seq_bits()[-1])
+    return rows[:half], low(rows[half:])
 
 
 def local(
@@ -742,8 +809,8 @@
     class_slots = jnp.arange(CLASS_ROWS, dtype=jnp.int32)
     seg_key = jnp.concatenate([seg_rows, jnp.where(class_slots < class_count, -1, IMGS + 1)])
     feature_q, feature_k = features(seg_query, seg_key)
-    enc_mask = (active(seg_query, seg_rows), feature_q, feature_k[: seg_rows.shape[0]])
-    dec_mask = (active(seg_query, seg_key), feature_q, feature_k)
+    enc_mask = (feature_q, feature_k[: seg_rows.shape[0]])
+    dec_mask = (feature_q, feature_k)
     valid_rows = (seg_query < IMGS).astype(jnp.float32)[:, None]
     enc_normed = low(norm_rows(inputs_f, gains_f[0]))
     enc_rows = gather_rows(enc_normed)
@@ -801,14 +868,18 @@
     dec_chunks, grad_attended = lax.optimization_barrier((dec_chunks, grad_attended))
     dec_sum = scatter_sums(from_blocks(dec_chunks, [TALL] + 7 * [PIECE]))
     one, two = attention_backward(grad_attended, dec_attn, dec_mask, lambda v: v)
-    grad_all = rows_back(one, two, w_middle, 9)
-    token_rows = row_count * lax.axis_size("seq")
-    here, coming = summed_rows(grad_all[:token_rows])
+    near, far = rows_back(one, two, w_middle, 9)
+    here, going = summed_rows(near, far)
+    going, one, two = lax.optimization_barrier((going, one, two))
+    coming = swap(going, seq_bits()[-1])
     dec_qkv_chunks = products(
-        [(dec_normed, [one[0], two[0]]), (dec_rows, [one[1], two[1]]), (dec_rows, [one[2], two[2]])]
+        [(dec_normed, [one[0], two[0]]), (dec_rows, [one[1], two[1]]), (dec_rows, [one[2], two[2]])],
+        first=9,
+        pieces=12,
     )
     _, class_back = jax.vjp(norm_rows, classes_f, gains_f[2])
-    grad_classes_kv, grad_gain_class = class_back(grad_all[token_rows : token_rows + class_count])
+    grad_classes_kv, grad_gain_class = class_back(near[far.shape[0] : far.shape[0] + class_count])
+    coming, dec_qkv_chunks = lax.optimization_barrier((coming, dec_qkv_chunks))
     back, gain_rows = norm_back(here + coming.astype(jnp.float32), encoded, gains_f[2])
     grad_encoded = back + grad_middle
     padded_mask_gain = jnp.pad(grad_mask_gain, (0, D - class_count))
@@ -821,41 +892,42 @@
         ],
         axis=0,
     )
-    shared = Running(everywhere(shared))
-    dec_proj = Running(stepped_sums(from_blocks(dec_qkv_chunks, 3 * [PIECE])))
-    grad_encoded = tie(grad_encoded, dec_proj, shared)
+    per_block = CLASS_ROWS // BLOCKS
+    shared = low(jnp.pad(shared, ((0, CLASS_ROWS - shared.shape[0]), (0, 0))))
+    shared = shared.reshape(BLOCKS, per_block, 2, WIDE).transpose(0, 2, 1, 3)
     grad_branch, grad_upward, grad_middle, grad_attn, grad_attended, grad_gain_one = feed_forward_back(
         grad_encoded, enc_upward, enc_middle, gains_f[1], w_middle, 8, w_middle
     )
     enc_chunks = products(
-        [(enc_active, [grad_branch]), (enc_second, [grad_upward]), (enc_low, [grad_attn])]
-    )
-    enc_chunks, grad_attended, dec_sum = lax.optimization_barrier((enc_chunks, grad_attended, dec_sum))
-    enc_sum = scatter_sums(from_blocks(enc_chunks, [TALL] + 5 * [PIECE]))
-    grad_attended = tie(grad_attended, dec_proj, shared)
-    one, two = attention_backward(
-        grad_attended, enc_attn, enc_mask, lambda v: tie(v, dec_proj, shared)
-    )
-    one, two = tie((one, two), dec_proj, shared)
-    grad_all = rows_back(one, two, w_first, 0)
-    here, coming = summed_rows(grad_all)
-    grad_all, one, two = lax.optimization_barrier((grad_all, one, two))
+        [(enc_active, [grad_branch]), (enc_second, [grad_upward]), (enc_low, [grad_attn])],
+        into=dec_qkv_chunks,
+        pieces=12,
+    )
+    enc_chunks, grad_attended = lax.optimization_barrier((enc_chunks, grad_attended))
+    enc_sum = scatter_sums(from_blocks(enc_chunks, [TALL] + 8 * [PIECE]))
+    dec_sum = Running(waited(dec_sum))
+    one, two = attention_backward(grad_attended, enc_attn, enc_mask, lambda v: tie(v, dec_sum))
+    here, going = summed_rows(*rows_back(one, two, w_first, 0))
+    going, one, two = lax.optimization_barrier((going, one, two))
+    coming = swap(going, seq_bits()[-1])
     enc_qkv_chunks = products(
         [(enc_normed, [one[0], two[0]]), (enc_rows, [one[1], two[1]]), (enc_rows, [one[2], two[2]])]
     )
-    enc_proj = Running(stepped_sums(from_blocks(enc_qkv_chunks, 3 * [PIECE])))
-    here, coming = tie((here, coming), enc_proj, shared)
+    enc_qkv_chunks = jnp.concatenate([enc_qkv_chunks, shared], axis=2)
+    enc_proj = Running(stepped_sums(from_blocks(enc_qkv_chunks, 3 * [PIECE] + [per_block])))
+    here, coming = tie((here, coming), enc_proj)
     back, gain_rows = norm_back(here + coming.astype(jnp.float32), inputs_f, gains_f[0])
     grad_inputs = back + grad_middle
     late = Running(everywhere(jnp.stack([jnp.sum(gain_rows, axis=0), grad_gain_one[0]])))
     square, wide, tall = (D, D), (D, 4 * D), (4 * D, D)
-    thirds = [square] * 3
-    out_enc_qkv = jnp.concatenate(collect(enc_proj.finish(), thirds), axis=1)
+    qkv = [square, square, square]
+    (out_enc_qkv,), shares = collect(enc_proj.finish(), qkv, [0, 0, 0])
+    dec_sum, shares = lax.optimization_barrier((dec_sum.finish(), shares))
+    shared = across([t[-(per_block * BLOCKS >> len(chip_bits())) :] for t in shares]).astype(jnp.float32)
     late = late.finish()
-    out_dec_qkv = jnp.concatenate(collect(dec_proj.finish(), thirds), axis=1)
-    shared = shared.finish()
-    out_dec = collect(dec_sum, [tall, wide, square, square, square])
-    out_enc = collect(enc_sum, [tall, wide, square])
+    out_dec, _ = collect(dec_sum, [tall, wide, square, square, square], range(5))
+    out_enc, _ = collect(enc_sum, [tall, wide, square] + qkv, [0, 1, 2, 3, 3, 3])
+    out_dec_qkv = out_enc[3]
     gain_sums = jnp.concatenate([late, shared[class_count : class_count + 3]], axis=0)
     return (
         mask_out[None],

time: 748 us -> 686 us (0.917)
  Pallas kernels: 356 us -> 302 us
  waiting for transfers between devices: 185 us -> 233 us
  starting transfers between devices: 81.1 us -> 42.9 us
  other arithmetic: 54.6 us -> 45.8 us
  local copies, waits for them, and re-layouts: 40.9 us -> 33.4 us
    pallas_call x14 -> x17, Pallas kernels: 290 us -> 243 us  [the longest x4 77.4 us: attend_back(): pl.pallas_call(bwd_kernel, grid=(count,), in_specs=[pl.BlockSpec((2, rows...]
    reduce_scatter x2, waiting for transfers between devices: 0.02 us -> 45 us  [scatter_sums(): lax.psum_scatter(chunks.reshape((-1,) + chunks.shape[2:]), BOTH, scatter_...]
    ppermute x62 -> x42, starting transfers between devices: 81 us -> 42.8 us  [swap(): return lax.ppermute(values, ('seq', 'dp'), pairs)]
    all_gather x2, waiting for transfers between devices: 0.01 us -> 20.5 us  [gather_weights(): return lax.all_gather(bundle(shards), BOTH, axis=0)]
    ppermute x62 -> x42, waiting for transfers between devices: 185 us -> 167 us  [swap(): return lax.ppermute(values, ('seq', 'dp'), pairs)]
    unnamed x105 -> x121, local copies, waits for them, and re-layouts: 15.7 us -> 17.5 us
  transfers between devices with their start and end apart: 66 -> 46, of which waited for: 25 -> 22; matrix products, arithmetic and copies ran while one was open for 10% -> 9% of each run, Pallas kernels for 41% -> 37%
where the time goes in v3:
time: 686 us; the launch traced here: 681 us
  Pallas kernels  302 us (44%)
  waiting for transfers between devices  233 us (34%)
  other arithmetic  45.8 us (7%)
  starting transfers between devices  42.9 us (6%)
  local copies, waits for them, and re-layouts  33.4 us (5%)
  between operations  15.2 us (2%)
  matrix products  8.12 us (1%)
    ppermute x42, waiting for transfers between devices, swap(): return lax.ppermute(values, ('seq', 'dp'), pairs)  167 us
    pallas_call x4, Pallas kernels, attend_back(): pl.pallas_call(bwd_kernel, grid=(count,), in_specs=[pl.BlockSpec((2, rows...  77.4 us
    pallas_call x4, Pallas kernels, products(): pl.pallas_call(functools.partial(products_kernel, plan, len(arrays)), gri...  61 us
    pallas_call x2, Pallas kernels, attend(): pl.pallas_call(fwd_kernel, grid=(pairs,), in_specs=[row, pl.BlockSpec((nk...  49.2 us
    reduce_scatter x2, waiting for transfers between devices, scatter_sums(): lax.psum_scatter(chunks.reshape((-1,) + chunks.shape[2:]), BOTH, scatter_...  45 us
    ppermute x42, starting transfers between devices, swap(): return lax.ppermute(values, ('seq', 'dp'), pairs)  42.8 us
    pallas_call x2, Pallas kernels, feed_forward_back(): pl.pallas_call(mlp_back_kernel, grid=(4,), in_specs=[whole(full), tile, w...  30.9 us
    pallas_call x2, Pallas kernels, feed_forward(): pl.pallas_call(mlp_kernel, grid=(4,), in_specs=[whole(full), whole(full),...  28.7 us
  transfers between devices with their start and end apart: 46, of which 22 were waited for; matrix products, arithmetic and copies ran while one was open for 9% of the time, Pallas kernels for 37%

profile of v3, /device:TPU:0, one launch (start us, length us, event | category | flops | bytes accessed | tf_op | source)
XLA Modules:
  0.0 680.7 jit_solution(13732209614268635224)
XLA Ops:
  61.5 14.5 %collective-permute-done.7 = bf16[4,144,384]{2,1,0:T(8,128)(2,1)S(1)} collective-permute-done((bf16[4,144,384]{2,1,0:T(8,128)(2,1)S(1)}, bf16[4,144,384]{2,1,0:T(8,128)(2,1)S(1)}, u32[]{:S(2)}, u32[]{:S(2)}) %collective-permute-start.7) | collective-permute-done | bytes 442400 | tf_op jit(solution)/shard_map/ppermute | solution.py:199
  108.7 23.2 %attend.2 = (f32[512,768]{1,0:T(8,128)}, bf16[512,768]{1,0:T(8,128)(2,1)}, bf16[12,512,128]{2,1,0:T(8,128)(2,1)}) custom-call(bf16[512,768]{1,0:T(8,128)(2,1)} %get-tuple-element.120.q_ref, bf16[2048,1536]{1,0:T(8,128)(2,1)} %get-tuple-element.121.k_ref.v_ref, bf16[2048,1536]{1,0:T(8,128)(2,1)} %get-tuple-element.121.k_ref.v_ref, ...), custom_call_target="tpu_custom_call" | custom-call | flops 512 | bytes 512 | tf_op jit(solution)/shard_map/attend/pallas_call | solution.py:54
  140.6 14.0 %feed_forward.2 = (f32[512,768]{1,0:T(8,128)}, bf16[512,768]{1,0:T(8,128)(2,1)}, bf16[512,3072]{1,0:T(8,128)(2,1)}, bf16[512,3072]{1,0:T(8,128)(2,1)}, f32[512,768]{1,0:T(8,128)}, /*index=5*/bf16[512,768]{1,0:T(8,128)(2,1)}) custom-call(bf16[512,768]{1,0:T(8,128)(2,1)} %bitcast.166, bf16[512,768]{1,0:T(8,128)(2,1)} %get-tuple-element.123.o_ref.refs_4_, ...), custom_call_target="tpu_custom_call" | custom-call | flops 512 | bytes 512 | tf_op jit(solution)/shard_map/feed_forward/pallas_call | solution.py:373
  156.1 21.9 %collective-permute-done.9 = bf16[512,768]{1,0:T(8,128)(2,1)S(1)} collective-permute-done((bf16[512,768]{1,0:T(8,128)(2,1)}, bf16[512,768]{1,0:T(8,128)(2,1)S(1)}, u32[]{:S(2)}, u32[]{:S(2)}) %collective-permute-start.9) | collective-permute-done | bytes 786464 | tf_op jit(solution)/shard_map/ppermute | solution.py:199
  184.8 12.2 %project.3 = (bf16[2304,1536]{1,0:T(8,128)(2,1)}, bf16[512,768]{1,0:T(8,128)(2,1)}) custom-call(bf16[2304,768]{1,0:T(8,128)(2,1)} %fusion.2.rows_ref.refs_3_, bf16[16,2,624,384]{3,2,1,0:T(8,128)(2,1)} %bitcast.150), custom_call_target="tpu_custom_call" | custom-call | flops 512 | bytes 512 | tf_op jit(solution)/shard_map/project/pallas_call | solution.py:308
  197.0 26.0 %attend.3 = (f32[512,768]{1,0:T(8,128)}, bf16[512,768]{1,0:T(8,128)(2,1)}, bf16[12,512,128]{2,1,0:T(8,128)(2,1)}) custom-call(bf16[512,768]{1,0:T(8,128)(2,1)} %get-tuple-element.126.q_ref, bf16[2304,1536]{1,0:T(8,128)(2,1)} %get-tuple-element.127.k_ref.v_ref, bf16[2304,1536]{1,0:T(8,128)(2,1)} %get-tuple-element.127.k_ref.v_ref, ...), custom_call_target="tpu_custom_call" | custom-call | flops 512 | bytes 512 | tf_op jit(solution)/shard_map/attend/pallas_call | solution.py:54
  223.0 11.9 %all-gather.7.cloned.1.call-done = bf16[15360,384]{1,0:T(8,128)(2,1)} async-done(((bf16[480,384]{1,0:T(8,128)(2,1)}), bf16[15360,384]{1,0:T(8,128)(2,1)}) %all-gather.7.cloned.1.call-update) | async-done | bytes 11796496 | tf_op jit(solution)/shard_map/all_gather | solution.py:623
  238.0 14.7 %feed_forward.3 = (f32[512,768]{1,0:T(8,128)}, bf16[512,768]{1,0:T(8,128)(2,1)}, bf16[512,3072]{1,0:T(8,128)(2,1)}, bf16[512,3072]{1,0:T(8,128)(2,1)}, f32[512,768]{1,0:T(8,128)}, /*index=5*/bf16[512,768]{1,0:T(8,128)(2,1)}) custom-call(f32[512,768]{1,0:T(8,128)} %get-tuple-element.124.h_ref, bf16[512,768]{1,0:T(8,128)(2,1)} %get-tuple-element.129.o_ref.refs_4_, ...), custom_call_target="tpu_custom_call" | custom-call | flops 512 | bytes 512 | tf_op jit(solution)/shard_map/feed_forward/pallas_call | solution.py:373
  264.2 15.3 %feed_forward_back.2 = (bf16[512,768]{1,0:T(8,128)(2,1)}, bf16[512,3072]{1,0:T(8,128)(2,1)}, f32[512,768]{1,0:T(8,128)}, bf16[512,768]{1,0:T(8,128)(2,1)}, bf16[512,768]{1,0:T(8,128)(2,1)}, /*index=5*/f32[1,768]{1,0:T(1,128)}) custom-call(f32[512,768]{1,0:T(8,128)} %broadcast_add_fusion.g_ref, bf16[512,3072]{1,0:T(8,128)(2,1)} %get-tuple-element.137.u_ref, ...), custom_call_target="tpu_custom_call" | custom-call | flops 512 | bytes 512 | tf_op jit(solution)/shard_map/feed_forward_back/pallas_call | solution.py:431
  279.5 17.1 %products.4 = bf16[16,2,528,384]{3,2,1,0:T(8,128)(2,1)} custom-call(bf16[512,3072]{1,0:T(8,128)(2,1)} %get-tuple-element.135.refs_0_, bf16[512,768]{1,0:T(8,128)(2,1)} %get-tuple-element.139.refs_1_, bf16[512,768]{1,0:T(8,128)(2,1)} %get-tuple-element.140.refs_2_, bf16[512,3072]{1,0:T(8,128)(2,1)} %get-tuple-element.141.refs_3_, ...), custom_call_target="tpu_custom_call" | custom-call | flops 512 | bytes 512 | tf_op jit(solution)/shard_map/products/pallas_call | solution.py:561
  296.7 20.4 %attend_back.5 = (bf16[512,384]{1,0:T(8,128)(2,1)}, bf16[2304,384]{1,0:T(8,128)(2,1)}, bf16[2304,384]{1,0:T(8,128)(2,1)}) custom-call(bf16[12,512,128]{2,1,0:T(8,128)(2,1)} %get-tuple-element.134.qa_ref, bf16[2304,1536]{1,0:T(8,128)(2,1)} %get-tuple-element.127.k_ref.v_ref, bf16[2304,1536]{1,0:T(8,128)(2,1)} %get-tuple-element.127.k_ref.v_ref, ...), custom_call_target="tpu_custom_call" | custom-call | flops 512 | bytes 512 | tf_op jit(solution)/shard_map/attend_back/pallas_call | solution.py:116
  317.1 20.3 %attend_back.4 = (bf16[512,384]{1,0:T(8,128)(2,1)}, bf16[2304,384]{1,0:T(8,128)(2,1)}, bf16[2304,384]{1,0:T(8,128)(2,1)}) custom-call(bf16[12,512,128]{2,1,0:T(8,128)(2,1)} %get-tuple-element.134.qa_ref, bf16[2304,1536]{1,0:T(8,128)(2,1)} %get-tuple-element.127.k_ref.v_ref, bf16[2304,1536]{1,0:T(8,128)(2,1)} %get-tuple-element.127.k_ref.v_ref, ...), custom_call_target="tpu_custom_call" | custom-call | flops 512 | bytes 512 | tf_op jit(solution)/shard_map/attend_back/pallas_call | solution.py:116
  337.4 15.1 %rows_back.2 = (f32[1280,768]{1,0:T(8,128)}, bf16[1024,768]{1,0:T(8,128)(2,1)}) custom-call(bf16[2304,384]{1,0:T(8,128)(2,1)} %get-tuple-element.157.dk0.refs_4_, bf16[2304,384]{1,0:T(8,128)(2,1)} %get-tuple-element.158.dk1.refs_5_, bf16[2304,384]{1,0:T(8,128)(2,1)} %get-tuple-element.159.dv0.refs_6_, bf16[2304,384]{1,0:T(8,128)(2,1)} %get-tuple-element.160.dv1.refs_7_, ...), custom_call_target="tpu_custom_call" | custom-call | flops 256 | bytes 256 | tf_op jit(solution)/shard_map/rows_back/pallas_call | solution.py:489
  362.1 14.7 %products.5.refs_6_ = bf16[16,2,576,384]{3,2,1,0:T(8,128)(2,1)} custom-call(bf16[512,768]{1,0:T(8,128)(2,1)} %get-tuple-element.125.refs_0_, bf16[512,384]{1,0:T(8,128)(2,1)} %get-tuple-element.155.dq0.refs_1_, bf16[512,384]{1,0:T(8,128)(2,1)} %get-tuple-element.156.dq1.refs_2_, bf16[2304,768]{1,0:T(8,128)(2,1)} %fusion.2.rows_ref.refs_3_, ...), custom_call_target="tpu_custom_call" | custom-call | flops 2304 | bytes 2304 | tf_op jit(solution)/shard_map/products/pallas_call | solution.py:561
  387.2 15.6 %feed_forward_back.3 = (bf16[512,768]{1,0:T(8,128)(2,1)}, bf16[512,3072]{1,0:T(8,128)(2,1)}, f32[512,768]{1,0:T(8,128)}, bf16[512,768]{1,0:T(8,128)(2,1)}, bf16[512,768]{1,0:T(8,128)(2,1)}, /*index=5*/f32[1,768]{1,0:T(1,128)}) custom-call(f32[512,768]{1,0:T(8,128)} %multiply_add_fusion.g_ref, bf16[512,3072]{1,0:T(8,128)(2,1)} %get-tuple-element.163.u_ref, ...), custom_call_target="tpu_custom_call" | custom-call | flops 512 | bytes 512 | tf_op jit(solution)/shard_map/feed_forward_back/pallas_call | solution.py:431
  402.8 14.8 %products.6 = bf16[16,2,576,384]{3,2,1,0:T(8,128)(2,1)} custom-call(bf16[512,3072]{1,0:T(8,128)(2,1)} %get-tuple-element.133.refs_0_, bf16[512,768]{1,0:T(8,128)(2,1)} %get-tuple-element.165.refs_1_, bf16[512,768]{1,0:T(8,128)(2,1)} %get-tuple-element.166.refs_2_, bf16[512,3072]{1,0:T(8,128)(2,1)} %get-tuple-element.167.refs_3_, ...), custom_call_target="tpu_custom_call", output_to_operand_aliasing={{}: (6, {})} | custom-call | flops 512 | bytes 512 | tf_op jit(solution)/shard_map/products/pallas_call | solution.py:561
  417.6 18.2 %attend_back.6 = (bf16[512,384]{1,0:T(8,128)(2,1)}, bf16[2048,384]{1,0:T(8,128)(2,1)}, bf16[2048,384]{1,0:T(8,128)(2,1)}) custom-call(bf16[12,512,128]{2,1,0:T(8,128)(2,1)} %get-tuple-element.132.qa_ref, bf16[2048,1536]{1,0:T(8,128)(2,1)} %get-tuple-element.121.k_ref.v_ref, bf16[2048,1536]{1,0:T(8,128)(2,1)} %get-tuple-element.121.k_ref.v_ref, ...), custom_call_target="tpu_custom_call" | custom-call | flops 512 | bytes 512 | tf_op jit(solution)/shard_map/attend_back/pallas_call | solution.py:116
  435.9 17.6 %reduce-scatter.3.cloned.1.call-done = bf16[1,528,384]{2,1,0:T(8,128)(2,1)} async-done(((bf16[32,528,384]{2,1,0:T(8,128)(2,1)}), bf16[1,528,384]{2,1,0:T(8,128)(2,1)}) %reduce-scatter.3.cloned.1.call-update) | async-done | bytes 405520 | tf_op jit(solution)/shard_map/reduce_scatter | solution.py:705
  453.5 18.4 %attend_back.7 = (bf16[512,384]{1,0:T(8,128)(2,1)}, bf16[2048,384]{1,0:T(8,128)(2,1)}, bf16[2048,384]{1,0:T(8,128)(2,1)}) custom-call(bf16[12,512,128]{2,1,0:T(8,128)(2,1)} %get-tuple-element.132.qa_ref, bf16[2048,1536]{1,0:T(8,128)(2,1)} %get-tuple-element.121.k_ref.v_ref, bf16[2048,1536]{1,0:T(8,128)(2,1)} %get-tuple-element.121.k_ref.v_ref, ...), custom_call_target="tpu_custom_call" | custom-call | flops 512 | bytes 512 | tf_op jit(solution)/shard_map/attend_back/pallas_call | solution.py:116
  472.0 12.4 %rows_back.3 = (f32[1536,768]{1,0:T(8,128)}, bf16[1024,768]{1,0:T(8,128)(2,1)}) custom-call(bf16[2048,384]{1,0:T(8,128)(2,1)} %get-tuple-element.189.dk0.refs_4_, bf16[2048,384]{1,0:T(8,128)(2,1)} %get-tuple-element.190.dk1.refs_5_, bf16[2048,384]{1,0:T(8,128)(2,1)} %get-tuple-element.191.dv0.refs_6_, bf16[2048,384]{1,0:T(8,128)(2,1)} %get-tuple-element.192.dv1.refs_7_, ...), custom_call_target="tpu_custom_call" | custom-call | flops 512 | bytes 512 | tf_op jit(solution)/shard_map/rows_back/pallas_call | solution.py:489
  496.1 14.4 %products.7 = bf16[16,2,144,384]{3,2,1,0:T(8,128)(2,1)} custom-call(bf16[512,768]{1,0:T(8,128)(2,1)} %copy-done.11, bf16[512,384]{1,0:T(8,128)(2,1)} %get-tuple-element.187.dq0.refs_1_, bf16[512,384]{1,0:T(8,128)(2,1)} %get-tuple-element.188.dq1.refs_2_, bf16[2048,768]{1,0:T(8,128)(2,1)} %pad_maximum_fusion.1.rows_ref.refs_3_, ...), custom_call_target="tpu_custom_call" | custom-call | flops 2048 | bytes 2048 | tf_op jit(solution)/shard_map/products/pallas_call | solution.py:561
  520.7 25.8 %collective-permute-done.14 = bf16[512,768]{1,0:T(8,128)(2,1)} collective-permute-done((bf16[512,768]{1,0:T(8,128)(2,1)}, bf16[512,768]{1,0:T(8,128)(2,1)}, u32[]{:S(2)}, u32[]{:S(2)}) %collective-permute-start.14) | collective-permute-done | bytes 786464 | tf_op jit(solution)/shard_map/ppermute | solution.py:199
  555.7 25.3 %collective-permute-done.16 = bf16[4,160,384]{2,1,0:T(8,128)(2,1)} collective-permute-done((bf16[4,160,384]{2,1,0:T(8,128)(2,1)}, bf16[4,160,384]{2,1,0:T(8,128)(2,1)}, u32[]{:S(2)}, u32[]{:S(2)}) %collective-permute-start.16) | collective-permute-done | bytes 491552 | tf_op jit(solution)/shard_map/ppermute | solution.py:199
  620.9 27.4 %reduce-scatter.5.cloned.1.call-done = bf16[1,576,384]{2,1,0:T(8,128)(2,1)} async-done(((bf16[32,576,384]{2,1,0:T(8,128)(2,1)}), bf16[1,576,384]{2,1,0:T(8,128)(2,1)}) %reduce-scatter.5.cloned.1.call-update) | async-done | bytes 442384 | tf_op jit(solution)/shard_map/reduce_scatter | solution.py:705
  (344 shorter events, 234.2 us)
Async XLA Ops:
  7.2 133.4 %all-gather.5.cloned.1.call-start = ((), (), s32[]{:S(2)}) async-start(), calls=%async_computation.4 | async-start | bytes 15814656 | tf_op jit(solution)/shard_map/all_gather | solution.py:623
  14.9 219.9 %all-gather.7.cloned.1.call-start = ((), (), s32[]{:S(2)}) async-start(), calls=%async_computation.5 | async-start | bytes 12165120 | tf_op jit(solution)/shard_map/all_gather | solution.py:623
  21.4 432.1 %reduce-scatter.3.cloned.1.call-start = ((), (), s32[]{:S(2)}) async-start(), calls=%async_computation.2 | async-start | bytes 13381632 | tf_op jit(solution)/shard_map/reduce_scatter | solution.py:705
  26.7 16.5 %collective-permute-start.1 = (bf16[1,144,384]{2,1,0:T(8,128)(2,1)S(1)}, bf16[1,144,384]{2,1,0:T(8,128)(2,1)S(1)}, u32[]{:S(2)}, u32[]{:S(2)}) collective-permute-start(bf16[1,144,384]{2,1,0:T(8,128)(2,1)S(1)} %maximum_bitcast_fusion.2), channel_id=1, source_target_pairs={{0,4},{8,12},{16,20},{24,28},{1,5},{9,13},{17,21},{25,29},{2,6},{1... | collective-permute-start | bytes 331784 | tf_op jit(solution)/shard_map/ppermute | solution.py:199
  26.7 16.5 %collective-permute-start = (bf16[1,144,384]{2,1,0:T(8,128)(2,1)S(1)}, bf16[1,144,384]{2,1,0:T(8,128)(2,1)S(1)}, u32[]{:S(2)}, u32[]{:S(2)}) collective-permute-start(bf16[1,144,384]{2,1,0:T(8,128)(2,1)S(1)} %maximum_bitcast_fusion.2), channel_id=1, source_target_pairs={{0,2},{8,10},{16,18},{24,26},{1,3},{9,11},{17,19},{25,27},{2,0},{1... | collective-permute-start | bytes 331784 | tf_op jit(solution)/shard_map/ppermute | solution.py:199
  43.4 18.1 %collective-permute-start.6 = (bf16[4,144,384]{2,1,0:T(8,128)(2,1)S(1)}, bf16[4,144,384]{2,1,0:T(8,128)(2,1)S(1)}, u32[]{:S(2)}, u32[]{:S(2)}) collective-permute-start(bf16[4,144,384]{2,1,0:T(8,128)(2,1)S(1)} %maximum_bitcast_fusion), channel_id=1, source_target_pairs={{0,1},{8,9},{16,17},{24,25},{1,0},{9,8},{17,16},{25,24},{2,3},{10,... | collective-permute-start | bytes 1327112 | tf_op jit(solution)/shard_map/ppermute | solution.py:199
  46.3 29.7 %collective-permute-start.7 = (bf16[4,144,384]{2,1,0:T(8,128)(2,1)S(1)}, bf16[4,144,384]{2,1,0:T(8,128)(2,1)S(1)}, u32[]{:S(2)}, u32[]{:S(2)}) collective-permute-start(bf16[4,144,384]{2,1,0:T(8,128)(2,1)S(1)} %maximum_bitcast_fusion), channel_id=1, source_target_pairs={{0,17},{8,25},{16,1},{24,9},{1,16},{9,24},{17,0},{25,8},{2,19},{10... | collective-permute-start | bytes 1327112 | tf_op jit(solution)/shard_map/ppermute | solution.py:199
  47.4 28.5 %collective-permute-start.5 = (bf16[4,144,384]{2,1,0:T(8,128)(2,1)S(1)}, bf16[4,144,384]{2,1,0:T(8,128)(2,1)S(1)}, u32[]{:S(2)}, u32[]{:S(2)}) collective-permute-start(bf16[4,144,384]{2,1,0:T(8,128)(2,1)S(1)} %maximum_bitcast_fusion), channel_id=1, source_target_pairs={{0,16},{8,24},{16,0},{24,8},{1,17},{9,25},{17,1},{25,9},{2,18},{10... | collective-permute-start | bytes 1327112 | tf_op jit(solution)/shard_map/ppermute | solution.py:199
  48.7 39.8 %collective-permute-start.3 = (bf16[512,768]{1,0:T(8,128)(2,1)S(1)}, bf16[512,768]{1,0:T(8,128)(2,1)S(1)}, u32[]{:S(2)}, u32[]{:S(2)}) collective-permute-start(bf16[512,768]{1,0:T(8,128)(2,1)S(1)} %fusion.13.refs_0_), channel_id=1, source_target_pairs={{0,16},{8,24},{16,0},{24,8},{1,17},{9,25},{17,1},{25,9},{2,18},{10... | collective-permute-start | bytes 2359304 | tf_op jit(solution)/shard_map/ppermute | solution.py:199
  154.6 23.4 %collective-permute-start.9 = (bf16[512,768]{1,0:T(8,128)(2,1)}, bf16[512,768]{1,0:T(8,128)(2,1)S(1)}, u32[]{:S(2)}, u32[]{:S(2)}) collective-permute-start(bf16[512,768]{1,0:T(8,128)(2,1)} %get-tuple-element.125.refs_0_), channel_id=1, source_target_pairs={{0,16},{8,24},{16,0},{24,8},{1,17},{9,25},{17,1},{25,9},{2,18},{10... | collective-permute-start | bytes 2359304 | tf_op jit(solution)/shard_map/ppermute | solution.py:199
  296.6 351.7 %reduce-scatter.5.cloned.1.call-start = ((), (), s32[]{:S(2)}) async-start(), calls=%async_computation.3 | async-start | bytes 14598144 | tf_op jit(solution)/shard_map/reduce_scatter | solution.py:705
  360.2 21.5 %collective-permute-start.12 = (bf16[512,768]{1,0:T(8,128)(2,1)S(1)}, bf16[512,768]{1,0:T(8,128)(2,1)S(1)}, u32[]{:S(2)}, u32[]{:S(2)}) collective-permute-start(bf16[512,768]{1,0:T(8,128)(2,1)S(1)} %slice.242), channel_id=1, source_target_pairs={{0,16},{8,24},{16,0},{24,8},{1,17},{9,25},{17,1},{25,9},{2,18},{10... | collective-permute-start | bytes 2359304 | tf_op jit(solution)/shard_map/ppermute | solution.py:199
  514.0 32.5 %collective-permute-start.14 = (bf16[512,768]{1,0:T(8,128)(2,1)}, bf16[512,768]{1,0:T(8,128)(2,1)}, u32[]{:S(2)}, u32[]{:S(2)}) collective-permute-start(bf16[512,768]{1,0:T(8,128)(2,1)} %slice.241), channel_id=1, source_target_pairs={{0,16},{8,24},{16,0},{24,8},{1,17},{9,25},{17,1},{25,9},{2,18},{10... | collective-permute-start | bytes 2359304 | tf_op jit(solution)/shard_map/ppermute | solution.py:199
  547.7 33.3 %collective-permute-start.16 = (bf16[4,160,384]{2,1,0:T(8,128)(2,1)}, bf16[4,160,384]{2,1,0:T(8,128)(2,1)}, u32[]{:S(2)}, u32[]{:S(2)}) collective-permute-start(bf16[4,160,384]{2,1,0:T(8,128)(2,1)} %get-tuple-element.285), channel_id=1, source_target_pairs={{0,16},{8,24},{16,0},{24,8},{1,17},{9,25},{17,1},{25,9},{2,18},{10... | collective-permute-start | bytes 1474568 | tf_op jit(solution)/shard_map/ppermute | solution.py:199
  549.1 32.0 %collective-permute-start.18 = (bf16[4,160,384]{2,1,0:T(8,128)(2,1)}, bf16[4,160,384]{2,1,0:T(8,128)(2,1)}, u32[]{:S(2)}, u32[]{:S(2)}) collective-permute-start(bf16[4,160,384]{2,1,0:T(8,128)(2,1)} %get-tuple-element.286), channel_id=1, source_target_pairs={{0,17},{8,25},{16,1},{24,9},{1,16},{9,24},{17,0},{25,8},{2,19},{10... | collective-permute-start | bytes 1474568 | tf_op jit(solution)/shard_map/ppermute | solution.py:199
  550.5 34.6 %collective-permute-start.17 = (bf16[4,160,384]{2,1,0:T(8,128)(2,1)S(1)}, bf16[4,160,384]{2,1,0:T(8,128)(2,1)}, u32[]{:S(2)}, u32[]{:S(2)}) collective-permute-start(bf16[4,160,384]{2,1,0:T(8,128)(2,1)S(1)} %get-tuple-element.287), channel_id=1, source_target_pairs={{0,1},{8,9},{16,17},{24,25},{1,0},{9,8},{17,16},{25,24},{2,3},{10,... | collective-permute-start | bytes 1474568 | tf_op jit(solution)/shard_map/ppermute | solution.py:199
  554.3 58.8 %collective-permute-start.30 = (f32[2,768]{1,0:T(2,128)S(1)}, f32[2,768]{1,0:T(2,128)S(1)}, u32[]{:S(2)}, u32[]{:S(2)}) collective-permute-start(f32[2,768]{1,0:T(2,128)S(1)} %pad_maximum_fusion.13), channel_id=1, source_target_pairs={{0,16},{8,24},{16,0},{24,8},{1,17},{9,25},{17,1},{25,9},{2,18},{10... | collective-permute-start | bytes 18440 | tf_op jit(solution)/shard_map/ppermute | solution.py:199
  555.7 57.4 %collective-permute-start.31 = (f32[2,768]{1,0:T(2,128)S(1)}, f32[2,768]{1,0:T(2,128)S(1)}, u32[]{:S(2)}, u32[]{:S(2)}) collective-permute-start(f32[2,768]{1,0:T(2,128)S(1)} %pad_maximum_fusion.13), channel_id=1, source_target_pairs={{0,24},{8,16},{16,8},{24,0},{1,25},{9,17},{17,9},{25,1},{2,26},{10... | collective-permute-start | bytes 18440 | tf_op jit(solution)/shard_map/ppermute | solution.py:199
  592.8 20.3 %collective-permute-start.29 = (f32[2,768]{1,0:T(2,128)S(1)}, f32[2,768]{1,0:T(2,128)S(1)}, u32[]{:S(2)}, u32[]{:S(2)}) collective-permute-start(f32[2,768]{1,0:T(2,128)S(1)} %pad_maximum_fusion.13), channel_id=1, source_target_pairs={{0,8},{8,0},{16,24},{24,16},{1,9},{9,1},{17,25},{25,17},{2,10},{10... | collective-permute-start | bytes 18440 | tf_op jit(solution)/shard_map/ppermute | solution.py:199
  616.7 32.9 %collective-permute-start.26 = (bf16[1,32,768]{2,1,0:T(8,128)(2,1)S(1)}, bf16[1,32,768]{2,1,0:T(8,128)(2,1)S(1)}, u32[]{:S(2)}, u32[]{:S(2)}) collective-permute-start(bf16[1,32,768]{2,1,0:T(8,128)(2,1)S(1)} %maximum_bitcast_fusion.3), channel_id=1, source_target_pairs={{0,2},{8,10},{16,18},{24,26},{1,3},{9,11},{17,19},{25,27},{2,0},{1... | collective-permute-start | bytes 147464 | tf_op jit(solution)/shard_map/ppermute | solution.py:199
  616.8 33.5 %collective-permute-start.27 = (bf16[1,32,768]{2,1,0:T(8,128)(2,1)S(1)}, bf16[1,32,768]{2,1,0:T(8,128)(2,1)S(1)}, u32[]{:S(2)}, u32[]{:S(2)}) collective-permute-start(bf16[1,32,768]{2,1,0:T(8,128)(2,1)S(1)} %maximum_bitcast_fusion.3), channel_id=1, source_target_pairs={{0,3},{8,11},{16,19},{24,27},{1,2},{9,10},{17,18},{25,26},{2,1},{1... | collective-permute-start | bytes 147464 | tf_op jit(solution)/shard_map/ppermute | solution.py:199
  618.3 32.1 %collective-permute-start.25 = (bf16[1,32,768]{2,1,0:T(8,128)(2,1)S(1)}, bf16[1,32,768]{2,1,0:T(8,128)(2,1)S(1)}, u32[]{:S(2)}, u32[]{:S(2)}) collective-permute-start(bf16[1,32,768]{2,1,0:T(8,128)(2,1)S(1)} %maximum_bitcast_fusion.3), channel_id=1, source_target_pairs={{0,1},{8,9},{16,17},{24,25},{1,0},{9,8},{17,16},{25,24},{2,3},{10,... | collective-permute-start | bytes 147464 | tf_op jit(solution)/shard_map/ppermute | solution.py:199
  620.3 34.8 %collective-permute-start.35 = (f32[2,768]{1,0:T(2,128)S(1)}, f32[2,768]{1,0:T(2,128)S(1)}, u32[]{:S(2)}, u32[]{:S(2)}) collective-permute-start(f32[2,768]{1,0:T(2,128)S(1)} %add_add_fusion.4), channel_id=1, source_target_pairs={{0,4},{8,12},{16,20},{24,28},{1,5},{9,13},{17,21},{25,29},{2,6},{1... | collective-permute-start | bytes 18440 | tf_op jit(solution)/shard_map/ppermute | solution.py:199
  649.6 18.2 %collective-permute-start.40 = (bf16[528,384]{1,0:T(8,128)(2,1)S(1)}, bf16[528,384]{1,0:T(8,128)(2,1)S(1)}, u32[]{:S(2)}, u32[]{:S(2)}) collective-permute-start(bf16[528,384]{1,0:T(8,128)(2,1)S(1)} %bitcast.144), channel_id=1, source_target_pairs={{0,16},{8,24},{16,0},{24,8},{1,17},{9,25},{17,1},{25,9},{2,18},{10... | collective-permute-start | bytes 1216520 | tf_op jit(solution)/shard_map/ppermute | solution.py:199
  (74 other events, 784.1 us)
Sparse Core Ops, SparseCore 0:
  15.0 125.4 all-gather.4
  144.0 90.7 all-gather.6
  296.7 156.7 reduce-scatter.2
  459.4 188.8 reduce-scatter.4

commit v4 on v3

--- a/solution.py
+++ b/solution.py
@@ -243,6 +243,16 @@
     return absolute([mine if m == 0 else swap(mine, m) for m in masks_of(bits)], bits)
 
 
+def halve(total, bit, near, done):
+    low_bits = 1 if len(near) - done == 1 else 1 << near.index(bit)
+    values = total.reshape((total.shape[0] // (2 * low_bits), 2, low_bits) + total.shape[1:])
+    own = own_bit(bit)
+    arrived = swap(lax.dynamic_index_in_dim(values, 1 - own, 1, keepdims=False), bit)
+    kept = lax.dynamic_index_in_dim(values, own, 1, keepdims=False)
+    result = low(kept.astype(jnp.float32) + arrived.astype(jnp.float32))
+    return result.reshape((-1,) + total.shape[1:])
+
+
 def share_low(total, group, width):
     values = total.reshape((total.shape[0] // width, width) + total.shape[1:])
     own = lax.axis_index(BOTH)
@@ -502,8 +512,9 @@
     )(one[1], two[1], one[2], two[2], one[0], two[0], weights, weights, weights)
 
 
-def products_kernel(plan, count_in, *refs):
-    ins, (out_ref, turned) = refs[:count_in], refs[-2:]
+def products_kernel(plan, count_in, outs, *refs):
+    ins, turned = refs[outs - 1 : outs - 1 + count_in], refs[-1]
+    out_refs = refs[-1 - outs : -1]
     step = pl.program_id(0)
     for left, rights, begin, tiles, tall in plan:
         count = ins[left].shape[0]
@@ -535,12 +546,21 @@
                     ins[rights[0]][:, pl.ds(pl.multiple_of(n * WIDE + c * half, WIDE), WIDE)] for c in range(2)
                 ]
                 right = jnp.concatenate(parts, axis=1)
-            part = dot_nn(rows, right).astype(out_ref.dtype)
-            for c in range(2):
-                out_ref[:, c] = part[:, columns(c)].reshape(BLOCKS, PIECE, WIDE)
-
-
-def products(wanted, into=None, first=0, pieces=None):
+            part = dot_nn(rows, right).astype(jnp.bfloat16)
+            chunk = [part[:, columns(c)].reshape(BLOCKS, PIECE, WIDE) for c in range(2)]
+            if outs == 1:
+                for c in range(2):
+                    out_refs[0][:, c] = chunk[c]
+            else:
+                for core in range(2):
+
+                    @pl.when(refs[0][0] == core)
+                    def _():
+                        out_refs[0][...] = chunk[1 - core]
+                        out_refs[1][...] = chunk[core]
+
+
+def products(wanted, core=None, into=(), first=0, pieces=None):
     arrays, plan, steps = [], [], 0
 
     def place(array):
@@ -555,22 +575,34 @@
         tiles = left.shape[1] // D if tall else sum(r.shape[1] for r in rights) // D
         plan.append((place(left), [place(r) for r in rights], steps, tiles, tall))
         steps += tiles
-    given = [] if into is None else [into]
     longest = max(left.shape[0] for left, _ in wanted)
     height = TALL if any(p[4] for p in plan) else PIECE
-    return pl.pallas_call(
-        functools.partial(products_kernel, plan, len(arrays)),
+    rows = (pieces or steps) * PIECE
+    outs = 1 if core is None else 2
+    if core is None:
+        block, shape = (BLOCKS, 2, PIECE, WIDE), (BLOCKS, 2, rows, WIDE)
+        where = lambda t: (0, 0, first + t, 0)
+    else:
+        block, shape = (BLOCKS, PIECE, WIDE), (BLOCKS, rows, WIDE)
+        where = lambda t, _: (0, first + t, 0)
+    spec = pltpu.PrefetchScalarGridSpec(
+        num_scalar_prefetch=outs - 1,
         grid=(steps,),
-        in_specs=[pl.BlockSpec(a.shape, lambda t: (0, 0), pipeline_mode=pl.Buffered(1)) for a in arrays]
-        + [pl.BlockSpec(memory_space=pl.ANY)] * len(given),
-        out_specs=pl.BlockSpec((BLOCKS, 2, PIECE, WIDE), lambda t: (0, 0, first + t, 0)),
-        out_shape=jax.ShapeDtypeStruct((BLOCKS, 2, (pieces or steps) * PIECE, WIDE), jnp.bfloat16),
-        input_output_aliases={len(arrays): 0} if given else {},
+        in_specs=[pl.BlockSpec(a.shape, lambda t, *_: (0, 0), pipeline_mode=pl.Buffered(1)) for a in arrays]
+        + [pl.BlockSpec(memory_space=pl.ANY)] * len(into),
+        out_specs=[pl.BlockSpec(block, where)] * outs,
         scratch_shapes=[pltpu.VMEM((BLOCKS, height, longest), jnp.bfloat16)],
+    )
+    result = pl.pallas_call(
+        functools.partial(products_kernel, plan, len(arrays), outs),
+        grid_spec=spec,
+        out_shape=[jax.ShapeDtypeStruct(shape, jnp.bfloat16)] * outs,
+        input_output_aliases={outs - 1 + len(arrays) + i: i for i in range(len(into))},
         compiler_params=pltpu.CompilerParams(vmem_limit_bytes=60 << 20),
         cost_estimate=cheap(longest),
         name="products",
-    )(*arrays, *given)
+    )(*([] if core is None else [core.reshape(1)]), *arrays, *into)
+    return result[0] if core is None else result
 
 
 def to_blocks(gathered, sizes):
@@ -705,12 +737,23 @@
     return lax.psum_scatter(chunks.reshape((-1,) + chunks.shape[2:]), BOTH, scatter_dimension=0)
 
 
-def stepped_sums(chunks):
-    core = own_bit(1)
-    arrived = swap(lax.dynamic_index_in_dim(chunks, 1 - core, 1, keepdims=False), 1)
-    kept = lax.dynamic_index_in_dim(chunks, core, 1, keepdims=False)
-    total = (yield [low(kept.astype(jnp.float32) + arrived.astype(jnp.float32))])[0]
-    for group in groups_of(chip_bits()):
+def stepped_sums(send, keep, sizes, classes):
+    if 1 << len(chip_bits()) != BLOCKS:
+        chunks = from_blocks(jnp.stack([send, keep], axis=1), sizes)
+        send, keep = chunks[:, 0], chunks[:, 1]
+    arrived = swap(send, 1)
+    total = low(keep.astype(jnp.float32) + arrived.astype(jnp.float32))
+    bits = chip_bits()
+    if classes == 2:
+        near, bits = bits[:2], bits[2:]
+        cut = total.shape[1] // 2
+        parts = yield [total[:, :cut], total[:, cut:]]
+        for i in range(2):
+            parts = yield [halve(t, bit, near, i) for t, bit in zip(parts, (near[i], near[1 - i]))]
+        total = jnp.concatenate(parts, axis=1)
+    else:
+        total = (yield [total])[0]
+    for group in groups_of(bits):
         total = (yield [share_low(total, group, 1 << len(group))])[0]
     return total[0]
 
@@ -794,6 +837,7 @@
     last_shards = (dec_down, dec_up, patch_proj, class_proj)
     w_middle = to_blocks(gather_weights(middle_shards), sizes_of(middle_shards))
     gathered_last = gather_weights(last_shards)
+    core = own_bit(1)
     row_count = tokens.shape[1]
     index = lax.axis_index("seq")
     seq_lengths = lengths[0]
@@ -874,6 +918,7 @@
     coming = swap(going, seq_bits()[-1])
     dec_qkv_chunks = products(
         [(dec_normed, [one[0], two[0]]), (dec_rows, [one[1], two[1]]), (dec_rows, [one[2], two[2]])],
+        core,
         first=9,
         pieces=12,
     )
@@ -900,33 +945,40 @@
     )
     enc_chunks = products(
         [(enc_active, [grad_branch]), (enc_second, [grad_upward]), (enc_low, [grad_attn])],
+        core,
         into=dec_qkv_chunks,
         pieces=12,
     )
     enc_chunks, grad_attended = lax.optimization_barrier((enc_chunks, grad_attended))
-    enc_sum = scatter_sums(from_blocks(enc_chunks, [TALL] + 8 * [PIECE]))
+    enc_sum = Running(stepped_sums(*enc_chunks, [TALL] + 8 * [PIECE], 2))
     dec_sum = Running(waited(dec_sum))
-    one, two = attention_backward(grad_attended, enc_attn, enc_mask, lambda v: tie(v, dec_sum))
+    one, two = attention_backward(grad_attended, enc_attn, enc_mask, lambda v: tie(v, enc_sum))
+    one, two = tie((one, two), dec_sum)
     here, going = summed_rows(*rows_back(one, two, w_first, 0))
-    going, one, two = lax.optimization_barrier((going, one, two))
+    going, one, two = tie((going, one, two), enc_sum)
     coming = swap(going, seq_bits()[-1])
     enc_qkv_chunks = products(
-        [(enc_normed, [one[0], two[0]]), (enc_rows, [one[1], two[1]]), (enc_rows, [one[2], two[2]])]
-    )
-    enc_qkv_chunks = jnp.concatenate([enc_qkv_chunks, shared], axis=2)
-    enc_proj = Running(stepped_sums(from_blocks(enc_qkv_chunks, 3 * [PIECE] + [per_block])))
-    here, coming = tie((here, coming), enc_proj)
+        [(enc_normed, [one[0], two[0]]), (enc_rows, [one[1], two[1]]), (enc_rows, [one[2], two[2]])],
+        core,
+    )
+    enc_qkv_chunks, coming, enc_sum.values = lax.optimization_barrier((enc_qkv_chunks, coming, enc_sum.values))
+    enc_qkv_chunks = [
+        jnp.concatenate([t, lax.dynamic_index_in_dim(shared, c, 1, keepdims=False)], axis=1)
+        for t, c in zip(enc_qkv_chunks, (1 - core, core))
+    ]
+    enc_proj = Running(stepped_sums(*enc_qkv_chunks, 3 * [PIECE] + [per_block], 1))
+    here, coming = tie((here, coming), enc_proj, enc_sum)
     back, gain_rows = norm_back(here + coming.astype(jnp.float32), inputs_f, gains_f[0])
     grad_inputs = back + grad_middle
+    gain_rows, dec_sum = tie((gain_rows, dec_sum.finish()), enc_proj, enc_sum)
     late = Running(everywhere(jnp.stack([jnp.sum(gain_rows, axis=0), grad_gain_one[0]])))
     square, wide, tall = (D, D), (D, 4 * D), (4 * D, D)
     qkv = [square, square, square]
     (out_enc_qkv,), shares = collect(enc_proj.finish(), qkv, [0, 0, 0])
-    dec_sum, shares = lax.optimization_barrier((dec_sum.finish(), shares))
     shared = across([t[-(per_block * BLOCKS >> len(chip_bits())) :] for t in shares]).astype(jnp.float32)
     late = late.finish()
     out_dec, _ = collect(dec_sum, [tall, wide, square, square, square], range(5))
-    out_enc, _ = collect(enc_sum, [tall, wide, square] + qkv, [0, 1, 2, 3, 3, 3])
+    out_enc, _ = collect(enc_sum.finish(), [tall, wide, square] + qkv, [0, 1, 2, 3, 3, 3])
     out_dec_qkv = out_enc[3]
     gain_sums = jnp.concatenate([late, shared[class_count : class_count + 3]], axis=0)
     return (

time: 686 us -> 658 us (0.959)
  waiting for transfers between devices: 233 us -> 170 us
  other arithmetic: 45.8 us -> 64.5 us
  local copies, waits for them, and re-layouts: 33.4 us -> 43 us
    reduce_scatter x2 -> x1, waiting for transfers between devices: 45 us -> 0.01 us  [scatter_sums(): lax.psum_scatter(chunks.reshape((-1,) + chunks.shape[2:]), BOTH, scatter_...]
    ppermute x42 -> x50, waiting for transfers between devices: 167 us -> 151 us  [swap(): return lax.ppermute(values, ('seq', 'dp'), pairs)]
    convert_element_type x4 -> x6, other arithmetic: 2.69 us -> 15.5 us  [low(): return values.astype(jnp.bfloat16)]
    reshape x0 -> x3, other arithmetic: none -> 7.5 us  [halve(): return result.reshape((-1,) + total.shape[1:])]
    ppermute x42 -> x50, starting transfers between devices: 42.8 us -> 48.6 us  [swap(): return lax.ppermute(values, ('seq', 'dp'), pairs)]
    unnamed x121 -> x130, local copies, waits for them, and re-layouts: 17.5 us -> 17.4 us
  transfers between devices with their start and end apart: 46 -> 53, of which waited for: 22 -> 27; matrix products, arithmetic and copies ran while one was open for 9% -> 12% of each run, Pallas kernels for 37% -> 39%
where the time goes in v4:
time: 658 us; the launch traced here: 652 us
  Pallas kernels  303 us (46%)
  waiting for transfers between devices  170 us (26%)
  other arithmetic  64.5 us (10%)
  starting transfers between devices  48.8 us (7%)
  local copies, waits for them, and re-layouts  43 us (7%)
  between operations  15.3 us (2%)
  matrix products  7.52 us (1%)
    ppermute x50, waiting for transfers between devices, swap(): return lax.ppermute(values, ('seq', 'dp'), pairs)  151 us
    pallas_call x4, Pallas kernels, attend_back(): pl.pallas_call(bwd_kernel, grid=(count,), in_specs=[pl.BlockSpec((2, rows...  78.1 us
    pallas_call x4, Pallas kernels, products(): pl.pallas_call(functools.partial(products_kernel, plan, len(arrays), outs...  61.4 us
    pallas_call x2, Pallas kernels, attend(): pl.pallas_call(fwd_kernel, grid=(pairs,), in_specs=[row, pl.BlockSpec((nk...  49.2 us
    ppermute x50, starting transfers between devices, swap(): return lax.ppermute(values, ('seq', 'dp'), pairs)  48.6 us
    pallas_call x2, Pallas kernels, feed_forward_back(): pl.pallas_call(mlp_back_kernel, grid=(4,), in_specs=[whole(full), tile, w...  31 us
    pallas_call x2, Pallas kernels, feed_forward(): pl.pallas_call(mlp_kernel, grid=(4,), in_specs=[whole(full), whole(full),...  28.7 us
    pallas_call x2, Pallas kernels, rows_back(): pl.pallas_call(functools.partial(rows_back_kernel, steps, half), grid=(co...  26.8 us
  transfers between devices with their start and end apart: 53, of which 27 were waited for; matrix products, arithmetic and copies ran while one was open for 12% of the time, Pallas kernels for 39%

profile of v4, /device:TPU:0, one launch (start us, length us, event | category | flops | bytes accessed | tf_op | source)
XLA Modules:
  0.0 651.9 jit_solution(5216460324587887076)
XLA Ops:
  32.0 11.2 %collective-permute-done.1 = bf16[1,144,384]{2,1,0:T(8,128)(2,1)S(1)} collective-permute-done((bf16[1,144,384]{2,1,0:T(8,128)(2,1)S(1)}, bf16[1,144,384]{2,1,0:T(8,128)(2,1)S(1)}, u32[]{:S(2)}, u32[]{:S(2)}) %collective-permute-start.1) | collective-permute-done | bytes 110624 | tf_op jit(solution)/shard_map/ppermute | solution.py:199
  50.4 11.0 %collective-permute-done.6 = bf16[4,144,384]{2,1,0:T(8,128)(2,1)S(1)} collective-permute-done((bf16[4,144,384]{2,1,0:T(8,128)(2,1)S(1)}, bf16[4,144,384]{2,1,0:T(8,128)(2,1)S(1)}, u32[]{:S(2)}, u32[]{:S(2)}) %collective-permute-start.6) | collective-permute-done | bytes 442400 | tf_op jit(solution)/shard_map/ppermute | solution.py:199
  61.5 14.5 %collective-permute-done.7 = bf16[4,144,384]{2,1,0:T(8,128)(2,1)S(1)} collective-permute-done((bf16[4,144,384]{2,1,0:T(8,128)(2,1)S(1)}, bf16[4,144,384]{2,1,0:T(8,128)(2,1)S(1)}, u32[]{:S(2)}, u32[]{:S(2)}) %collective-permute-start.7) | collective-permute-done | bytes 442400 | tf_op jit(solution)/shard_map/ppermute | solution.py:199
  99.6 10.5 %project.2 = (bf16[2048,1536]{1,0:T(8,128)(2,1)}, bf16[512,768]{1,0:T(8,128)(2,1)}) custom-call(bf16[2048,768]{1,0:T(8,128)(2,1)} %pad_maximum_fusion.1.rows_ref.refs_4_, bf16[16,2,144,384]{3,2,1,0:T(8,128)(2,1)} %pad_maximum_fusion.w_ref.wq_ref.wk_ref.wv_ref), custom_call_target="tpu_custom_call" | custom-call | flops 512 | bytes 512 | tf_op jit(solution)/shard_map/project/pallas_call | solution.py:318
  110.2 23.2 %attend.2 = (f32[512,768]{1,0:T(8,128)}, bf16[512,768]{1,0:T(8,128)(2,1)}, bf16[12,512,128]{2,1,0:T(8,128)(2,1)}) custom-call(bf16[512,768]{1,0:T(8,128)(2,1)} %get-tuple-element.144.q_ref, bf16[2048,1536]{1,0:T(8,128)(2,1)} %get-tuple-element.145.k_ref.v_ref, bf16[2048,1536]{1,0:T(8,128)(2,1)} %get-tuple-element.145.k_ref.v_ref, ...), custom_call_target="tpu_custom_call" | custom-call | flops 512 | bytes 512 | tf_op jit(solution)/shard_map/attend/pallas_call | solution.py:54
  140.6 14.0 %feed_forward.2 = (f32[512,768]{1,0:T(8,128)}, bf16[512,768]{1,0:T(8,128)(2,1)}, bf16[512,3072]{1,0:T(8,128)(2,1)}, bf16[512,3072]{1,0:T(8,128)(2,1)}, f32[512,768]{1,0:T(8,128)}, /*index=5*/bf16[512,768]{1,0:T(8,128)(2,1)}) custom-call(bf16[512,768]{1,0:T(8,128)(2,1)} %bitcast.214, bf16[512,768]{1,0:T(8,128)(2,1)} %get-tuple-element.147.o_ref.refs_5_, ...), custom_call_target="tpu_custom_call" | custom-call | flops 512 | bytes 512 | tf_op jit(solution)/shard_map/feed_forward/pallas_call | solution.py:383
  156.1 21.9 %collective-permute-done.9 = bf16[512,768]{1,0:T(8,128)(2,1)S(1)} collective-permute-done((bf16[512,768]{1,0:T(8,128)(2,1)}, bf16[512,768]{1,0:T(8,128)(2,1)S(1)}, u32[]{:S(2)}, u32[]{:S(2)}) %collective-permute-start.9) | collective-permute-done | bytes 786464 | tf_op jit(solution)/shard_map/ppermute | solution.py:199
  184.8 12.2 %project.3 = (bf16[2304,1536]{1,0:T(8,128)(2,1)}, bf16[512,768]{1,0:T(8,128)(2,1)}) custom-call(bf16[2304,768]{1,0:T(8,128)(2,1)} %fusion.1.rows_ref.refs_4_, bf16[16,2,624,384]{3,2,1,0:T(8,128)(2,1)} %bitcast.199), custom_call_target="tpu_custom_call" | custom-call | flops 512 | bytes 512 | tf_op jit(solution)/shard_map/project/pallas_call | solution.py:318
  197.0 26.0 %attend.3 = (f32[512,768]{1,0:T(8,128)}, bf16[512,768]{1,0:T(8,128)(2,1)}, bf16[12,512,128]{2,1,0:T(8,128)(2,1)}) custom-call(bf16[512,768]{1,0:T(8,128)(2,1)} %get-tuple-element.150.q_ref, bf16[2304,1536]{1,0:T(8,128)(2,1)} %get-tuple-element.151.k_ref.v_ref, bf16[2304,1536]{1,0:T(8,128)(2,1)} %get-tuple-element.151.k_ref.v_ref, ...), custom_call_target="tpu_custom_call" | custom-call | flops 512 | bytes 512 | tf_op jit(solution)/shard_map/attend/pallas_call | solution.py:54
  223.0 11.8 %all-gather.7.cloned.1.call-done = bf16[15360,384]{1,0:T(8,128)(2,1)} async-done(((bf16[480,384]{1,0:T(8,128)(2,1)}), bf16[15360,384]{1,0:T(8,128)(2,1)}) %all-gather.7.cloned.1.call-update) | async-done | bytes 11796496 | tf_op jit(solution)/shard_map/all_gather | solution.py:655
  237.2 14.7 %feed_forward.3 = (f32[512,768]{1,0:T(8,128)}, bf16[512,768]{1,0:T(8,128)(2,1)}, bf16[512,3072]{1,0:T(8,128)(2,1)}, bf16[512,3072]{1,0:T(8,128)(2,1)}, f32[512,768]{1,0:T(8,128)}, /*index=5*/bf16[512,768]{1,0:T(8,128)(2,1)}) custom-call(f32[512,768]{1,0:T(8,128)} %get-tuple-element.148.h_ref, bf16[512,768]{1,0:T(8,128)(2,1)} %get-tuple-element.153.o_ref.refs_4_, ...), custom_call_target="tpu_custom_call" | custom-call | flops 512 | bytes 512 | tf_op jit(solution)/shard_map/feed_forward/pallas_call | solution.py:383
  262.9 15.3 %feed_forward_back.2 = (bf16[512,768]{1,0:T(8,128)(2,1)}, bf16[512,3072]{1,0:T(8,128)(2,1)}, f32[512,768]{1,0:T(8,128)}, bf16[512,768]{1,0:T(8,128)(2,1)}, bf16[512,768]{1,0:T(8,128)(2,1)}, /*index=5*/f32[1,768]{1,0:T(1,128)}) custom-call(f32[512,768]{1,0:T(8,128)} %broadcast_add_fusion.g_ref, bf16[512,3072]{1,0:T(8,128)(2,1)} %get-tuple-element.161.u_ref, ...), custom_call_target="tpu_custom_call" | custom-call | flops 512 | bytes 512 | tf_op jit(solution)/shard_map/feed_forward_back/pallas_call | solution.py:441
  278.1 16.9 %products.4 = bf16[16,2,528,384]{3,2,1,0:T(8,128)(2,1)} custom-call(bf16[512,3072]{1,0:T(8,128)(2,1)} %get-tuple-element.159.refs_0_, bf16[512,768]{1,0:T(8,128)(2,1)} %get-tuple-element.163.refs_1_, bf16[512,768]{1,0:T(8,128)(2,1)} %get-tuple-element.164.refs_2_, bf16[512,3072]{1,0:T(8,128)(2,1)} %get-tuple-element.165.refs_3_, ...), custom_call_target="tpu_custom_call" | custom-call | flops 512 | bytes 512 | tf_op jit(solution)/shard_map/products/pallas_call | solution.py:596
  295.1 20.6 %attend_back.5 = (bf16[512,384]{1,0:T(8,128)(2,1)}, bf16[2304,384]{1,0:T(8,128)(2,1)}, bf16[2304,384]{1,0:T(8,128)(2,1)}) custom-call(bf16[12,512,128]{2,1,0:T(8,128)(2,1)} %get-tuple-element.158.qa_ref, bf16[2304,1536]{1,0:T(8,128)(2,1)} %get-tuple-element.151.k_ref.v_ref, bf16[2304,1536]{1,0:T(8,128)(2,1)} %get-tuple-element.151.k_ref.v_ref, ...), custom_call_target="tpu_custom_call" | custom-call | flops 512 | bytes 512 | tf_op jit(solution)/shard_map/attend_back/pallas_call | solution.py:116
  315.7 20.3 %attend_back.4 = (bf16[512,384]{1,0:T(8,128)(2,1)}, bf16[2304,384]{1,0:T(8,128)(2,1)}, bf16[2304,384]{1,0:T(8,128)(2,1)}) custom-call(bf16[12,512,128]{2,1,0:T(8,128)(2,1)} %get-tuple-element.158.qa_ref, bf16[2304,1536]{1,0:T(8,128)(2,1)} %get-tuple-element.151.k_ref.v_ref, bf16[2304,1536]{1,0:T(8,128)(2,1)} %get-tuple-element.151.k_ref.v_ref, ...), custom_call_target="tpu_custom_call" | custom-call | flops 512 | bytes 512 | tf_op jit(solution)/shard_map/attend_back/pallas_call | solution.py:116
  336.0 15.0 %rows_back.2 = (f32[1280,768]{1,0:T(8,128)}, bf16[1024,768]{1,0:T(8,128)(2,1)}) custom-call(bf16[2304,384]{1,0:T(8,128)(2,1)} %get-tuple-element.181.dk0.refs_5_, bf16[2304,384]{1,0:T(8,128)(2,1)} %get-tuple-element.182.dk1.refs_6_, bf16[2304,384]{1,0:T(8,128)(2,1)} %get-tuple-element.183.dv0.refs_7_, bf16[2304,384]{1,0:T(8,128)(2,1)} %get-tuple-element.184.dv1.refs_8_, ...), custom_call_target="tpu_custom_call" | custom-call | flops 256 | bytes 256 | tf_op jit(solution)/shard_map/rows_back/pallas_call | solution.py:499
  360.8 15.1 %products.5 = (bf16[16,576,384]{2,1,0:T(8,128)(2,1)}, bf16[16,576,384]{2,1,0:T(8,128)(2,1)}) custom-call(s32[1]{0:T(128)} %bitcast.29.refs_0_, bf16[512,768]{1,0:T(8,128)(2,1)} %get-tuple-element.149.refs_1_, bf16[512,384]{1,0:T(8,128)(2,1)} %get-tuple-element.179.dq0.refs_2_, bf16[512,384]{1,0:T(8,128)(2,1)} %get-tuple-element.180.dq1.refs_3_, ...), custom_call_target="tpu_custom_call" | custom-call | flops 2304 | bytes 2304 | tf_op jit(solution)/shard_map/products/pallas_call | solution.py:596
  385.9 15.7 %feed_forward_back.3 = (bf16[512,768]{1,0:T(8,128)(2,1)}, bf16[512,3072]{1,0:T(8,128)(2,1)}, f32[512,768]{1,0:T(8,128)}, bf16[512,768]{1,0:T(8,128)(2,1)}, bf16[512,768]{1,0:T(8,128)(2,1)}, /*index=5*/f32[1,768]{1,0:T(1,128)}) custom-call(f32[512,768]{1,0:T(8,128)} %multiply_add_fusion.g_ref, bf16[512,3072]{1,0:T(8,128)(2,1)} %get-tuple-element.189.u_ref, ...), custom_call_target="tpu_custom_call" | custom-call | flops 512 | bytes 512 | tf_op jit(solution)/shard_map/feed_forward_back/pallas_call | solution.py:441
  401.7 15.1 %products.6 = (bf16[16,576,384]{2,1,0:T(8,128)(2,1)}, bf16[16,576,384]{2,1,0:T(8,128)(2,1)}) custom-call(s32[1]{0:T(128)} %bitcast.29.refs_0_, bf16[512,3072]{1,0:T(8,128)(2,1)} %get-tuple-element.157.refs_1_, bf16[512,768]{1,0:T(8,128)(2,1)} %get-tuple-element.191.refs_2_, ...), custom_call_target="tpu_custom_call", output_to_operand_aliasing={{0}: (7, {}), {1}: (8, {})} | custom-call | flops 512 | bytes 512 | tf_op jit(solution)/shard_map/products/pallas_call | solution.py:596
  416.7 18.4 %attend_back.6 = (bf16[512,384]{1,0:T(8,128)(2,1)}, bf16[2048,384]{1,0:T(8,128)(2,1)}, bf16[2048,384]{1,0:T(8,128)(2,1)}) custom-call(bf16[12,512,128]{2,1,0:T(8,128)(2,1)} %get-tuple-element.156.qa_ref, bf16[2048,1536]{1,0:T(8,128)(2,1)} %get-tuple-element.145.k_ref.v_ref, bf16[2048,1536]{1,0:T(8,128)(2,1)} %get-tuple-element.145.k_ref.v_ref, ...), custom_call_target="tpu_custom_call" | custom-call | flops 512 | bytes 512 | tf_op jit(solution)/shard_map/attend_back/pallas_call | solution.py:116
  455.2 18.7 %attend_back.7 = (bf16[512,384]{1,0:T(8,128)(2,1)}, bf16[2048,384]{1,0:T(8,128)(2,1)}, bf16[2048,384]{1,0:T(8,128)(2,1)}) custom-call(bf16[12,512,128]{2,1,0:T(8,128)(2,1)} %get-tuple-element.156.qa_ref, bf16[2048,1536]{1,0:T(8,128)(2,1)} %get-tuple-element.145.k_ref.v_ref, bf16[2048,1536]{1,0:T(8,128)(2,1)} %get-tuple-element.145.k_ref.v_ref, ...), custom_call_target="tpu_custom_call" | custom-call | flops 512 | bytes 512 | tf_op jit(solution)/shard_map/attend_back/pallas_call | solution.py:116
  474.0 11.8 %rows_back.3 = (f32[1536,768]{1,0:T(8,128)}, bf16[1024,768]{1,0:T(8,128)(2,1)}) custom-call(bf16[2048,384]{1,0:T(8,128)(2,1)} %get-tuple-element.227.dk0.refs_5_, bf16[2048,384]{1,0:T(8,128)(2,1)} %get-tuple-element.228.dk1.refs_6_, bf16[2048,384]{1,0:T(8,128)(2,1)} %get-tuple-element.229.dv0.refs_7_, bf16[2048,384]{1,0:T(8,128)(2,1)} %get-tuple-element.230.dv1.refs_8_, ...), custom_call_target="tpu_custom_call" | custom-call | flops 512 | bytes 512 | tf_op jit(solution)/shard_map/rows_back/pallas_call | solution.py:499
  513.9 14.4 %products.7 = (bf16[16,144,384]{2,1,0:T(8,128)(2,1)}, bf16[16,144,384]{2,1,0:T(8,128)(2,1)}) custom-call(s32[1]{0:T(128)} %bitcast.29.refs_0_, bf16[512,768]{1,0:T(8,128)(2,1)} %copy-done.9, bf16[512,384]{1,0:T(8,128)(2,1)} %get-tuple-element.225.dq0.refs_2_, bf16[512,384]{1,0:T(8,128)(2,1)} %get-tuple-element.226.dq1.refs_3_, ...), custom_call_target="tpu_custom_call" | custom-call | flops 2048 | bytes 2048 | tf_op jit(solution)/shard_map/products/pallas_call | solution.py:596
  575.0 20.0 %collective-permute-done.25 = bf16[1,576,384]{2,1,0:T(8,128)(2,1)S(1)} collective-permute-done((bf16[1,576,384]{2,1,0:T(8,128)(2,1)S(1)}, bf16[1,576,384]{2,1,0:T(8,128)(2,1)S(1)}, u32[]{:S(2)}, u32[]{:S(2)}) %collective-permute-start.25) | collective-permute-done | bytes 442400 | tf_op jit(solution)/shard_map/ppermute | solution.py:199
  (381 shorter events, 248.2 us)
Async XLA Ops:
  7.2 133.4 %all-gather.5.cloned.1.call-start = ((), (), s32[]{:S(2)}) async-start(), calls=%async_computation.2 | async-start | bytes 15814656 | tf_op jit(solution)/shard_map/all_gather | solution.py:655
  14.9 219.9 %all-gather.7.cloned.1.call-start = ((), (), s32[]{:S(2)}) async-start(), calls=%async_computation.3 | async-start | bytes 12165120 | tf_op jit(solution)/shard_map/all_gather | solution.py:655
  21.4 452.6 %reduce-scatter.2.cloned.1.call-start = ((), (), s32[]{:S(2)}) async-start(), calls=%async_computation.1 | async-start | bytes 13381632 | tf_op jit(solution)/shard_map/reduce_scatter | solution.py:737
  26.7 16.5 %collective-permute-start.1 = (bf16[1,144,384]{2,1,0:T(8,128)(2,1)S(1)}, bf16[1,144,384]{2,1,0:T(8,128)(2,1)S(1)}, u32[]{:S(2)}, u32[]{:S(2)}) collective-permute-start(bf16[1,144,384]{2,1,0:T(8,128)(2,1)S(1)} %maximum_bitcast_fusion.2), channel_id=1, source_target_pairs={{0,4},{8,12},{16,20},{24,28},{1,5},{9,13},{17,21},{25,29},{2,6},{1... | collective-permute-start | bytes 331784 | tf_op jit(solution)/shard_map/ppermute | solution.py:199
  26.7 16.5 %collective-permute-start = (bf16[1,144,384]{2,1,0:T(8,128)(2,1)S(1)}, bf16[1,144,384]{2,1,0:T(8,128)(2,1)S(1)}, u32[]{:S(2)}, u32[]{:S(2)}) collective-permute-start(bf16[1,144,384]{2,1,0:T(8,128)(2,1)S(1)} %maximum_bitcast_fusion.2), channel_id=1, source_target_pairs={{0,2},{8,10},{16,18},{24,26},{1,3},{9,11},{17,19},{25,27},{2,0},{1... | collective-permute-start | bytes 331784 | tf_op jit(solution)/shard_map/ppermute | solution.py:199
  43.4 18.1 %collective-permute-start.6 = (bf16[4,144,384]{2,1,0:T(8,128)(2,1)S(1)}, bf16[4,144,384]{2,1,0:T(8,128)(2,1)S(1)}, u32[]{:S(2)}, u32[]{:S(2)}) collective-permute-start(bf16[4,144,384]{2,1,0:T(8,128)(2,1)S(1)} %maximum_bitcast_fusion), channel_id=1, source_target_pairs={{0,1},{8,9},{16,17},{24,25},{1,0},{9,8},{17,16},{25,24},{2,3},{10,... | collective-permute-start | bytes 1327112 | tf_op jit(solution)/shard_map/ppermute | solution.py:199
  46.3 29.7 %collective-permute-start.7 = (bf16[4,144,384]{2,1,0:T(8,128)(2,1)S(1)}, bf16[4,144,384]{2,1,0:T(8,128)(2,1)S(1)}, u32[]{:S(2)}, u32[]{:S(2)}) collective-permute-start(bf16[4,144,384]{2,1,0:T(8,128)(2,1)S(1)} %maximum_bitcast_fusion), channel_id=1, source_target_pairs={{0,17},{8,25},{16,1},{24,9},{1,16},{9,24},{17,0},{25,8},{2,19},{10... | collective-permute-start | bytes 1327112 | tf_op jit(solution)/shard_map/ppermute | solution.py:199
  47.5 28.5 %collective-permute-start.5 = (bf16[4,144,384]{2,1,0:T(8,128)(2,1)S(1)}, bf16[4,144,384]{2,1,0:T(8,128)(2,1)S(1)}, u32[]{:S(2)}, u32[]{:S(2)}) collective-permute-start(bf16[4,144,384]{2,1,0:T(8,128)(2,1)S(1)} %maximum_bitcast_fusion), channel_id=1, source_target_pairs={{0,16},{8,24},{16,0},{24,8},{1,17},{9,25},{17,1},{25,9},{2,18},{10... | collective-permute-start | bytes 1327112 | tf_op jit(solution)/shard_map/ppermute | solution.py:199
  48.7 39.8 %collective-permute-start.3 = (bf16[512,768]{1,0:T(8,128)(2,1)S(1)}, bf16[512,768]{1,0:T(8,128)(2,1)S(1)}, u32[]{:S(2)}, u32[]{:S(2)}) collective-permute-start(bf16[512,768]{1,0:T(8,128)(2,1)S(1)} %fusion.13.refs_1_), channel_id=1, source_target_pairs={{0,16},{8,24},{16,0},{24,8},{1,17},{9,25},{17,1},{25,9},{2,18},{10... | collective-permute-start | bytes 2359304 | tf_op jit(solution)/shard_map/ppermute | solution.py:199
  154.6 23.5 %collective-permute-start.9 = (bf16[512,768]{1,0:T(8,128)(2,1)}, bf16[512,768]{1,0:T(8,128)(2,1)S(1)}, u32[]{:S(2)}, u32[]{:S(2)}) collective-permute-start(bf16[512,768]{1,0:T(8,128)(2,1)} %get-tuple-element.149.refs_1_), channel_id=1, source_target_pairs={{0,16},{8,24},{16,0},{24,8},{1,17},{9,25},{17,1},{25,9},{2,18},{10... | collective-permute-start | bytes 2359304 | tf_op jit(solution)/shard_map/ppermute | solution.py:199
  358.8 21.3 %collective-permute-start.12 = (bf16[512,768]{1,0:T(8,128)(2,1)S(1)}, bf16[512,768]{1,0:T(8,128)(2,1)S(1)}, u32[]{:S(2)}, u32[]{:S(2)}) collective-permute-start(bf16[512,768]{1,0:T(8,128)(2,1)S(1)} %slice.263), channel_id=1, source_target_pairs={{0,16},{8,24},{16,0},{24,8},{1,17},{9,25},{17,1},{25,9},{2,18},{10... | collective-permute-start | bytes 2359304 | tf_op jit(solution)/shard_map/ppermute | solution.py:199
  416.7 18.4 %collective-permute-start.13 = (bf16[16,576,384]{2,1,0:T(8,128)(2,1)}, bf16[16,576,384]{2,1,0:T(8,128)(2,1)}, u32[]{:S(2)}, u32[]{:S(2)}) collective-permute-start(bf16[16,576,384]{2,1,0:T(8,128)(2,1)} %get-tuple-element.206), channel_id=1, source_target_pairs={{0,8},{8,0},{16,24},{24,16},{1,9},{9,1},{17,25},{25,17},{2,10},{10... | collective-permute-start | bytes 21233672 | tf_op jit(solution)/shard_map/ppermute | solution.py:199
  451.8 41.3 %collective-permute-start.16 = (bf16[4,2,288,384]{3,2,1,0:T(8,128)(2,1)}, bf16[4,2,288,384]{3,2,1,0:T(8,128)(2,1)}, u32[]{:S(2)}, u32[]{:S(2)}) collective-permute-start(bf16[4,2,288,384]{3,2,1,0:T(8,128)(2,1)} %dynamic-slice_bitcast_fusion), channel_id=1, source_target_pairs={{0,1},{8,9},{16,17},{24,25},{1,0},{9,8},{17,16},{25,24},{2,3},{10,... | collective-permute-start | bytes 5308424 | tf_op jit(solution)/shard_map/ppermute | solution.py:199
  454.7 41.0 %collective-permute-start.15 = (bf16[8,1,288,384]{3,2,0,1:T(8,128)(2,1)}, bf16[8,1,288,384]{3,2,0,1:T(8,128)(2,1)}, u32[]{:S(2)}, u32[]{:S(2)}) collective-permute-start(bf16[8,1,288,384]{3,2,0,1:T(8,128)(2,1)} %dynamic-slice_bitcast_fusion.1), channel_id=1, source_target_pairs={{0,16},{8,24},{16,0},{24,8},{1,17},{9,25},{17,1},{25,9},{2,18},{10... | collective-permute-start | bytes 5308424 | tf_op jit(solution)/shard_map/ppermute | solution.py:199
  502.5 25.8 %collective-permute-start.19 = (bf16[4,1,288,384]{3,2,0,1:T(8,128)(2,1)}, bf16[4,1,288,384]{3,2,0,1:T(8,128)(2,1)}, u32[]{:S(2)}, u32[]{:S(2)}) collective-permute-start(bf16[4,1,288,384]{3,2,0,1:T(8,128)(2,1)} %dynamic-slice_bitcast_fusion.2), channel_id=1, source_target_pairs={{0,16},{8,24},{16,0},{24,8},{1,17},{9,25},{17,1},{25,9},{2,18},{10... | collective-permute-start | bytes 2654216 | tf_op jit(solution)/shard_map/ppermute | solution.py:199
  503.7 27.3 %collective-permute-start.18 = (bf16[4,1,288,384]{3,2,0,1:T(8,128)(2,1)}, bf16[4,1,288,384]{3,2,0,1:T(8,128)(2,1)}, u32[]{:S(2)}, u32[]{:S(2)}) collective-permute-start(bf16[4,1,288,384]{3,2,0,1:T(8,128)(2,1)} %dynamic-slice_bitcast_fusion.3), channel_id=1, source_target_pairs={{0,1},{8,9},{16,17},{24,25},{1,0},{9,8},{17,16},{25,24},{2,3},{10,... | collective-permute-start | bytes 2654216 | tf_op jit(solution)/shard_map/ppermute | solution.py:199
  507.9 33.0 %collective-permute-start.17 = (bf16[512,768]{1,0:T(8,128)(2,1)}, bf16[512,768]{1,0:T(8,128)(2,1)}, u32[]{:S(2)}, u32[]{:S(2)}) collective-permute-start(bf16[512,768]{1,0:T(8,128)(2,1)} %slice.262), channel_id=1, source_target_pairs={{0,16},{8,24},{16,0},{24,8},{1,17},{9,25},{17,1},{25,9},{2,18},{10... | collective-permute-start | bytes 2359304 | tf_op jit(solution)/shard_map/ppermute | solution.py:199
  553.7 21.2 %collective-permute-start.26 = (bf16[1,576,384]{2,1,0:T(8,128)(2,1)S(1)}, bf16[1,576,384]{2,1,0:T(8,128)(2,1)S(1)}, u32[]{:S(2)}, u32[]{:S(2)}) collective-permute-start(bf16[1,576,384]{2,1,0:T(8,128)(2,1)S(1)} %get-tuple-element.340), channel_id=1, source_target_pairs={{0,6},{8,14},{16,22},{24,30},{1,7},{9,15},{17,23},{25,31},{2,4},{1... | collective-permute-start | bytes 1327112 | tf_op jit(solution)/shard_map/ppermute | solution.py:199
  556.7 38.3 %collective-permute-start.25 = (bf16[1,576,384]{2,1,0:T(8,128)(2,1)S(1)}, bf16[1,576,384]{2,1,0:T(8,128)(2,1)S(1)}, u32[]{:S(2)}, u32[]{:S(2)}) collective-permute-start(bf16[1,576,384]{2,1,0:T(8,128)(2,1)S(1)} %get-tuple-element.341), channel_id=1, source_target_pairs={{0,4},{8,12},{16,20},{24,28},{1,5},{9,13},{17,21},{25,29},{2,6},{1... | collective-permute-start | bytes 1327112 | tf_op jit(solution)/shard_map/ppermute | solution.py:199
  556.9 38.4 %collective-permute-start.21 = (bf16[4,160,384]{2,1,0:T(8,128)(2,1)S(1)}, bf16[4,160,384]{2,1,0:T(8,128)(2,1)S(1)}, u32[]{:S(2)}, u32[]{:S(2)}) collective-permute-start(bf16[4,160,384]{2,1,0:T(8,128)(2,1)S(1)} %get-tuple-element.336), channel_id=1, source_target_pairs={{0,16},{8,24},{16,0},{24,8},{1,17},{9,25},{17,1},{25,9},{2,18},{10... | collective-permute-start | bytes 1474568 | tf_op jit(solution)/shard_map/ppermute | solution.py:199
  557.7 37.6 %collective-permute-start.23 = (bf16[4,160,384]{2,1,0:T(8,128)(2,1)S(1)}, bf16[4,160,384]{2,1,0:T(8,128)(2,1)S(1)}, u32[]{:S(2)}, u32[]{:S(2)}) collective-permute-start(bf16[4,160,384]{2,1,0:T(8,128)(2,1)S(1)} %get-tuple-element.337), channel_id=1, source_target_pairs={{0,17},{8,25},{16,1},{24,9},{1,16},{9,24},{17,0},{25,8},{2,19},{10... | collective-permute-start | bytes 1474568 | tf_op jit(solution)/shard_map/ppermute | solution.py:199
  562.8 32.5 %collective-permute-start.22 = (bf16[4,160,384]{2,1,0:T(8,128)(2,1)S(1)}, bf16[4,160,384]{2,1,0:T(8,128)(2,1)S(1)}, u32[]{:S(2)}, u32[]{:S(2)}) collective-permute-start(bf16[4,160,384]{2,1,0:T(8,128)(2,1)S(1)} %get-tuple-element.338), channel_id=1, source_target_pairs={{0,1},{8,9},{16,17},{24,25},{1,0},{9,8},{17,16},{25,24},{2,3},{10,... | collective-permute-start | bytes 1474568 | tf_op jit(solution)/shard_map/ppermute | solution.py:199
  616.7 21.7 %collective-permute-start.48 = (bf16[528,384]{1,0:T(8,128)(2,1)S(1)}, bf16[528,384]{1,0:T(8,128)(2,1)S(1)}, u32[]{:S(2)}, u32[]{:S(2)}) collective-permute-start(bf16[528,384]{1,0:T(8,128)(2,1)S(1)} %bitcast.193), channel_id=1, source_target_pairs={{0,16},{8,24},{16,0},{24,8},{1,17},{9,25},{17,1},{25,9},{2,18},{10... | collective-permute-start | bytes 1216520 | tf_op jit(solution)/shard_map/ppermute | solution.py:199
  617.5 21.4 %collective-permute-start.45 = (bf16[576,384]{1,0:T(8,128)(2,1)S(1)}, bf16[576,384]{1,0:T(8,128)(2,1)S(1)}, u32[]{:S(2)}, u32[]{:S(2)}) collective-permute-start(bf16[576,384]{1,0:T(8,128)(2,1)S(1)} %bitcast.187), channel_id=1, source_target_pairs={{0,16},{8,24},{16,0},{24,8},{1,17},{9,25},{17,1},{25,9},{2,18},{10... | collective-permute-start | bytes 1327112 | tf_op jit(solution)/shard_map/ppermute | solution.py:199
  (84 other events, 718.4 us)
Sparse Core Ops, SparseCore 0:
  15.0 125.4 all-gather.4
  144.0 90.7 all-gather.6
  295.2 156.7 reduce-scatter.1

commit v5 on v4

--- a/solution.py
+++ b/solution.py
@@ -737,7 +737,82 @@
     return lax.psum_scatter(chunks.reshape((-1,) + chunks.shape[2:]), BOTH, scatter_dimension=0)
 
 
+def add_and_part_kernel(cut, own_ref, keep_ref, arrived_ref, *outs):
+    def total(index, rows):
+        return (keep_ref[index, rows].astype(jnp.float32) + arrived_ref[index, rows].astype(jnp.float32)).astype(jnp.bfloat16)
+
+    first, second = slice(0, cut), slice(cut, None)
+    y, x = own_ref[0], own_ref[1]
+    for i in range(2):
+        outs[0][i] = total(2 * i + 1 - y, first)
+        outs[1][i] = total(2 * i + y, first)
+        outs[2][i] = total(2 - 2 * x + i, second)
+        outs[3][i] = total(2 * x + i, second)
+
+
+def add_and_part(keep, arrived, cut):
+    places, rows, _ = keep.shape
+    bits = chip_bits()
+    four = pl.BlockSpec((4, rows, WIDE), lambda t, _: (t, 0, 0))
+    heights = (cut, cut, rows - cut, rows - cut)
+    spec = pltpu.PrefetchScalarGridSpec(
+        num_scalar_prefetch=1,
+        grid=(places // 4,),
+        in_specs=[four, four],
+        out_specs=[pl.BlockSpec((2, h, WIDE), lambda t, _: (t, 0, 0)) for h in heights],
+    )
+    return pl.pallas_call(
+        functools.partial(add_and_part_kernel, cut),
+        grid_spec=spec,
+        out_shape=[jax.ShapeDtypeStruct((places // 2, h, WIDE), jnp.bfloat16) for h in heights],
+        compiler_params=pltpu.CompilerParams(vmem_limit_bytes=40 << 20),
+        cost_estimate=cheap(D),
+        name="add_and_part",
+    )(jnp.stack([own_bit(bits[0]), own_bit(bits[1])]), keep, arrived)
+
+
+def add_and_halve_kernel(own_ref, keep_ref, arrived_ref, going_ref, kept_ref):
+    own = own_ref[0]
+    for ref, index in ((going_ref, 1 - own), (kept_ref, own)):
+        ref[0] = (keep_ref[index].astype(jnp.float32) + arrived_ref[index].astype(jnp.float32)).astype(jnp.bfloat16)
+
+
+def add_and_halve(keep, arrived, own):
+    places, rows, _ = keep.shape
+    pair = pl.BlockSpec((2, rows, WIDE), lambda t, _: (t, 0, 0))
+    one = pl.BlockSpec((1, rows, WIDE), lambda t, _: (t, 0, 0))
+    spec = pltpu.PrefetchScalarGridSpec(
+        num_scalar_prefetch=1, grid=(places // 2,), in_specs=[pair, pair], out_specs=[one, one]
+    )
+    return pl.pallas_call(
+        add_and_halve_kernel,
+        grid_spec=spec,
+        out_shape=[jax.ShapeDtypeStruct((places // 2, rows, WIDE), jnp.bfloat16)] * 2,
+        compiler_params=pltpu.CompilerParams(vmem_limit_bytes=40 << 20),
+        cost_estimate=cheap(D),
+        name="add_and_halve",
+    )(own.reshape(1), keep, arrived)
+
+
 def stepped_sums(send, keep, sizes, classes):
+    if classes == 2 and 1 << len(chip_bits()) == BLOCKS:
+        bits = chip_bits()
+        cut = keep.shape[1] // 2
+        parts = yield add_and_part(keep, swap(send, 1), cut)
+        ways = (bits[0], bits[1])
+        parts = yield [
+            part
+            for way, other, (going, kept) in zip(ways, ways[::-1], (parts[:2], parts[2:]))
+            for part in add_and_halve(kept, swap(going, way), own_bit(other))
+        ]
+        total = [
+            low(kept.astype(jnp.float32) + swap(going, way).astype(jnp.float32))
+            for way, (going, kept) in zip(ways[::-1], (parts[:2], parts[2:]))
+        ]
+        total = (yield [jnp.concatenate(total, axis=1)])[0]
+        for group in groups_of(bits[2:]):
+            total = (yield [share_low(total, group, 1 << len(group))])[0]
+        return total[0]
     if 1 << len(chip_bits()) != BLOCKS:
         chunks = from_blocks(jnp.stack([send, keep], axis=1), sizes)
         send, keep = chunks[:, 0], chunks[:, 1]

time: 658 us -> 652 us (level)
  other arithmetic: 64.5 us -> 44.4 us
  waiting for transfers between devices: 170 us -> 183 us
  Pallas kernels: 303 us -> 315 us
  local copies, waits for them, and re-layouts: 43 us -> 34 us
    pallas_call x0 -> x3, Pallas kernels: none -> 12.8 us  [the longest x2 6.47 us: add_and_halve(): pl.pallas_call(add_and_halve_kernel, grid_spec=spec, out_shape=[jax.Shape...]
    ppermute x50, waiting for transfers between devices: 151 us -> 163 us  [swap(): return lax.ppermute(values, ('seq', 'dp'), pairs)]
    convert_element_type x6, other arithmetic: 15.5 us -> 5.63 us  [low(): return values.astype(jnp.bfloat16)]
    reshape x3 -> x0, other arithmetic: 7.5 us -> none  [halve(): return result.reshape((-1,) + total.shape[1:])]
    unnamed x130 -> x131, local copies, waits for them, and re-layouts: 17.4 us -> 21.3 us
  transfers between devices with their start and end apart: 53 -> 53, of which waited for: 27 -> 27; matrix products, arithmetic and copies ran while one was open for 12% -> 8% of each run, Pallas kernels for 39% -> 41%
where the time goes in v5:
time: 652 us; the launch traced here: 646 us
  Pallas kernels  315 us (48%)
  waiting for transfers between devices  183 us (28%)
  starting transfers between devices  47.8 us (7%)
  other arithmetic  44.4 us (7%)
  local copies, waits for them, and re-layouts  34 us (5%)
  between operations  15.2 us (2%)
  matrix products  6.82 us (1%)
    ppermute x50, waiting for transfers between devices, swap(): return lax.ppermute(values, ('seq', 'dp'), pairs)  163 us
    pallas_call x4, Pallas kernels, attend_back(): pl.pallas_call(bwd_kernel, grid=(count,), in_specs=[pl.BlockSpec((2, rows...  77.9 us
    pallas_call x4, Pallas kernels, products(): pl.pallas_call(functools.partial(products_kernel, plan, len(arrays), outs...  61.3 us
    pallas_call x2, Pallas kernels, attend(): pl.pallas_call(fwd_kernel, grid=(pairs,), in_specs=[row, pl.BlockSpec((nk...  49.2 us
    ppermute x50, starting transfers between devices, swap(): return lax.ppermute(values, ('seq', 'dp'), pairs)  47.7 us
    pallas_call x2, Pallas kernels, feed_forward_back(): pl.pallas_call(mlp_back_kernel, grid=(4,), in_specs=[whole(full), tile, w...  30.8 us
    pallas_call x2, Pallas kernels, feed_forward(): pl.pallas_call(mlp_kernel, grid=(4,), in_specs=[whole(full), whole(full),...  28.5 us
    pallas_call x2, Pallas kernels, rows_back(): pl.pallas_call(functools.partial(rows_back_kernel, steps, half), grid=(co...  27 us
  transfers between devices with their start and end apart: 53, of which 27 were waited for; matrix products, arithmetic and copies ran while one was open for 8% of the time, Pallas kernels for 41%

profile of v5, /device:TPU:0, one launch (start us, length us, event | category | flops | bytes accessed | tf_op | source)
XLA Modules:
  0.0 646.2 jit_solution(12031216855198649400)
XLA Ops:
  32.0 11.2 %collective-permute-done.1 = bf16[1,144,384]{2,1,0:T(8,128)(2,1)S(1)} collective-permute-done((bf16[1,144,384]{2,1,0:T(8,128)(2,1)S(1)}, bf16[1,144,384]{2,1,0:T(8,128)(2,1)S(1)}, u32[]{:S(2)}, u32[]{:S(2)}) %collective-permute-start.1) | collective-permute-done | bytes 110624 | tf_op jit(solution)/shard_map/ppermute | solution.py:199
  50.4 11.0 %collective-permute-done.6 = bf16[4,144,384]{2,1,0:T(8,128)(2,1)S(1)} collective-permute-done((bf16[4,144,384]{2,1,0:T(8,128)(2,1)S(1)}, bf16[4,144,384]{2,1,0:T(8,128)(2,1)S(1)}, u32[]{:S(2)}, u32[]{:S(2)}) %collective-permute-start.6) | collective-permute-done | bytes 442400 | tf_op jit(solution)/shard_map/ppermute | solution.py:199
  61.4 14.5 %collective-permute-done.7 = bf16[4,144,384]{2,1,0:T(8,128)(2,1)S(1)} collective-permute-done((bf16[4,144,384]{2,1,0:T(8,128)(2,1)S(1)}, bf16[4,144,384]{2,1,0:T(8,128)(2,1)S(1)}, u32[]{:S(2)}, u32[]{:S(2)}) %collective-permute-start.7) | collective-permute-done | bytes 442400 | tf_op jit(solution)/shard_map/ppermute | solution.py:199
  109.1 23.2 %attend.2 = (f32[512,768]{1,0:T(8,128)}, bf16[512,768]{1,0:T(8,128)(2,1)}, bf16[12,512,128]{2,1,0:T(8,128)(2,1)}) custom-call(bf16[512,768]{1,0:T(8,128)(2,1)} %get-tuple-element.154.q_ref, bf16[2048,1536]{1,0:T(8,128)(2,1)} %get-tuple-element.155.k_ref.v_ref, bf16[2048,1536]{1,0:T(8,128)(2,1)} %get-tuple-element.155.k_ref.v_ref, ...), custom_call_target="tpu_custom_call" | custom-call | flops 512 | bytes 512 | tf_op jit(solution)/shard_map/attend/pallas_call | solution.py:54
  140.6 14.0 %feed_forward.2 = (f32[512,768]{1,0:T(8,128)}, bf16[512,768]{1,0:T(8,128)(2,1)}, bf16[512,3072]{1,0:T(8,128)(2,1)}, bf16[512,3072]{1,0:T(8,128)(2,1)}, f32[512,768]{1,0:T(8,128)}, /*index=5*/bf16[512,768]{1,0:T(8,128)(2,1)}) custom-call(bf16[512,768]{1,0:T(8,128)(2,1)} %bitcast.179, bf16[512,768]{1,0:T(8,128)(2,1)} %get-tuple-element.157.o_ref.refs_5_, ...), custom_call_target="tpu_custom_call" | custom-call | flops 512 | bytes 512 | tf_op jit(solution)/shard_map/feed_forward/pallas_call | solution.py:383
  156.1 21.9 %collective-permute-done.9 = bf16[512,768]{1,0:T(8,128)(2,1)S(1)} collective-permute-done((bf16[512,768]{1,0:T(8,128)(2,1)}, bf16[512,768]{1,0:T(8,128)(2,1)S(1)}, u32[]{:S(2)}, u32[]{:S(2)}) %collective-permute-start.9) | collective-permute-done | bytes 786464 | tf_op jit(solution)/shard_map/ppermute | solution.py:199
  184.8 12.1 %project.3 = (bf16[2304,1536]{1,0:T(8,128)(2,1)}, bf16[512,768]{1,0:T(8,128)(2,1)}) custom-call(bf16[2304,768]{1,0:T(8,128)(2,1)} %fusion.1.rows_ref.refs_4_, bf16[16,2,624,384]{3,2,1,0:T(8,128)(2,1)} %bitcast.164), custom_call_target="tpu_custom_call" | custom-call | flops 512 | bytes 512 | tf_op jit(solution)/shard_map/project/pallas_call | solution.py:318
  196.9 26.0 %attend.3 = (f32[512,768]{1,0:T(8,128)}, bf16[512,768]{1,0:T(8,128)(2,1)}, bf16[12,512,128]{2,1,0:T(8,128)(2,1)}) custom-call(bf16[512,768]{1,0:T(8,128)(2,1)} %get-tuple-element.160.q_ref, bf16[2304,1536]{1,0:T(8,128)(2,1)} %get-tuple-element.161.k_ref.v_ref, bf16[2304,1536]{1,0:T(8,128)(2,1)} %get-tuple-element.161.k_ref.v_ref, ...), custom_call_target="tpu_custom_call" | custom-call | flops 512 | bytes 512 | tf_op jit(solution)/shard_map/attend/pallas_call | solution.py:54
  222.9 11.9 %all-gather.7.cloned.1.call-done = bf16[15360,384]{1,0:T(8,128)(2,1)} async-done(((bf16[480,384]{1,0:T(8,128)(2,1)}), bf16[15360,384]{1,0:T(8,128)(2,1)}) %all-gather.7.cloned.1.call-update) | async-done | bytes 11796496 | tf_op jit(solution)/shard_map/all_gather | solution.py:655
  237.8 14.5 %feed_forward.3 = (f32[512,768]{1,0:T(8,128)}, bf16[512,768]{1,0:T(8,128)(2,1)}, bf16[512,3072]{1,0:T(8,128)(2,1)}, bf16[512,3072]{1,0:T(8,128)(2,1)}, f32[512,768]{1,0:T(8,128)}, /*index=5*/bf16[512,768]{1,0:T(8,128)(2,1)}) custom-call(f32[512,768]{1,0:T(8,128)} %get-tuple-element.158.h_ref, bf16[512,768]{1,0:T(8,128)(2,1)} %get-tuple-element.163.o_ref.refs_4_, ...), custom_call_target="tpu_custom_call" | custom-call | flops 512 | bytes 512 | tf_op jit(solution)/shard_map/feed_forward/pallas_call | solution.py:383
  263.2 15.3 %feed_forward_back.2 = (bf16[512,768]{1,0:T(8,128)(2,1)}, bf16[512,3072]{1,0:T(8,128)(2,1)}, f32[512,768]{1,0:T(8,128)}, bf16[512,768]{1,0:T(8,128)(2,1)}, bf16[512,768]{1,0:T(8,128)(2,1)}, /*index=5*/f32[1,768]{1,0:T(1,128)}) custom-call(f32[512,768]{1,0:T(8,128)} %broadcast_add_fusion.g_ref, bf16[512,3072]{1,0:T(8,128)(2,1)} %get-tuple-element.171.u_ref, ...), custom_call_target="tpu_custom_call" | custom-call | flops 512 | bytes 512 | tf_op jit(solution)/shard_map/feed_forward_back/pallas_call | solution.py:441
  278.5 17.0 %products.4 = bf16[16,2,528,384]{3,2,1,0:T(8,128)(2,1)} custom-call(bf16[512,3072]{1,0:T(8,128)(2,1)} %get-tuple-element.169.refs_0_, bf16[512,768]{1,0:T(8,128)(2,1)} %get-tuple-element.173.refs_1_, bf16[512,768]{1,0:T(8,128)(2,1)} %get-tuple-element.174.refs_2_, bf16[512,3072]{1,0:T(8,128)(2,1)} %get-tuple-element.175.refs_3_, ...), custom_call_target="tpu_custom_call" | custom-call | flops 512 | bytes 512 | tf_op jit(solution)/shard_map/products/pallas_call | solution.py:596
  295.6 20.7 %attend_back.5 = (bf16[512,384]{1,0:T(8,128)(2,1)}, bf16[2304,384]{1,0:T(8,128)(2,1)}, bf16[2304,384]{1,0:T(8,128)(2,1)}) custom-call(bf16[12,512,128]{2,1,0:T(8,128)(2,1)} %get-tuple-element.168.qa_ref, bf16[2304,1536]{1,0:T(8,128)(2,1)} %get-tuple-element.161.k_ref.v_ref, bf16[2304,1536]{1,0:T(8,128)(2,1)} %get-tuple-element.161.k_ref.v_ref, ...), custom_call_target="tpu_custom_call" | custom-call | flops 512 | bytes 512 | tf_op jit(solution)/shard_map/attend_back/pallas_call | solution.py:116
  316.3 20.3 %attend_back.4 = (bf16[512,384]{1,0:T(8,128)(2,1)}, bf16[2304,384]{1,0:T(8,128)(2,1)}, bf16[2304,384]{1,0:T(8,128)(2,1)}) custom-call(bf16[12,512,128]{2,1,0:T(8,128)(2,1)} %get-tuple-element.168.qa_ref, bf16[2304,1536]{1,0:T(8,128)(2,1)} %get-tuple-element.161.k_ref.v_ref, bf16[2304,1536]{1,0:T(8,128)(2,1)} %get-tuple-element.161.k_ref.v_ref, ...), custom_call_target="tpu_custom_call" | custom-call | flops 512 | bytes 512 | tf_op jit(solution)/shard_map/attend_back/pallas_call | solution.py:116
  336.6 15.0 %rows_back.2 = (f32[1280,768]{1,0:T(8,128)}, bf16[1024,768]{1,0:T(8,128)(2,1)}) custom-call(bf16[2304,384]{1,0:T(8,128)(2,1)} %get-tuple-element.191.dk0.refs_5_, bf16[2304,384]{1,0:T(8,128)(2,1)} %get-tuple-element.192.dk1.refs_6_, bf16[2304,384]{1,0:T(8,128)(2,1)} %get-tuple-element.193.dv0.refs_7_, bf16[2304,384]{1,0:T(8,128)(2,1)} %get-tuple-element.194.dv1.refs_8_, ...), custom_call_target="tpu_custom_call" | custom-call | flops 256 | bytes 256 | tf_op jit(solution)/shard_map/rows_back/pallas_call | solution.py:499
  361.4 15.0 %products.5 = (bf16[16,576,384]{2,1,0:T(8,128)(2,1)}, bf16[16,576,384]{2,1,0:T(8,128)(2,1)}) custom-call(s32[1]{0:T(128)} %bitcast.29.refs_0_, bf16[512,768]{1,0:T(8,128)(2,1)} %get-tuple-element.159.refs_1_, bf16[512,384]{1,0:T(8,128)(2,1)} %get-tuple-element.189.dq0.refs_2_, bf16[512,384]{1,0:T(8,128)(2,1)} %get-tuple-element.190.dq1.refs_3_, ...), custom_call_target="tpu_custom_call" | custom-call | flops 2304 | bytes 2304 | tf_op jit(solution)/shard_map/products/pallas_call | solution.py:596
  386.4 15.5 %feed_forward_back.3 = (bf16[512,768]{1,0:T(8,128)(2,1)}, bf16[512,3072]{1,0:T(8,128)(2,1)}, f32[512,768]{1,0:T(8,128)}, bf16[512,768]{1,0:T(8,128)(2,1)}, bf16[512,768]{1,0:T(8,128)(2,1)}, /*index=5*/f32[1,768]{1,0:T(1,128)}) custom-call(f32[512,768]{1,0:T(8,128)} %multiply_add_fusion.g_ref, bf16[512,3072]{1,0:T(8,128)(2,1)} %get-tuple-element.199.u_ref, ...), custom_call_target="tpu_custom_call" | custom-call | flops 512 | bytes 512 | tf_op jit(solution)/shard_map/feed_forward_back/pallas_call | solution.py:441
  401.9 15.0 %products.6 = (bf16[16,576,384]{2,1,0:T(8,128)(2,1)}, bf16[16,576,384]{2,1,0:T(8,128)(2,1)}) custom-call(s32[1]{0:T(128)} %bitcast.29.refs_0_, bf16[512,3072]{1,0:T(8,128)(2,1)} %get-tuple-element.167.refs_1_, bf16[512,768]{1,0:T(8,128)(2,1)} %get-tuple-element.201.refs_2_, ...), custom_call_target="tpu_custom_call", output_to_operand_aliasing={{0}: (7, {}), {1}: (8, {})} | custom-call | flops 512 | bytes 512 | tf_op jit(solution)/shard_map/products/pallas_call | solution.py:596
  417.0 18.6 %attend_back.6 = (bf16[512,384]{1,0:T(8,128)(2,1)}, bf16[2048,384]{1,0:T(8,128)(2,1)}, bf16[2048,384]{1,0:T(8,128)(2,1)}) custom-call(bf16[12,512,128]{2,1,0:T(8,128)(2,1)} %get-tuple-element.166.qa_ref, bf16[2048,1536]{1,0:T(8,128)(2,1)} %get-tuple-element.155.k_ref.v_ref, bf16[2048,1536]{1,0:T(8,128)(2,1)} %get-tuple-element.155.k_ref.v_ref, ...), custom_call_target="tpu_custom_call" | custom-call | flops 512 | bytes 512 | tf_op jit(solution)/shard_map/attend_back/pallas_call | solution.py:116
  446.9 18.3 %attend_back.7 = (bf16[512,384]{1,0:T(8,128)(2,1)}, bf16[2048,384]{1,0:T(8,128)(2,1)}, bf16[2048,384]{1,0:T(8,128)(2,1)}) custom-call(bf16[12,512,128]{2,1,0:T(8,128)(2,1)} %get-tuple-element.166.qa_ref, bf16[2048,1536]{1,0:T(8,128)(2,1)} %get-tuple-element.155.k_ref.v_ref, bf16[2048,1536]{1,0:T(8,128)(2,1)} %get-tuple-element.155.k_ref.v_ref, ...), custom_call_target="tpu_custom_call" | custom-call | flops 512 | bytes 512 | tf_op jit(solution)/shard_map/attend_back/pallas_call | solution.py:116
  465.2 12.0 %rows_back.3 = (f32[1536,768]{1,0:T(8,128)}, bf16[1024,768]{1,0:T(8,128)(2,1)}) custom-call(bf16[2048,384]{1,0:T(8,128)(2,1)} %get-tuple-element.247.dk0.refs_5_, bf16[2048,384]{1,0:T(8,128)(2,1)} %get-tuple-element.248.dk1.refs_6_, bf16[2048,384]{1,0:T(8,128)(2,1)} %get-tuple-element.249.dv0.refs_7_, bf16[2048,384]{1,0:T(8,128)(2,1)} %get-tuple-element.250.dv1.refs_8_, ...), custom_call_target="tpu_custom_call" | custom-call | flops 512 | bytes 512 | tf_op jit(solution)/shard_map/rows_back/pallas_call | solution.py:499
  504.6 14.2 %products.7 = (bf16[16,144,384]{2,1,0:T(8,128)(2,1)}, bf16[16,144,384]{2,1,0:T(8,128)(2,1)}) custom-call(s32[1]{0:T(128)} %bitcast.29.refs_0_, bf16[512,768]{1,0:T(8,128)(2,1)} %copy-done.11, bf16[512,384]{1,0:T(8,128)(2,1)} %get-tuple-element.245.dq0.refs_2_, bf16[512,384]{1,0:T(8,128)(2,1)} %get-tuple-element.246.dq1.refs_3_, ...), custom_call_target="tpu_custom_call" | custom-call | flops 2048 | bytes 2048 | tf_op jit(solution)/shard_map/products/pallas_call | solution.py:596
  524.5 12.3 %collective-permute-done.17 = bf16[512,768]{1,0:T(8,128)(2,1)S(1)} collective-permute-done((bf16[512,768]{1,0:T(8,128)(2,1)}, bf16[512,768]{1,0:T(8,128)(2,1)S(1)}, u32[]{:S(2)}, u32[]{:S(2)}) %collective-permute-start.17) | collective-permute-done | bytes 786464 | tf_op jit(solution)/shard_map/ppermute | solution.py:199
  570.3 19.0 %collective-permute-done.25 = bf16[1,576,384]{2,1,0:T(8,128)(2,1)S(1)} collective-permute-done((bf16[1,576,384]{2,1,0:T(8,128)(2,1)S(1)}, bf16[1,576,384]{2,1,0:T(8,128)(2,1)S(1)}, u32[]{:S(2)}, u32[]{:S(2)}) %collective-permute-start.25) | collective-permute-done | bytes 442400 | tf_op jit(solution)/shard_map/ppermute | solution.py:199
  (377 shorter events, 242.3 us)
Async XLA Ops:
  7.2 133.4 %all-gather.5.cloned.1.call-start = ((), (), s32[]{:S(2)}) async-start(), calls=%async_computation.2 | async-start | bytes 15814656 | tf_op jit(solution)/shard_map/all_gather | solution.py:655
  14.9 219.9 %all-gather.7.cloned.1.call-start = ((), (), s32[]{:S(2)}) async-start(), calls=%async_computation.3 | async-start | bytes 12165120 | tf_op jit(solution)/shard_map/all_gather | solution.py:655
  21.4 443.9 %reduce-scatter.2.cloned.1.call-start = ((), (), s32[]{:S(2)}) async-start(), calls=%async_computation.1 | async-start | bytes 13381632 | tf_op jit(solution)/shard_map/reduce_scatter | solution.py:737
  26.7 16.5 %collective-permute-start.1 = (bf16[1,144,384]{2,1,0:T(8,128)(2,1)S(1)}, bf16[1,144,384]{2,1,0:T(8,128)(2,1)S(1)}, u32[]{:S(2)}, u32[]{:S(2)}) collective-permute-start(bf16[1,144,384]{2,1,0:T(8,128)(2,1)S(1)} %maximum_bitcast_fusion.2), channel_id=1, source_target_pairs={{0,4},{8,12},{16,20},{24,28},{1,5},{9,13},{17,21},{25,29},{2,6},{1... | collective-permute-start | bytes 331784 | tf_op jit(solution)/shard_map/ppermute | solution.py:199
  26.7 16.5 %collective-permute-start = (bf16[1,144,384]{2,1,0:T(8,128)(2,1)S(1)}, bf16[1,144,384]{2,1,0:T(8,128)(2,1)S(1)}, u32[]{:S(2)}, u32[]{:S(2)}) collective-permute-start(bf16[1,144,384]{2,1,0:T(8,128)(2,1)S(1)} %maximum_bitcast_fusion.2), channel_id=1, source_target_pairs={{0,2},{8,10},{16,18},{24,26},{1,3},{9,11},{17,19},{25,27},{2,0},{1... | collective-permute-start | bytes 331784 | tf_op jit(solution)/shard_map/ppermute | solution.py:199
  43.4 18.1 %collective-permute-start.6 = (bf16[4,144,384]{2,1,0:T(8,128)(2,1)S(1)}, bf16[4,144,384]{2,1,0:T(8,128)(2,1)S(1)}, u32[]{:S(2)}, u32[]{:S(2)}) collective-permute-start(bf16[4,144,384]{2,1,0:T(8,128)(2,1)S(1)} %maximum_bitcast_fusion), channel_id=1, source_target_pairs={{0,1},{8,9},{16,17},{24,25},{1,0},{9,8},{17,16},{25,24},{2,3},{10,... | collective-permute-start | bytes 1327112 | tf_op jit(solution)/shard_map/ppermute | solution.py:199
  46.3 29.7 %collective-permute-start.7 = (bf16[4,144,384]{2,1,0:T(8,128)(2,1)S(1)}, bf16[4,144,384]{2,1,0:T(8,128)(2,1)S(1)}, u32[]{:S(2)}, u32[]{:S(2)}) collective-permute-start(bf16[4,144,384]{2,1,0:T(8,128)(2,1)S(1)} %maximum_bitcast_fusion), channel_id=1, source_target_pairs={{0,17},{8,25},{16,1},{24,9},{1,16},{9,24},{17,0},{25,8},{2,19},{10... | collective-permute-start | bytes 1327112 | tf_op jit(solution)/shard_map/ppermute | solution.py:199
  47.4 28.5 %collective-permute-start.5 = (bf16[4,144,384]{2,1,0:T(8,128)(2,1)S(1)}, bf16[4,144,384]{2,1,0:T(8,128)(2,1)S(1)}, u32[]{:S(2)}, u32[]{:S(2)}) collective-permute-start(bf16[4,144,384]{2,1,0:T(8,128)(2,1)S(1)} %maximum_bitcast_fusion), channel_id=1, source_target_pairs={{0,16},{8,24},{16,0},{24,8},{1,17},{9,25},{17,1},{25,9},{2,18},{10... | collective-permute-start | bytes 1327112 | tf_op jit(solution)/shard_map/ppermute | solution.py:199
  48.7 39.8 %collective-permute-start.3 = (bf16[512,768]{1,0:T(8,128)(2,1)S(1)}, bf16[512,768]{1,0:T(8,128)(2,1)S(1)}, u32[]{:S(2)}, u32[]{:S(2)}) collective-permute-start(bf16[512,768]{1,0:T(8,128)(2,1)S(1)} %fusion.8.refs_1_), channel_id=1, source_target_pairs={{0,16},{8,24},{16,0},{24,8},{1,17},{9,25},{17,1},{25,9},{2,18},{10... | collective-permute-start | bytes 2359304 | tf_op jit(solution)/shard_map/ppermute | solution.py:199
  154.6 23.4 %collective-permute-start.9 = (bf16[512,768]{1,0:T(8,128)(2,1)}, bf16[512,768]{1,0:T(8,128)(2,1)S(1)}, u32[]{:S(2)}, u32[]{:S(2)}) collective-permute-start(bf16[512,768]{1,0:T(8,128)(2,1)} %get-tuple-element.159.refs_1_), channel_id=1, source_target_pairs={{0,16},{8,24},{16,0},{24,8},{1,17},{9,25},{17,1},{25,9},{2,18},{10... | collective-permute-start | bytes 2359304 | tf_op jit(solution)/shard_map/ppermute | solution.py:199
  359.4 21.2 %collective-permute-start.12 = (bf16[512,768]{1,0:T(8,128)(2,1)S(1)}, bf16[512,768]{1,0:T(8,128)(2,1)S(1)}, u32[]{:S(2)}, u32[]{:S(2)}) collective-permute-start(bf16[512,768]{1,0:T(8,128)(2,1)S(1)} %slice.253), channel_id=1, source_target_pairs={{0,16},{8,24},{16,0},{24,8},{1,17},{9,25},{17,1},{25,9},{2,18},{10... | collective-permute-start | bytes 2359304 | tf_op jit(solution)/shard_map/ppermute | solution.py:199
  416.9 18.7 %collective-permute-start.13 = (bf16[16,576,384]{2,1,0:T(8,128)(2,1)}, bf16[16,576,384]{2,1,0:T(8,128)(2,1)}, u32[]{:S(2)}, u32[]{:S(2)}) collective-permute-start(bf16[16,576,384]{2,1,0:T(8,128)(2,1)} %get-tuple-element.216), channel_id=1, source_target_pairs={{0,8},{8,0},{16,24},{24,16},{1,9},{9,1},{17,25},{25,17},{2,10},{10... | collective-permute-start | bytes 21233672 | tf_op jit(solution)/shard_map/ppermute | solution.py:199
  445.3 41.3 %collective-permute-start.15 = (bf16[8,288,384]{2,1,0:T(8,128)(2,1)}, bf16[8,288,384]{2,1,0:T(8,128)(2,1)}, u32[]{:S(2)}, u32[]{:S(2)}) collective-permute-start(bf16[8,288,384]{2,1,0:T(8,128)(2,1)} %get-tuple-element.238), channel_id=1, source_target_pairs={{0,16},{8,24},{16,0},{24,8},{1,17},{9,25},{17,1},{25,9},{2,18},{10... | collective-permute-start | bytes 5308424 | tf_op jit(solution)/shard_map/ppermute | solution.py:199
  445.3 45.1 %collective-permute-start.16 = (bf16[8,288,384]{2,1,0:T(8,128)(2,1)}, bf16[8,288,384]{2,1,0:T(8,128)(2,1)}, u32[]{:S(2)}, u32[]{:S(2)}) collective-permute-start(bf16[8,288,384]{2,1,0:T(8,128)(2,1)} %get-tuple-element.242), channel_id=1, source_target_pairs={{0,1},{8,9},{16,17},{24,25},{1,0},{9,8},{17,16},{25,24},{2,3},{10,... | collective-permute-start | bytes 5308424 | tf_op jit(solution)/shard_map/ppermute | solution.py:199
  496.0 22.9 %collective-permute-start.18 = (bf16[4,288,384]{2,1,0:T(8,128)(2,1)}, bf16[4,288,384]{2,1,0:T(8,128)(2,1)}, u32[]{:S(2)}, u32[]{:S(2)}) collective-permute-start(bf16[4,288,384]{2,1,0:T(8,128)(2,1)} %get-tuple-element.255), channel_id=1, source_target_pairs={{0,1},{8,9},{16,17},{24,25},{1,0},{9,8},{17,16},{25,24},{2,3},{10,... | collective-permute-start | bytes 2654216 | tf_op jit(solution)/shard_map/ppermute | solution.py:199
  498.9 22.8 %collective-permute-start.19 = (bf16[4,288,384]{2,1,0:T(8,128)(2,1)S(1)}, bf16[4,288,384]{2,1,0:T(8,128)(2,1)}, u32[]{:S(2)}, u32[]{:S(2)}) collective-permute-start(bf16[4,288,384]{2,1,0:T(8,128)(2,1)S(1)} %get-tuple-element.257), channel_id=1, source_target_pairs={{0,16},{8,24},{16,0},{24,8},{1,17},{9,25},{17,1},{25,9},{2,18},{10... | collective-permute-start | bytes 2654216 | tf_op jit(solution)/shard_map/ppermute | solution.py:199
  501.3 35.5 %collective-permute-start.17 = (bf16[512,768]{1,0:T(8,128)(2,1)}, bf16[512,768]{1,0:T(8,128)(2,1)S(1)}, u32[]{:S(2)}, u32[]{:S(2)}) collective-permute-start(bf16[512,768]{1,0:T(8,128)(2,1)} %slice.252), channel_id=1, source_target_pairs={{0,16},{8,24},{16,0},{24,8},{1,17},{9,25},{17,1},{25,9},{2,18},{10... | collective-permute-start | bytes 2359304 | tf_op jit(solution)/shard_map/ppermute | solution.py:199
  548.0 22.3 %collective-permute-start.26 = (bf16[1,576,384]{2,1,0:T(8,128)(2,1)S(1)}, bf16[1,576,384]{2,1,0:T(8,128)(2,1)S(1)}, u32[]{:S(2)}, u32[]{:S(2)}) collective-permute-start(bf16[1,576,384]{2,1,0:T(8,128)(2,1)S(1)} %get-tuple-element.358), channel_id=1, source_target_pairs={{0,6},{8,14},{16,22},{24,30},{1,7},{9,15},{17,23},{25,31},{2,4},{1... | collective-permute-start | bytes 1327112 | tf_op jit(solution)/shard_map/ppermute | solution.py:199
  551.2 38.1 %collective-permute-start.25 = (bf16[1,576,384]{2,1,0:T(8,128)(2,1)S(1)}, bf16[1,576,384]{2,1,0:T(8,128)(2,1)S(1)}, u32[]{:S(2)}, u32[]{:S(2)}) collective-permute-start(bf16[1,576,384]{2,1,0:T(8,128)(2,1)S(1)} %get-tuple-element.359), channel_id=1, source_target_pairs={{0,4},{8,12},{16,20},{24,28},{1,5},{9,13},{17,21},{25,29},{2,6},{1... | collective-permute-start | bytes 1327112 | tf_op jit(solution)/shard_map/ppermute | solution.py:199
  551.4 38.1 %collective-permute-start.21 = (bf16[4,160,384]{2,1,0:T(8,128)(2,1)S(1)}, bf16[4,160,384]{2,1,0:T(8,128)(2,1)S(1)}, u32[]{:S(2)}, u32[]{:S(2)}) collective-permute-start(bf16[4,160,384]{2,1,0:T(8,128)(2,1)S(1)} %get-tuple-element.354), channel_id=1, source_target_pairs={{0,16},{8,24},{16,0},{24,8},{1,17},{9,25},{17,1},{25,9},{2,18},{10... | collective-permute-start | bytes 1474568 | tf_op jit(solution)/shard_map/ppermute | solution.py:199
  552.4 37.1 %collective-permute-start.23 = (bf16[4,160,384]{2,1,0:T(8,128)(2,1)S(1)}, bf16[4,160,384]{2,1,0:T(8,128)(2,1)S(1)}, u32[]{:S(2)}, u32[]{:S(2)}) collective-permute-start(bf16[4,160,384]{2,1,0:T(8,128)(2,1)S(1)} %get-tuple-element.355), channel_id=1, source_target_pairs={{0,17},{8,25},{16,1},{24,9},{1,16},{9,24},{17,0},{25,8},{2,19},{10... | collective-permute-start | bytes 1474568 | tf_op jit(solution)/shard_map/ppermute | solution.py:199
  558.2 31.3 %collective-permute-start.22 = (bf16[4,160,384]{2,1,0:T(8,128)(2,1)S(1)}, bf16[4,160,384]{2,1,0:T(8,128)(2,1)S(1)}, u32[]{:S(2)}, u32[]{:S(2)}) collective-permute-start(bf16[4,160,384]{2,1,0:T(8,128)(2,1)S(1)} %get-tuple-element.356), channel_id=1, source_target_pairs={{0,1},{8,9},{16,17},{24,25},{1,0},{9,8},{17,16},{25,24},{2,3},{10,... | collective-permute-start | bytes 1474568 | tf_op jit(solution)/shard_map/ppermute | solution.py:199
  611.0 21.7 %collective-permute-start.48 = (bf16[528,384]{1,0:T(8,128)(2,1)S(1)}, bf16[528,384]{1,0:T(8,128)(2,1)S(1)}, u32[]{:S(2)}, u32[]{:S(2)}) collective-permute-start(bf16[528,384]{1,0:T(8,128)(2,1)S(1)} %bitcast.158), channel_id=1, source_target_pairs={{0,16},{8,24},{16,0},{24,8},{1,17},{9,25},{17,1},{25,9},{2,18},{10... | collective-permute-start | bytes 1216520 | tf_op jit(solution)/shard_map/ppermute | solution.py:199
  611.9 21.2 %collective-permute-start.45 = (bf16[576,384]{1,0:T(8,128)(2,1)S(1)}, bf16[576,384]{1,0:T(8,128)(2,1)S(1)}, u32[]{:S(2)}, u32[]{:S(2)}) collective-permute-start(bf16[576,384]{1,0:T(8,128)(2,1)S(1)} %bitcast.152), channel_id=1, source_target_pairs={{0,16},{8,24},{16,0},{24,8},{1,17},{9,25},{17,1},{25,9},{2,18},{10... | collective-permute-start | bytes 1327112 | tf_op jit(solution)/shard_map/ppermute | solution.py:199
  (85 other events, 653.8 us)
Sparse Core Ops, SparseCore 0:
  15.0 125.4 all-gather.4
  144.0 90.7 all-gather.6
  295.7 156.4 reduce-scatter.1

commit v6 on v5

--- a/solution.py
+++ b/solution.py
@@ -716,7 +716,7 @@
         functools.partial(collect_kernel, plan),
         grid_spec=spec,
         out_shape=[jax.ShapeDtypeStruct(shape, jnp.float32) for shape in shapes.values()],
-        compiler_params=pltpu.CompilerParams(vmem_limit_bytes=40 << 20),
+        compiler_params=pltpu.CompilerParams(vmem_limit_bytes=60 << 20),
         cost_estimate=cheap(D),
         name="collect",
     )(lax.axis_index("seq").reshape(1), *pieces)
@@ -1052,8 +1052,12 @@
     (out_enc_qkv,), shares = collect(enc_proj.finish(), qkv, [0, 0, 0])
     shared = across([t[-(per_block * BLOCKS >> len(chip_bits())) :] for t in shares]).astype(jnp.float32)
     late = late.finish()
-    out_dec, _ = collect(dec_sum, [tall, wide, square, square, square], range(5))
-    out_enc, _ = collect(enc_sum.finish(), [tall, wide, square] + qkv, [0, 1, 2, 3, 3, 3])
+    outs, _ = collect(
+        jnp.concatenate([dec_sum, enc_sum.finish()], axis=0),
+        [tall, wide, square, square, square, tall, wide, square] + qkv,
+        [0, 1, 2, 3, 4, 5, 6, 7, 8, 8, 8],
+    )
+    out_dec, out_enc = outs[:5], outs[5:]
     out_dec_qkv = out_enc[3]
     gain_sums = jnp.concatenate([late, shared[class_count : class_count + 3]], axis=0)
     return (

time: 652 us -> 660 us (1.012)
    ppermute x50 -> x47, waiting for transfers between devices: 163 us -> 168 us  [swap(): return lax.ppermute(values, ('seq', 'dp'), pairs)]
    ppermute x50 -> x47, starting transfers between devices: 47.7 us -> 44.8 us  [swap(): return lax.ppermute(values, ('seq', 'dp'), pairs)]
    unnamed x131 -> x147, local copies, waits for them, and re-layouts: 21.3 us -> 23.2 us
  transfers between devices with their start and end apart: 53 -> 50, of which waited for: 27 -> 28; matrix products, arithmetic and copies ran while one was open for 8% -> 8% of each run, Pallas kernels for 41% -> 41%
where the time goes in v6:
time: 660 us; the launch traced here: 654 us
  Pallas kernels  317 us (48%)
  waiting for transfers between devices  188 us (28%)
  other arithmetic  45.5 us (7%)
  starting transfers between devices  44.9 us (7%)
  local copies, waits for them, and re-layouts  35.8 us (5%)
  between operations  15.3 us (2%)
  matrix products  6.83 us (1%)
    ppermute x47, waiting for transfers between devices, swap(): return lax.ppermute(values, ('seq', 'dp'), pairs)  168 us
    pallas_call x4, Pallas kernels, attend_back(): pl.pallas_call(bwd_kernel, grid=(count,), in_specs=[pl.BlockSpec((2, rows...  77.9 us
    pallas_call x4, Pallas kernels, products(): pl.pallas_call(functools.partial(products_kernel, plan, len(arrays), outs...  61.4 us
    pallas_call x2, Pallas kernels, attend(): pl.pallas_call(fwd_kernel, grid=(pairs,), in_specs=[row, pl.BlockSpec((nk...  49.2 us
    ppermute x47, starting transfers between devices, swap(): return lax.ppermute(values, ('seq', 'dp'), pairs)  44.8 us
    pallas_call x2, Pallas kernels, feed_forward_back(): pl.pallas_call(mlp_back_kernel, grid=(4,), in_specs=[whole(full), tile, w...  30.8 us
    pallas_call x2, Pallas kernels, feed_forward(): pl.pallas_call(mlp_kernel, grid=(4,), in_specs=[whole(full), whole(full),...  28.5 us
    pallas_call x2, Pallas kernels, rows_back(): pl.pallas_call(functools.partial(rows_back_kernel, steps, half), grid=(co...  26.9 us
  transfers between devices with their start and end apart: 50, of which 28 were waited for; matrix products, arithmetic and copies ran while one was open for 8% of the time, Pallas kernels for 41%

profile of v6, /device:TPU:0, one launch (start us, length us, event | category | flops | bytes accessed | tf_op | source)
XLA Modules:
  0.0 653.9 jit_solution(12042177871325945465)
XLA Ops:
  32.0 11.2 %collective-permute-done.1 = bf16[1,144,384]{2,1,0:T(8,128)(2,1)S(1)} collective-permute-done((bf16[1,144,384]{2,1,0:T(8,128)(2,1)S(1)}, bf16[1,144,384]{2,1,0:T(8,128)(2,1)S(1)}, u32[]{:S(2)}, u32[]{:S(2)}) %collective-permute-start.1) | collective-permute-done | bytes 110624 | tf_op jit(solution)/shard_map/ppermute | solution.py:199
  50.4 11.0 %collective-permute-done.6 = bf16[4,144,384]{2,1,0:T(8,128)(2,1)S(1)} collective-permute-done((bf16[4,144,384]{2,1,0:T(8,128)(2,1)S(1)}, bf16[4,144,384]{2,1,0:T(8,128)(2,1)S(1)}, u32[]{:S(2)}, u32[]{:S(2)}) %collective-permute-start.6) | collective-permute-done | bytes 442400 | tf_op jit(solution)/shard_map/ppermute | solution.py:199
  61.4 14.5 %collective-permute-done.7 = bf16[4,144,384]{2,1,0:T(8,128)(2,1)S(1)} collective-permute-done((bf16[4,144,384]{2,1,0:T(8,128)(2,1)S(1)}, bf16[4,144,384]{2,1,0:T(8,128)(2,1)S(1)}, u32[]{:S(2)}, u32[]{:S(2)}) %collective-permute-start.7) | collective-permute-done | bytes 442400 | tf_op jit(solution)/shard_map/ppermute | solution.py:199
  109.0 23.2 %attend.2 = (f32[512,768]{1,0:T(8,128)}, bf16[512,768]{1,0:T(8,128)(2,1)}, bf16[12,512,128]{2,1,0:T(8,128)(2,1)}) custom-call(bf16[512,768]{1,0:T(8,128)(2,1)} %get-tuple-element.154.q_ref, bf16[2048,1536]{1,0:T(8,128)(2,1)} %get-tuple-element.155.k_ref.v_ref, bf16[2048,1536]{1,0:T(8,128)(2,1)} %get-tuple-element.155.k_ref.v_ref, ...), custom_call_target="tpu_custom_call" | custom-call | flops 512 | bytes 512 | tf_op jit(solution)/shard_map/attend/pallas_call | solution.py:54
  140.6 14.0 %feed_forward.2 = (f32[512,768]{1,0:T(8,128)}, bf16[512,768]{1,0:T(8,128)(2,1)}, bf16[512,3072]{1,0:T(8,128)(2,1)}, bf16[512,3072]{1,0:T(8,128)(2,1)}, f32[512,768]{1,0:T(8,128)}, /*index=5*/bf16[512,768]{1,0:T(8,128)(2,1)}) custom-call(bf16[512,768]{1,0:T(8,128)(2,1)} %bitcast.170, bf16[512,768]{1,0:T(8,128)(2,1)} %get-tuple-element.157.o_ref.refs_5_, ...), custom_call_target="tpu_custom_call" | custom-call | flops 512 | bytes 512 | tf_op jit(solution)/shard_map/feed_forward/pallas_call | solution.py:383
  156.1 21.9 %collective-permute-done.9 = bf16[512,768]{1,0:T(8,128)(2,1)S(1)} collective-permute-done((bf16[512,768]{1,0:T(8,128)(2,1)}, bf16[512,768]{1,0:T(8,128)(2,1)S(1)}, u32[]{:S(2)}, u32[]{:S(2)}) %collective-permute-start.9) | collective-permute-done | bytes 786464 | tf_op jit(solution)/shard_map/ppermute | solution.py:199
  184.8 12.2 %project.3 = (bf16[2304,1536]{1,0:T(8,128)(2,1)}, bf16[512,768]{1,0:T(8,128)(2,1)}) custom-call(bf16[2304,768]{1,0:T(8,128)(2,1)} %fusion.1.rows_ref.refs_4_, bf16[16,2,624,384]{3,2,1,0:T(8,128)(2,1)} %bitcast.155), custom_call_target="tpu_custom_call" | custom-call | flops 512 | bytes 512 | tf_op jit(solution)/shard_map/project/pallas_call | solution.py:318
  197.0 26.0 %attend.3 = (f32[512,768]{1,0:T(8,128)}, bf16[512,768]{1,0:T(8,128)(2,1)}, bf16[12,512,128]{2,1,0:T(8,128)(2,1)}) custom-call(bf16[512,768]{1,0:T(8,128)(2,1)} %get-tuple-element.160.q_ref, bf16[2304,1536]{1,0:T(8,128)(2,1)} %get-tuple-element.161.k_ref.v_ref, bf16[2304,1536]{1,0:T(8,128)(2,1)} %get-tuple-element.161.k_ref.v_ref, ...), custom_call_target="tpu_custom_call" | custom-call | flops 512 | bytes 512 | tf_op jit(solution)/shard_map/attend/pallas_call | solution.py:54
  223.0 11.9 %all-gather.7.cloned.1.call-done = bf16[15360,384]{1,0:T(8,128)(2,1)} async-done(((bf16[480,384]{1,0:T(8,128)(2,1)}), bf16[15360,384]{1,0:T(8,128)(2,1)}) %all-gather.7.cloned.1.call-update) | async-done | bytes 11796496 | tf_op jit(solution)/shard_map/all_gather | solution.py:655
  237.8 14.5 %feed_forward.3 = (f32[512,768]{1,0:T(8,128)}, bf16[512,768]{1,0:T(8,128)(2,1)}, bf16[512,3072]{1,0:T(8,128)(2,1)}, bf16[512,3072]{1,0:T(8,128)(2,1)}, f32[512,768]{1,0:T(8,128)}, /*index=5*/bf16[512,768]{1,0:T(8,128)(2,1)}) custom-call(f32[512,768]{1,0:T(8,128)} %get-tuple-element.158.h_ref, bf16[512,768]{1,0:T(8,128)(2,1)} %get-tuple-element.163.o_ref.refs_4_, ...), custom_call_target="tpu_custom_call" | custom-call | flops 512 | bytes 512 | tf_op jit(solution)/shard_map/feed_forward/pallas_call | solution.py:383
  263.2 15.3 %feed_forward_back.2 = (bf16[512,768]{1,0:T(8,128)(2,1)}, bf16[512,3072]{1,0:T(8,128)(2,1)}, f32[512,768]{1,0:T(8,128)}, bf16[512,768]{1,0:T(8,128)(2,1)}, bf16[512,768]{1,0:T(8,128)(2,1)}, /*index=5*/f32[1,768]{1,0:T(1,128)}) custom-call(f32[512,768]{1,0:T(8,128)} %broadcast_add_fusion.g_ref, bf16[512,3072]{1,0:T(8,128)(2,1)} %get-tuple-element.171.u_ref, ...), custom_call_target="tpu_custom_call" | custom-call | flops 512 | bytes 512 | tf_op jit(solution)/shard_map/feed_forward_back/pallas_call | solution.py:441
  278.5 17.0 %products.4 = bf16[16,2,528,384]{3,2,1,0:T(8,128)(2,1)} custom-call(bf16[512,3072]{1,0:T(8,128)(2,1)} %get-tuple-element.169.refs_0_, bf16[512,768]{1,0:T(8,128)(2,1)} %get-tuple-element.173.refs_1_, bf16[512,768]{1,0:T(8,128)(2,1)} %get-tuple-element.174.refs_2_, bf16[512,3072]{1,0:T(8,128)(2,1)} %get-tuple-element.175.refs_3_, ...), custom_call_target="tpu_custom_call" | custom-call | flops 512 | bytes 512 | tf_op jit(solution)/shard_map/products/pallas_call | solution.py:596
  295.6 20.7 %attend_back.5 = (bf16[512,384]{1,0:T(8,128)(2,1)}, bf16[2304,384]{1,0:T(8,128)(2,1)}, bf16[2304,384]{1,0:T(8,128)(2,1)}) custom-call(bf16[12,512,128]{2,1,0:T(8,128)(2,1)} %get-tuple-element.168.qa_ref, bf16[2304,1536]{1,0:T(8,128)(2,1)} %get-tuple-element.161.k_ref.v_ref, bf16[2304,1536]{1,0:T(8,128)(2,1)} %get-tuple-element.161.k_ref.v_ref, ...), custom_call_target="tpu_custom_call" | custom-call | flops 512 | bytes 512 | tf_op jit(solution)/shard_map/attend_back/pallas_call | solution.py:116
  316.3 20.3 %attend_back.4 = (bf16[512,384]{1,0:T(8,128)(2,1)}, bf16[2304,384]{1,0:T(8,128)(2,1)}, bf16[2304,384]{1,0:T(8,128)(2,1)}) custom-call(bf16[12,512,128]{2,1,0:T(8,128)(2,1)} %get-tuple-element.168.qa_ref, bf16[2304,1536]{1,0:T(8,128)(2,1)} %get-tuple-element.161.k_ref.v_ref, bf16[2304,1536]{1,0:T(8,128)(2,1)} %get-tuple-element.161.k_ref.v_ref, ...), custom_call_target="tpu_custom_call" | custom-call | flops 512 | bytes 512 | tf_op jit(solution)/shard_map/attend_back/pallas_call | solution.py:116
  336.6 15.0 %rows_back.2 = (f32[1280,768]{1,0:T(8,128)}, bf16[1024,768]{1,0:T(8,128)(2,1)}) custom-call(bf16[2304,384]{1,0:T(8,128)(2,1)} %get-tuple-element.191.dk0.refs_5_, bf16[2304,384]{1,0:T(8,128)(2,1)} %get-tuple-element.192.dk1.refs_6_, bf16[2304,384]{1,0:T(8,128)(2,1)} %get-tuple-element.193.dv0.refs_7_, bf16[2304,384]{1,0:T(8,128)(2,1)} %get-tuple-element.194.dv1.refs_8_, ...), custom_call_target="tpu_custom_call" | custom-call | flops 256 | bytes 256 | tf_op jit(solution)/shard_map/rows_back/pallas_call | solution.py:499
  361.4 15.0 %products.5 = (bf16[16,576,384]{2,1,0:T(8,128)(2,1)}, bf16[16,576,384]{2,1,0:T(8,128)(2,1)}) custom-call(s32[1]{0:T(128)} %bitcast.29.refs_0_, bf16[512,768]{1,0:T(8,128)(2,1)} %get-tuple-element.159.refs_1_, bf16[512,384]{1,0:T(8,128)(2,1)} %get-tuple-element.189.dq0.refs_2_, bf16[512,384]{1,0:T(8,128)(2,1)} %get-tuple-element.190.dq1.refs_3_, ...), custom_call_target="tpu_custom_call" | custom-call | flops 2304 | bytes 2304 | tf_op jit(solution)/shard_map/products/pallas_call | solution.py:596
  386.4 15.5 %feed_forward_back.3 = (bf16[512,768]{1,0:T(8,128)(2,1)}, bf16[512,3072]{1,0:T(8,128)(2,1)}, f32[512,768]{1,0:T(8,128)}, bf16[512,768]{1,0:T(8,128)(2,1)}, bf16[512,768]{1,0:T(8,128)(2,1)}, /*index=5*/f32[1,768]{1,0:T(1,128)}) custom-call(f32[512,768]{1,0:T(8,128)} %multiply_add_fusion.g_ref, bf16[512,3072]{1,0:T(8,128)(2,1)} %get-tuple-element.199.u_ref, ...), custom_call_target="tpu_custom_call" | custom-call | flops 512 | bytes 512 | tf_op jit(solution)/shard_map/feed_forward_back/pallas_call | solution.py:441
  402.0 15.1 %products.6 = (bf16[16,576,384]{2,1,0:T(8,128)(2,1)}, bf16[16,576,384]{2,1,0:T(8,128)(2,1)}) custom-call(s32[1]{0:T(128)} %bitcast.29.refs_0_, bf16[512,3072]{1,0:T(8,128)(2,1)} %get-tuple-element.167.refs_1_, bf16[512,768]{1,0:T(8,128)(2,1)} %get-tuple-element.201.refs_2_, ...), custom_call_target="tpu_custom_call", output_to_operand_aliasing={{0}: (7, {}), {1}: (8, {})} | custom-call | flops 512 | bytes 512 | tf_op jit(solution)/shard_map/products/pallas_call | solution.py:596
  417.1 18.6 %attend_back.6 = (bf16[512,384]{1,0:T(8,128)(2,1)}, bf16[2048,384]{1,0:T(8,128)(2,1)}, bf16[2048,384]{1,0:T(8,128)(2,1)}) custom-call(bf16[12,512,128]{2,1,0:T(8,128)(2,1)} %get-tuple-element.166.qa_ref, bf16[2048,1536]{1,0:T(8,128)(2,1)} %get-tuple-element.155.k_ref.v_ref, bf16[2048,1536]{1,0:T(8,128)(2,1)} %get-tuple-element.155.k_ref.v_ref, ...), custom_call_target="tpu_custom_call" | custom-call | flops 512 | bytes 512 | tf_op jit(solution)/shard_map/attend_back/pallas_call | solution.py:116
  447.3 18.3 %attend_back.7 = (bf16[512,384]{1,0:T(8,128)(2,1)}, bf16[2048,384]{1,0:T(8,128)(2,1)}, bf16[2048,384]{1,0:T(8,128)(2,1)}) custom-call(bf16[12,512,128]{2,1,0:T(8,128)(2,1)} %get-tuple-element.166.qa_ref, bf16[2048,1536]{1,0:T(8,128)(2,1)} %get-tuple-element.155.k_ref.v_ref, bf16[2048,1536]{1,0:T(8,128)(2,1)} %get-tuple-element.155.k_ref.v_ref, ...), custom_call_target="tpu_custom_call" | custom-call | flops 512 | bytes 512 | tf_op jit(solution)/shard_map/attend_back/pallas_call | solution.py:116
  465.6 12.0 %rows_back.3 = (f32[1536,768]{1,0:T(8,128)}, bf16[1024,768]{1,0:T(8,128)(2,1)}) custom-call(bf16[2048,384]{1,0:T(8,128)(2,1)} %get-tuple-element.247.dk0.refs_5_, bf16[2048,384]{1,0:T(8,128)(2,1)} %get-tuple-element.248.dk1.refs_6_, bf16[2048,384]{1,0:T(8,128)(2,1)} %get-tuple-element.249.dv0.refs_7_, bf16[2048,384]{1,0:T(8,128)(2,1)} %get-tuple-element.250.dv1.refs_8_, ...), custom_call_target="tpu_custom_call" | custom-call | flops 512 | bytes 512 | tf_op jit(solution)/shard_map/rows_back/pallas_call | solution.py:499
  504.7 14.2 %products.7 = (bf16[16,144,384]{2,1,0:T(8,128)(2,1)}, bf16[16,144,384]{2,1,0:T(8,128)(2,1)}) custom-call(s32[1]{0:T(128)} %bitcast.29.refs_0_, bf16[512,768]{1,0:T(8,128)(2,1)} %copy-done.10, bf16[512,384]{1,0:T(8,128)(2,1)} %get-tuple-element.245.dq0.refs_2_, bf16[512,384]{1,0:T(8,128)(2,1)} %get-tuple-element.246.dq1.refs_3_, ...), custom_call_target="tpu_custom_call" | custom-call | flops 2048 | bytes 2048 | tf_op jit(solution)/shard_map/products/pallas_call | solution.py:596
  524.6 12.3 %collective-permute-done.17 = bf16[512,768]{1,0:T(8,128)(2,1)S(1)} collective-permute-done((bf16[512,768]{1,0:T(8,128)(2,1)}, bf16[512,768]{1,0:T(8,128)(2,1)S(1)}, u32[]{:S(2)}, u32[]{:S(2)}) %collective-permute-start.17) | collective-permute-done | bytes 786464 | tf_op jit(solution)/shard_map/ppermute | solution.py:199
  570.5 19.1 %collective-permute-done.25 = bf16[1,576,384]{2,1,0:T(8,128)(2,1)S(1)} collective-permute-done((bf16[1,576,384]{2,1,0:T(8,128)(2,1)S(1)}, bf16[1,576,384]{2,1,0:T(8,128)(2,1)S(1)}, u32[]{:S(2)}, u32[]{:S(2)}) %collective-permute-start.25) | collective-permute-done | bytes 442400 | tf_op jit(solution)/shard_map/ppermute | solution.py:199
  (387 shorter events, 249.9 us)
Async XLA Ops:
  7.2 133.4 %all-gather.5.cloned.1.call-start = ((), (), s32[]{:S(2)}) async-start(), calls=%async_computation.2 | async-start | bytes 15814656 | tf_op jit(solution)/shard_map/all_gather | solution.py:655
  14.9 219.9 %all-gather.7.cloned.1.call-start = ((), (), s32[]{:S(2)}) async-start(), calls=%async_computation.3 | async-start | bytes 12165120 | tf_op jit(solution)/shard_map/all_gather | solution.py:655
  21.4 444.2 %reduce-scatter.2.cloned.1.call-start = ((), (), s32[]{:S(2)}) async-start(), calls=%async_computation.1 | async-start | bytes 13381632 | tf_op jit(solution)/shard_map/reduce_scatter | solution.py:737
  26.7 16.5 %collective-permute-start = (bf16[1,144,384]{2,1,0:T(8,128)(2,1)S(1)}, bf16[1,144,384]{2,1,0:T(8,128)(2,1)S(1)}, u32[]{:S(2)}, u32[]{:S(2)}) collective-permute-start(bf16[1,144,384]{2,1,0:T(8,128)(2,1)S(1)} %maximum_bitcast_fusion.2), channel_id=1, source_target_pairs={{0,2},{8,10},{16,18},{24,26},{1,3},{9,11},{17,19},{25,27},{2,0},{1... | collective-permute-start | bytes 331784 | tf_op jit(solution)/shard_map/ppermute | solution.py:199
  43.4 18.1 %collective-permute-start.6 = (bf16[4,144,384]{2,1,0:T(8,128)(2,1)S(1)}, bf16[4,144,384]{2,1,0:T(8,128)(2,1)S(1)}, u32[]{:S(2)}, u32[]{:S(2)}) collective-permute-start(bf16[4,144,384]{2,1,0:T(8,128)(2,1)S(1)} %maximum_bitcast_fusion), channel_id=1, source_target_pairs={{0,1},{8,9},{16,17},{24,25},{1,0},{9,8},{17,16},{25,24},{2,3},{10,... | collective-permute-start | bytes 1327112 | tf_op jit(solution)/shard_map/ppermute | solution.py:199
  46.3 29.7 %collective-permute-start.7 = (bf16[4,144,384]{2,1,0:T(8,128)(2,1)S(1)}, bf16[4,144,384]{2,1,0:T(8,128)(2,1)S(1)}, u32[]{:S(2)}, u32[]{:S(2)}) collective-permute-start(bf16[4,144,384]{2,1,0:T(8,128)(2,1)S(1)} %maximum_bitcast_fusion), channel_id=1, source_target_pairs={{0,17},{8,25},{16,1},{24,9},{1,16},{9,24},{17,0},{25,8},{2,19},{10... | collective-permute-start | bytes 1327112 | tf_op jit(solution)/shard_map/ppermute | solution.py:199
  47.4 28.5 %collective-permute-start.5 = (bf16[4,144,384]{2,1,0:T(8,128)(2,1)S(1)}, bf16[4,144,384]{2,1,0:T(8,128)(2,1)S(1)}, u32[]{:S(2)}, u32[]{:S(2)}) collective-permute-start(bf16[4,144,384]{2,1,0:T(8,128)(2,1)S(1)} %maximum_bitcast_fusion), channel_id=1, source_target_pairs={{0,16},{8,24},{16,0},{24,8},{1,17},{9,25},{17,1},{25,9},{2,18},{10... | collective-permute-start | bytes 1327112 | tf_op jit(solution)/shard_map/ppermute | solution.py:199
  48.7 39.8 %collective-permute-start.3 = (bf16[512,768]{1,0:T(8,128)(2,1)S(1)}, bf16[512,768]{1,0:T(8,128)(2,1)S(1)}, u32[]{:S(2)}, u32[]{:S(2)}) collective-permute-start(bf16[512,768]{1,0:T(8,128)(2,1)S(1)} %fusion.8.refs_1_), channel_id=1, source_target_pairs={{0,16},{8,24},{16,0},{24,8},{1,17},{9,25},{17,1},{25,9},{2,18},{10... | collective-permute-start | bytes 2359304 | tf_op jit(solution)/shard_map/ppermute | solution.py:199
  154.6 23.4 %collective-permute-start.9 = (bf16[512,768]{1,0:T(8,128)(2,1)}, bf16[512,768]{1,0:T(8,128)(2,1)S(1)}, u32[]{:S(2)}, u32[]{:S(2)}) collective-permute-start(bf16[512,768]{1,0:T(8,128)(2,1)} %get-tuple-element.159.refs_1_), channel_id=1, source_target_pairs={{0,16},{8,24},{16,0},{24,8},{1,17},{9,25},{17,1},{25,9},{2,18},{10... | collective-permute-start | bytes 2359304 | tf_op jit(solution)/shard_map/ppermute | solution.py:199
  359.3 21.2 %collective-permute-start.12 = (bf16[512,768]{1,0:T(8,128)(2,1)S(1)}, bf16[512,768]{1,0:T(8,128)(2,1)S(1)}, u32[]{:S(2)}, u32[]{:S(2)}) collective-permute-start(bf16[512,768]{1,0:T(8,128)(2,1)S(1)} %slice.253), channel_id=1, source_target_pairs={{0,16},{8,24},{16,0},{24,8},{1,17},{9,25},{17,1},{25,9},{2,18},{10... | collective-permute-start | bytes 2359304 | tf_op jit(solution)/shard_map/ppermute | solution.py:199
  417.0 18.7 %collective-permute-start.13 = (bf16[16,576,384]{2,1,0:T(8,128)(2,1)}, bf16[16,576,384]{2,1,0:T(8,128)(2,1)}, u32[]{:S(2)}, u32[]{:S(2)}) collective-permute-start(bf16[16,576,384]{2,1,0:T(8,128)(2,1)} %get-tuple-element.216), channel_id=1, source_target_pairs={{0,8},{8,0},{16,24},{24,16},{1,9},{9,1},{17,25},{25,17},{2,10},{10... | collective-permute-start | bytes 21233672 | tf_op jit(solution)/shard_map/ppermute | solution.py:199
  445.4 41.3 %collective-permute-start.15 = (bf16[8,288,384]{2,1,0:T(8,128)(2,1)}, bf16[8,288,384]{2,1,0:T(8,128)(2,1)}, u32[]{:S(2)}, u32[]{:S(2)}) collective-permute-start(bf16[8,288,384]{2,1,0:T(8,128)(2,1)} %get-tuple-element.238), channel_id=1, source_target_pairs={{0,16},{8,24},{16,0},{24,8},{1,17},{9,25},{17,1},{25,9},{2,18},{10... | collective-permute-start | bytes 5308424 | tf_op jit(solution)/shard_map/ppermute | solution.py:199
  445.4 45.1 %collective-permute-start.16 = (bf16[8,288,384]{2,1,0:T(8,128)(2,1)}, bf16[8,288,384]{2,1,0:T(8,128)(2,1)}, u32[]{:S(2)}, u32[]{:S(2)}) collective-permute-start(bf16[8,288,384]{2,1,0:T(8,128)(2,1)} %get-tuple-element.242), channel_id=1, source_target_pairs={{0,1},{8,9},{16,17},{24,25},{1,0},{9,8},{17,16},{25,24},{2,3},{10,... | collective-permute-start | bytes 5308424 | tf_op jit(solution)/shard_map/ppermute | solution.py:199
  496.1 22.8 %collective-permute-start.18 = (bf16[4,288,384]{2,1,0:T(8,128)(2,1)}, bf16[4,288,384]{2,1,0:T(8,128)(2,1)}, u32[]{:S(2)}, u32[]{:S(2)}) collective-permute-start(bf16[4,288,384]{2,1,0:T(8,128)(2,1)} %get-tuple-element.255), channel_id=1, source_target_pairs={{0,1},{8,9},{16,17},{24,25},{1,0},{9,8},{17,16},{25,24},{2,3},{10,... | collective-permute-start | bytes 2654216 | tf_op jit(solution)/shard_map/ppermute | solution.py:199
  499.0 22.8 %collective-permute-start.19 = (bf16[4,288,384]{2,1,0:T(8,128)(2,1)S(1)}, bf16[4,288,384]{2,1,0:T(8,128)(2,1)}, u32[]{:S(2)}, u32[]{:S(2)}) collective-permute-start(bf16[4,288,384]{2,1,0:T(8,128)(2,1)S(1)} %get-tuple-element.257), channel_id=1, source_target_pairs={{0,16},{8,24},{16,0},{24,8},{1,17},{9,25},{17,1},{25,9},{2,18},{10... | collective-permute-start | bytes 2654216 | tf_op jit(solution)/shard_map/ppermute | solution.py:199
  501.4 35.4 %collective-permute-start.17 = (bf16[512,768]{1,0:T(8,128)(2,1)}, bf16[512,768]{1,0:T(8,128)(2,1)S(1)}, u32[]{:S(2)}, u32[]{:S(2)}) collective-permute-start(bf16[512,768]{1,0:T(8,128)(2,1)} %slice.252), channel_id=1, source_target_pairs={{0,16},{8,24},{16,0},{24,8},{1,17},{9,25},{17,1},{25,9},{2,18},{10... | collective-permute-start | bytes 2359304 | tf_op jit(solution)/shard_map/ppermute | solution.py:199
  548.3 22.2 %collective-permute-start.26 = (bf16[1,576,384]{2,1,0:T(8,128)(2,1)S(1)}, bf16[1,576,384]{2,1,0:T(8,128)(2,1)S(1)}, u32[]{:S(2)}, u32[]{:S(2)}) collective-permute-start(bf16[1,576,384]{2,1,0:T(8,128)(2,1)S(1)} %get-tuple-element.358), channel_id=1, source_target_pairs={{0,6},{8,14},{16,22},{24,30},{1,7},{9,15},{17,23},{25,31},{2,4},{1... | collective-permute-start | bytes 1327112 | tf_op jit(solution)/shard_map/ppermute | solution.py:199
  551.4 38.1 %collective-permute-start.25 = (bf16[1,576,384]{2,1,0:T(8,128)(2,1)S(1)}, bf16[1,576,384]{2,1,0:T(8,128)(2,1)S(1)}, u32[]{:S(2)}, u32[]{:S(2)}) collective-permute-start(bf16[1,576,384]{2,1,0:T(8,128)(2,1)S(1)} %get-tuple-element.359), channel_id=1, source_target_pairs={{0,4},{8,12},{16,20},{24,28},{1,5},{9,13},{17,21},{25,29},{2,6},{1... | collective-permute-start | bytes 1327112 | tf_op jit(solution)/shard_map/ppermute | solution.py:199
  551.6 38.2 %collective-permute-start.21 = (bf16[4,160,384]{2,1,0:T(8,128)(2,1)S(1)}, bf16[4,160,384]{2,1,0:T(8,128)(2,1)S(1)}, u32[]{:S(2)}, u32[]{:S(2)}) collective-permute-start(bf16[4,160,384]{2,1,0:T(8,128)(2,1)S(1)} %get-tuple-element.354), channel_id=1, source_target_pairs={{0,16},{8,24},{16,0},{24,8},{1,17},{9,25},{17,1},{25,9},{2,18},{10... | collective-permute-start | bytes 1474568 | tf_op jit(solution)/shard_map/ppermute | solution.py:199
  552.3 37.5 %collective-permute-start.23 = (bf16[4,160,384]{2,1,0:T(8,128)(2,1)S(1)}, bf16[4,160,384]{2,1,0:T(8,128)(2,1)S(1)}, u32[]{:S(2)}, u32[]{:S(2)}) collective-permute-start(bf16[4,160,384]{2,1,0:T(8,128)(2,1)S(1)} %get-tuple-element.355), channel_id=1, source_target_pairs={{0,17},{8,25},{16,1},{24,9},{1,16},{9,24},{17,0},{25,8},{2,19},{10... | collective-permute-start | bytes 1474568 | tf_op jit(solution)/shard_map/ppermute | solution.py:199
  558.3 31.5 %collective-permute-start.22 = (bf16[4,160,384]{2,1,0:T(8,128)(2,1)S(1)}, bf16[4,160,384]{2,1,0:T(8,128)(2,1)S(1)}, u32[]{:S(2)}, u32[]{:S(2)}) collective-permute-start(bf16[4,160,384]{2,1,0:T(8,128)(2,1)S(1)} %get-tuple-element.356), channel_id=1, source_target_pairs={{0,1},{8,9},{16,17},{24,25},{1,0},{9,8},{17,16},{25,24},{2,3},{10,... | collective-permute-start | bytes 1474568 | tf_op jit(solution)/shard_map/ppermute | solution.py:199
  609.0 21.3 %collective-permute-start.45 = (bf16[1104,384]{1,0:T(8,128)(2,1)S(1)}, bf16[1104,384]{1,0:T(8,128)(2,1)S(1)}, u32[]{:S(2)}, u32[]{:S(2)}) collective-permute-start(bf16[1104,384]{1,0:T(8,128)(2,1)S(1)} %pad_maximum_fusion.9.refs_0_), channel_id=1, source_target_pairs={{0,16},{8,24},{16,0},{24,8},{1,17},{9,25},{17,1},{25,9},{2,18},{10... | collective-permute-start | bytes 2543624 | tf_op jit(solution)/shard_map/ppermute | solution.py:199
  610.2 29.9 %collective-permute-start.44 = (bf16[1104,384]{1,0:T(8,128)(2,1)S(1)}, bf16[1104,384]{1,0:T(8,128)(2,1)S(1)}, u32[]{:S(2)}, u32[]{:S(2)}) collective-permute-start(bf16[1104,384]{1,0:T(8,128)(2,1)S(1)} %pad_maximum_fusion.9.refs_0_), channel_id=1, source_target_pairs={{0,8},{8,0},{16,24},{24,16},{1,9},{9,1},{17,25},{25,17},{2,10},{10... | collective-permute-start | bytes 2543624 | tf_op jit(solution)/shard_map/ppermute | solution.py:199
  619.4 17.6 %collective-permute-start.36 = (bf16[4,32,768]{2,1,0:T(8,128)(2,1)S(1)}, bf16[4,32,768]{2,1,0:T(8,128)(2,1)}, u32[]{:S(2)}, u32[]{:S(2)}) collective-permute-start(bf16[4,32,768]{2,1,0:T(8,128)(2,1)S(1)} %maximum_bitcast_fusion.1), channel_id=1, source_target_pairs={{0,4},{8,12},{16,20},{24,28},{1,5},{9,13},{17,21},{25,29},{2,6},{1... | collective-permute-start | bytes 589832 | tf_op jit(solution)/shard_map/ppermute | solution.py:199
  (90 other events, 726.5 us)
Sparse Core Ops, SparseCore 0:
  15.0 125.4 all-gather.4
  144.0 90.7 all-gather.6
  295.7 156.4 reduce-scatter.1
